TPU v7x, 32 devices: a whole 2x2x4 slice. The times are simulated.
32 devices in a mesh: fsdp: 8 (over z, x), sp: 4 (over y, core).
Axes of the slice: x: 2, y: 2, z: 4, core: 2. Of those that a mesh axis runs over, the one named last changes fastest.
Arguments:
- hidden_in: bfloat16 [32, 1024, 768], P('fsdp', 'sp'), may hold values from -6 to 6
- doc_starts: int32 [32, 4], P('fsdp'), may hold values from 0 to 1023, as said below
- w_qkv: bfloat16 [768, 2304], P('fsdp'), may hold values from -0.21875 to 0.21875
- query_bias: bfloat16 [768], P('fsdp'), may hold values from -3 to 3
- value_bias: bfloat16 [768], P('fsdp'), may hold values from -3 to 3
- w_out: bfloat16 [768, 768], P('fsdp'), may hold values from -1.75 to 1.75
- out_bias: bfloat16 [768], P('fsdp'), may hold values from -2 to 2
- norm1_gain: bfloat16 [768], P('fsdp'), may hold values from 0.5 to 1.5
- norm1_bias: bfloat16 [768], P('fsdp'), may hold values from -2 to 2
- w_up: bfloat16 [768, 3072], P('fsdp'), may hold values from -0.21875 to 0.21875
- up_bias: bfloat16 [3072], P('fsdp'), may hold values from -3 to 3
- w_down: bfloat16 [3072, 768], P('fsdp'), may hold values from -0.21875 to 0.21875
- down_bias: bfloat16 [768], P('fsdp'), may hold values from -2 to 2
- norm2_gain: bfloat16 [768], P('fsdp'), may hold values from 0.5 to 1.5
- norm2_bias: bfloat16 [768], P('fsdp'), may hold values from -2 to 2
- cotangent: bfloat16 [32, 1024, 768], P('fsdp', 'sp'), may hold values from -6 to 6
Outputs:
- layer_out: bfloat16 [32, 1024, 768], P('fsdp', 'sp')
- grad_input: bfloat16 [32, 1024, 768], P('fsdp', 'sp')
- grad_w_qkv: float32 [768, 2304], P('fsdp')
- grad_query_bias: float32 [768], P('fsdp')
- grad_value_bias: float32 [768], P('fsdp')
- grad_w_out: float32 [768, 768], P('fsdp')
- grad_out_bias: float32 [768], P('fsdp')
- grad_norm1_gain: float32 [768], P('fsdp')
- grad_norm1_bias: float32 [768], P('fsdp')
- grad_w_up: float32 [768, 3072], P('fsdp')
- grad_up_bias: float32 [3072], P('fsdp')
- grad_w_down: float32 [3072, 768], P('fsdp')
- grad_down_bias: float32 [768], P('fsdp')
- grad_norm2_gain: float32 [768], P('fsdp')
- grad_norm2_bias: float32 [768], P('fsdp')
Inputs may be any that keep to these rules, and one draw needn't show every extreme that they name: `doc_starts`: in each row entry 0 is 0 and the entries rise strictly; document j of a sequence spans its positions from entry j up to the next entry, or to position 1023.
All inputs are finite; a program needn't handle non-finite values.
Results may differ from a plain program's by a relative error of at most 0.018.
Values may be sent and summed in bfloat16 or wider, within the bound.
No kernel may reach another device: no remote copies, remote signals or barrier semaphores. Data moves between devices by JAX's collectives and lax.ppermute only.
A program may use at most 192 MiB of HBM per device.

v0:
```python
import jax
import jax.numpy as jnp
from jax import lax
from jax.experimental import pallas as pl
from jax.experimental.pallas import tpu as pltpu
from jax.sharding import PartitionSpec as P


D = 768
H = 12
HD = 64
FF = 3072
SEQ = 1024
PAIRS = H // 2
EPS = 1e-05
MASKED = -1000000000.0
SCALE = HD ** (-0.5)
BF = jnp.bfloat16
F32 = jnp.float32
ROWS = 256
MIB = 1 << 20


ERFC = (
    0.2820844758103095,
    0.28240952292464144,
    0.24285408258103366,
    0.20367679547693512,
    -0.028968306758876145,
    0.2814702272328375,
    -0.49017537256556365,
    0.28601194065835034,
    -0.059363409284156475,
)


def nn(a, b):
    return lax.dot_general(a, b, (((1,), (0,)), ((), ())), preferred_element_type=F32)


def nt(a, b):
    return lax.dot_general(a, b, (((1,), (1,)), ((), ())), preferred_element_type=F32)


def tn(a, b):
    return lax.dot_general(a, b, (((0,), (0,)), ((), ())), preferred_element_type=F32)


def gelu_with_slope(x):
    z = jnp.abs(x) * 0.7071067811865476
    t = 1.0 / (1.0 + 0.5 * z)
    e = jnp.exp(-0.5 * (x * x))
    poly = jnp.full_like(t, 0.5 * ERFC[-1])
    for c in ERFC[-2::-1]:
        poly = poly * t + 0.5 * c
    tail = poly * t * e
    cdf = jnp.where(x >= 0, 1.0 - tail, tail)
    return x * cdf, cdf + x * (e * 0.3989422804014327)


def norm_rows(v):
    c = v - jnp.mean(v, -1, keepdims=True)
    r = lax.rsqrt(jnp.mean(c * c, -1, keepdims=True) + EPS)
    return c * r, r


def norm_rows_back(a, xhat, rstd):
    return rstd * (a - jnp.mean(a, -1, keepdims=True) - xhat * jnp.mean(a * xhat, -1, keepdims=True))


def piece_copies(pieces, by_rows, cols, dst, sems, core, x_bit):
    copies = []
    lo, nc = cols
    for rc, ref in enumerate(pieces):
        _, count, nr, _ = ref.shape
        nr -= nr % (D // 8 // 2) if not by_rows else 0
        row0 = nr * lax.bitwise_xor(core, rc) if by_rows else 0
        col0 = 0 if by_rows else nc * lax.bitwise_xor(core, rc)
        stride = nr * (2 if by_rows else 1)
        for rx in range(2):
            for z in range(count):
                row = row0 + stride * (2 * z + lax.bitwise_xor(x_bit, rx))
                copies.append(
                    pltpu.make_async_copy(
                        ref.at[rx, z, pl.ds(0, nr), pl.ds(lo, nc)],
                        dst.at[
                            pl.ds(pl.multiple_of(row, nr), nr),
                            pl.ds(0 if by_rows else pl.multiple_of(col0, nc), nc),
                        ],
                        sems.at[(rc * 2 + rx) * count + z],
                    )
                )
    return copies


def whole_copies(ref, cols, dst, sems):
    lo, nc = cols
    return [pltpu.make_async_copy(ref.at[:, pl.ds(lo, nc)], dst, sems.at[0])]


def weight_copies(kind, refs, cols, full_cols, dst, sems, bits):
    if kind == "whole":
        return whole_copies(refs[0], full_cols, dst, sems)
    return piece_copies(refs, kind == "rows", full_cols if kind == "rows" else cols, dst, sems, *bits)


def copy_count(weight):
    kind, refs = weight
    return 1 if kind == "whole" else 4 * refs[0].shape[1]


def put_block(refs, step, value):
    for r, ref in enumerate(refs):
        @pl.when(step == r)
        def _():
            ref[...] = value


def start_all(copies):
    for c in copies:
        c.start()


def wait_all(copies):
    for c in copies:
        c.wait()


ANY = pl.BlockSpec(memory_space=pl.ANY)


def cost(us):
    return pl.CostEstimate(flops=int(us * 1e9), bytes_accessed=1 << 20, transcendentals=0)


def params(vmem=58):
    return pltpu.CompilerParams(
        dimension_semantics=("arbitrary",), vmem_limit_bytes=vmem * MIB
    )


def bits_of(me_ref):
    return lax.bitwise_and(me_ref[0], 1), me_ref[1]


def pack(me, w, vectors, copies):
    rows, width = w.shape[0], w.shape[1] // 2

    def kernel(me_ref, w_ref, *rest):
        v_refs, o_ref = rest[:-1], rest[-1]
        for z in range(copies):
            o_ref[z, :rows, :] = w_ref[...]
            o_ref[z, rows:, :] = jnp.zeros((16, width), BF)
        for i, v in enumerate(v_refs):
            for z in range(copies):
                o_ref[z, rows + i : rows + i + 1, : v.shape[0]] = v[...].reshape(1, -1)

    one = lambda v: pl.BlockSpec(v.shape, lambda i, me: (0,))
    return pl.pallas_call(
        kernel,
        grid_spec=pltpu.PrefetchScalarGridSpec(
            num_scalar_prefetch=1,
            grid=(1,),
            in_specs=[pl.BlockSpec((rows, width), lambda i, me: (0, lax.bitwise_and(me[0], 1)))]
            + [one(v) for v in vectors],
            out_specs=pl.BlockSpec((copies, rows + 16, width), lambda i, me: (0, 0, 0)),
        ),
        out_shape=jax.ShapeDtypeStruct((copies, rows + 16, width), BF),
        compiler_params=params(),
        cost_estimate=cost(2),
        name="pack",
    )(me, w, *vectors)


def deal(me, v):
    def kernel(me_ref, v_ref, *rest):
        o_refs, sems = rest[:-1], rest[-1]
        copies = [pltpu.make_async_copy(v_ref.at[lax.bitwise_xor(me_ref[0], r)], o, sems.at[r])
                  for r, o in enumerate(o_refs)]
        start_all(copies)
        wait_all(copies)

    n = v.shape[0]
    return pl.pallas_call(
        kernel,
        in_specs=[pl.BlockSpec(memory_space=pltpu.SMEM), ANY],
        out_specs=[ANY] * n,
        out_shape=[jax.ShapeDtypeStruct(v.shape[1:], v.dtype)] * n,
        scratch_shapes=[pltpu.SemaphoreType.DMA((n,))],
        cost_estimate=cost(2),
        name="deal",
    )(me, v)


def place(me, parts):
    def kernel(me_ref, *rest):
        p_refs, (o_ref, sems) = rest[:-2], rest[-2:]
        copies = [pltpu.make_async_copy(p, o_ref.at[lax.bitwise_xor(me_ref[0], r)], sems.at[r])
                  for r, p in enumerate(p_refs)]
        start_all(copies)
        wait_all(copies)

    n = len(parts)
    return pl.pallas_call(
        kernel,
        in_specs=[pl.BlockSpec(memory_space=pltpu.SMEM)] + [ANY] * n,
        out_specs=ANY,
        out_shape=jax.ShapeDtypeStruct((n,) + parts[0].shape, parts[0].dtype),
        scratch_shapes=[pltpu.SemaphoreType.DMA((n,))],
        cost_estimate=cost(2),
        name="place",
    )(me, *parts)


def project(me, x, weight, bias_row):
    kind, refs = weight
    n = 3 * D
    count = copy_count(weight)

    def kernel(me_ref, x_ref, b_ref, *rest):
        w_refs, (o_ref, w_ref, sems) = rest[:-3], rest[-3:]

        @pl.when(pl.program_id(0) == 0)
        def _():
            copies = weight_copies(kind, w_refs, (0, n // 2), (0, n), w_ref, sems, bits_of(me_ref))
            start_all(copies)
            wait_all(copies)

        xv = x_ref[...]
        for lo in range(0, n, D):
            o_ref[:, lo : lo + D] = (
                nn(xv, w_ref[:, lo : lo + D]) + b_ref[:, lo : lo + D]
            ).astype(BF)

    rows = x.shape[0]
    return pl.pallas_call(
        kernel,
        grid_spec=pltpu.PrefetchScalarGridSpec(
            num_scalar_prefetch=1,
            grid=(rows // ROWS,),
            in_specs=[
                pl.BlockSpec((ROWS, D), lambda i, me: (i, 0)),
                pl.BlockSpec((1, n), lambda i, me: (0, 0)),
            ]
            + [ANY] * len(refs),
            out_specs=pl.BlockSpec((ROWS, n), lambda i, me: (i, 0)),
            scratch_shapes=[pltpu.VMEM((D, n), BF), pltpu.SemaphoreType.DMA((count,))],
        ),
        out_shape=jax.ShapeDtypeStruct((rows, n), BF),
        compiler_params=params(),
        cost_estimate=cost(9),
        name="project",
    )(me, x, bias_row, *refs)


def attend(qkv, seg_col, seg_row, first, count, before):
    chunk = 256

    def kernel(q_ref, k_ref, v_ref, sc_ref, sr_ref, *rest):
        o_ref, lse_ref = rest[-2:]
        lane = lax.broadcasted_iota(jnp.int32, (1, 2 * HD), 1)
        k = k_ref[...]
        vt = v_ref[...].T
        seg_k = sc_ref[...]
        for c in range(SEQ // chunk):
            at = pl.ds(c * chunk, chunk)
            q = q_ref[at, :] * jnp.asarray(SCALE, BF)
            same = seg_k == sr_ref[:, at]
            outs = []
            for h in range(2):
                mine = (lane < HD) if h == 0 else (lane >= HD)
                s = nt(k, jnp.where(mine, q, jnp.zeros_like(q)))
                s = jnp.where(same, s, MASKED)
                m = jnp.max(s, 0, keepdims=True)
                p = jnp.exp(s - m)
                l = jnp.sum(p, 0, keepdims=True)
                lse_ref[0, h : h + 1, at] = m + jnp.log(l)
                o = nn(vt, p.astype(BF))
                outs.append(o[h * HD : (h + 1) * HD] * (1.0 / l))
            o_ref[at, :] = jnp.concatenate(outs, 0).T.astype(BF)

    spec = lambda off: pl.BlockSpec((SEQ, 2 * HD), lambda i: (0, i + off + first))
    full = lambda s: pl.BlockSpec(s, lambda i: (0,) * len(s))
    return pl.pallas_call(
        kernel,
        grid=(count,),
        in_specs=[spec(0), spec(PAIRS), spec(2 * PAIRS), full((SEQ, 1)), full((1, SEQ))]
        + [ANY] * len(before),
        out_specs=[spec(0), pl.BlockSpec((1, 8, SEQ), lambda i: (i + first, 0, 0))],
        input_output_aliases={5 + i: i for i in range(len(before))},
        out_shape=[
            jax.ShapeDtypeStruct((SEQ, D), BF),
            jax.ShapeDtypeStruct((PAIRS, 8, SEQ), F32),
        ],
        compiler_params=params(),
        cost_estimate=cost(6 * count),
        name="attend",
    )(qkv, qkv, qkv, seg_col, seg_row, *before)


def attend_back(qkv, context, grad_context, lse, seg_col, seg_row, start, count, before):
    chunk = 256

    def kernel(q_ref, k_ref, v_ref, o_ref, g_ref, lse_ref, sc_ref, sr_ref, *rest):
        dq_ref, dk_ref, dv_ref, sum_ref, acc_ref, kt_ref = rest[-6:]
        lane = lax.broadcasted_iota(jnp.int32, (1, 2 * HD), 1)
        first = lane < HD
        q = q_ref[...] * jnp.asarray(SCALE, BF)
        g = g_ref[...]
        zero = jnp.zeros_like(q)
        prod = (g.astype(F32) * o_ref[...].astype(F32)).T
        inner = [jnp.sum(prod[h * HD : (h + 1) * HD], 0, keepdims=True) for h in range(2)]
        qm = [jnp.where(first, q, zero), jnp.where(first, zero, q)]
        gm = [jnp.where(first, g, zero), jnp.where(first, zero, g)]
        seg_q = sr_ref[...]
        kt_ref[...] = k_ref[...].T
        acc_ref[...] = jnp.zeros_like(acc_ref)
        dv_total = jnp.zeros((1, 2 * HD), F32)
        for c in range(SEQ // chunk):
            at = pl.ds(c * chunk, chunk)
            k = k_ref[at, :]
            v = v_ref[at, :]
            same = sc_ref[at, :] == seg_q
            dks, dvs = [], []
            for h in range(2):
                s = jnp.where(same, nt(k, qm[h]), MASKED)
                p = jnp.exp(s - lse_ref[0, h : h + 1, :])
                ds = (p * (nt(v, gm[h]) - inner[h])).astype(BF)
                dvs.append(nn(p.astype(BF), g))
                dks.append(nn(ds, q))
                half = pl.ds(h * HD, HD)
                acc_ref[half, :] += nn(kt_ref[half, at], ds)
            dk_ref[at, :] = jnp.where(first, dks[0], dks[1]).astype(BF)
            dv = jnp.where(first, dvs[0], dvs[1]).astype(BF)
            dv_ref[at, :] = dv
            dv_total += jnp.sum(dv.astype(F32), 0, keepdims=True)
        dq = (acc_ref[...].T * SCALE).astype(BF)
        dq_ref[...] = dq
        sum_ref[0:1, :] = jnp.sum(dq.astype(F32), 0, keepdims=True)
        sum_ref[1:2, :] = dv_total

    spec = lambda off: pl.BlockSpec((SEQ, 2 * HD), lambda i: (0, i + off + start))
    full = lambda s: pl.BlockSpec(s, lambda i: (0,) * len(s))
    return pl.pallas_call(
        kernel,
        grid=(count,),
        in_specs=[spec(0), spec(PAIRS), spec(2 * PAIRS), spec(0), spec(0),
                  pl.BlockSpec((1, 8, SEQ), lambda i: (i + start, 0, 0)), full((SEQ, 1)),
                  full((1, SEQ))] + [ANY] * len(before),
        out_specs=[spec(0), spec(0), spec(0), pl.BlockSpec((8, 2 * HD), lambda i: (0, i + start))],
        input_output_aliases={8 + i: i for i in range(len(before))},
        out_shape=[jax.ShapeDtypeStruct((SEQ, D), BF)] * 3 + [jax.ShapeDtypeStruct((8, D), F32)],
        scratch_shapes=[pltpu.VMEM((2 * HD, SEQ), F32), pltpu.VMEM((2 * HD, SEQ), BF)],
        compiler_params=params(),
        cost_estimate=cost(6 * count),
        name="attend_back",
    )(qkv, qkv, qkv, context, grad_context, lse, seg_col, seg_row, *before)


def middle(me, context, x, g, vectors, up_bias, weight2, weight3):
    kind2, refs2 = weight2
    kind3, refs3 = weight3
    count = copy_count(weight2)
    blocks = x.shape[0] // ROWS

    def kernel(me_ref, c_ref, x_ref, g_ref, vec_ref, ub_ref, *rest):
        w2, w3 = rest[: len(refs2)], rest[len(refs2) : len(refs2) + len(refs3)]
        o_refs = rest[len(refs2) + len(refs3) :][:blocks]
        (act_ref, gpre_ref, n1_ref, gffn_ref, gattn_ref, gres_ref, gctx_ref,
         sum_ref, usum_ref, wo, wu, wd, slope, s_o, s_u, s_d) = rest[len(refs2) + len(refs3) + blocks :]
        step = pl.program_id(0)
        bits = bits_of(me_ref)
        co = weight_copies(kind2, w2, (0, D // 2), (0, D), wo, s_o, bits)
        cu = weight_copies(kind2, w2, (D // 2, FF // 2), (D, FF), wu, s_u, bits)
        cd = weight_copies(kind3, w3, None, (0, D), wd, s_d, bits)

        @pl.when(step == 0)
        def _():
            start_all(co)
            start_all(cu)
            start_all(cd)
            sum_ref[...] = jnp.zeros_like(sum_ref)
            usum_ref[...] = jnp.zeros_like(usum_ref)
            wait_all(co)

        out_bias, gain1, shift1 = vec_ref[0:1], vec_ref[1:2], vec_ref[2:3]
        down_bias, gain2, shift2 = vec_ref[3:4], vec_ref[4:5], vec_ref[5:6]
        attn = nn(c_ref[...], wo[...]) + out_bias
        xhat1, rstd1 = norm_rows(x_ref[...].astype(F32) + attn)
        normed1 = xhat1 * gain1 + shift1
        low1 = normed1.astype(BF)
        n1_ref[...] = low1

        @pl.when(step == 0)
        def _():
            wait_all(cu)
            wait_all(cd)

        ffn = jnp.zeros((ROWS, D), F32)
        for lo in range(0, FF, D):
            at = slice(lo, lo + D)
            pre = nn(low1, wu[:, at]) + ub_ref[:, at]
            act, sl = gelu_with_slope(pre)
            act = act.astype(BF)
            act_ref[:, at] = act
            slope[:, at] = sl
            ffn = ffn + nn(act, wd[at, :])
        xhat2, rstd2 = norm_rows(normed1 + (ffn + down_bias))
        out = (xhat2 * gain2 + shift2).astype(BF)
        put_block(o_refs, step, out)
        gr = g_ref[...].astype(F32)
        res2 = norm_rows_back(gr * gain2, xhat2, rstd2)
        gffn = res2.astype(BF)
        gffn_ref[...] = gffn
        rs = lambda v: jnp.sum(v, 0, keepdims=True)
        sum_ref[0:1] += rs(gr * xhat2)
        sum_ref[1:2] += rs(gr)
        sum_ref[2:3] += rs(gffn.astype(F32))
        gn1 = res2
        for lo in range(0, FF, D):
            at = slice(lo, lo + D)
            gpre = (nt(gffn, wd[at, :]) * slope[:, at]).astype(BF)
            gpre_ref[:, at] = gpre
            usum_ref[0:1, at] += rs(gpre.astype(F32))
            gn1 = gn1 + nt(gpre, wu[:, at])
        sum_ref[3:4] += rs(gn1 * xhat1)
        sum_ref[4:5] += rs(gn1)
        res1 = norm_rows_back(gn1 * gain1, xhat1, rstd1)
        gres_ref[...] = res1
        gattn = res1.astype(BF)
        gattn_ref[...] = gattn
        sum_ref[5:6] += rs(gattn.astype(F32))
        gctx_ref[...] = nt(gattn, wo[...]).astype(BF)

    rows = x.shape[0]
    blk = lambda n: pl.BlockSpec((ROWS, n), lambda i, me: (i, 0))
    full = lambda s: pl.BlockSpec(s, lambda i, me: (0,) * len(s))
    sd = jax.ShapeDtypeStruct
    return pl.pallas_call(
        kernel,
        grid_spec=pltpu.PrefetchScalarGridSpec(
            num_scalar_prefetch=1,
            grid=(rows // ROWS,),
            in_specs=[blk(D), blk(D), blk(D), full((8, D)), full((1, FF))]
            + [ANY] * (len(refs2) + len(refs3)),
            out_specs=[full((ROWS, D))] * blocks + [blk(FF), blk(FF), blk(D), blk(D), blk(D), blk(D), blk(D),
                       full((8, D)), full((8, FF))],
            scratch_shapes=[
                pltpu.VMEM((D, D), BF), pltpu.VMEM((D, FF), BF), pltpu.VMEM((FF, D), BF),
                pltpu.VMEM((ROWS, FF), F32),
                pltpu.SemaphoreType.DMA((count,)), pltpu.SemaphoreType.DMA((count,)),
                pltpu.SemaphoreType.DMA((count,)),
            ],
        ),
        out_shape=[sd((ROWS, D), BF)] * blocks + [sd((rows, FF), BF), sd((rows, FF), BF), sd((rows, D), BF),
                   sd((rows, D), BF), sd((rows, D), BF), sd((rows, D), F32), sd((rows, D), BF),
                   sd((8, D), F32), sd((8, FF), F32)],
        compiler_params=params(),
        cost_estimate=cost(48),
        name="middle",
    )(me, context, x, g, vectors, up_bias, *refs2, *refs3)


def grad_down(me, act, grad_ffn, fsdp):
    per = FF // fsdp
    steps = 8
    width = FF // steps
    inner = width // per

    def kernel(me_ref, a_ref, g_ref, send_ref, keep_ref, acc_ref):
        core, _ = bits_of(me_ref)
        acc_ref[...] = tn(a_ref[...], g_ref[...])
        n = per // 2
        for i in range(inner):
            take = lambda b: acc_ref[pl.ds(pl.multiple_of(i * per + n * b, n), n), :].astype(BF)
            send_ref[i] = take(1 - core)
            keep_ref[i] = take(core)

    rows = act.shape[0]
    out = jax.ShapeDtypeStruct((fsdp, per // 2, D), BF)
    ospec = pl.BlockSpec((inner, per // 2, D), lambda i, me: (i, 0, 0))
    return pl.pallas_call(
        kernel,
        grid_spec=pltpu.PrefetchScalarGridSpec(
            num_scalar_prefetch=1,
            grid=(steps,),
            in_specs=[pl.BlockSpec((rows, width), lambda i, me: (0, i)),
                      pl.BlockSpec((rows, D), lambda i, me: (0, 0))],
            out_specs=[ospec, ospec],
            scratch_shapes=[pltpu.VMEM((width, D), F32)],
        ),
        out_shape=[out, out],
        compiler_params=params(),
        cost_estimate=cost(12),
        name="grad_down",
    )(me, act, grad_ffn)


def halves_out(rows, width):
    specs = [pl.BlockSpec((rows, width), lambda i, me: (0, 0))] * 2
    shapes = [jax.ShapeDtypeStruct((rows, width), BF)] * 2
    return specs, shapes


def half_of(i, core):
    return jnp.where(i == 0, 1 - core, core)


def grad_up_out(me, low1, grad_pre, context, grad_attn):
    wu, wo = FF // 2, D // 2

    def kernel(me_ref, l_ref, p_ref, c_ref, a_ref, send_ref, keep_ref):
        def fill(o_ref):
            o_ref[:, :wo] = tn(c_ref[...], a_ref[...]).astype(BF)
            low = l_ref[...]
            for lo in range(0, wu, D):
                o_ref[:, wo + lo : wo + lo + D] = tn(low, p_ref[:, lo : lo + D]).astype(BF)

        pl.when(pl.program_id(0) == 0)(lambda: fill(send_ref))
        pl.when(pl.program_id(0) == 1)(lambda: fill(keep_ref))

    rows = low1.shape[0]
    half = lambda n: pl.BlockSpec(
        (rows, n), lambda i, me: (0, half_of(i, lax.bitwise_and(me[0], 1))))
    full = pl.BlockSpec((rows, D), lambda i, me: (0, 0))
    specs, shapes = halves_out(D, wu + wo)
    return pl.pallas_call(
        kernel,
        grid_spec=pltpu.PrefetchScalarGridSpec(
            num_scalar_prefetch=1, grid=(2,),
            in_specs=[full, half(wu), full, half(wo)], out_specs=specs),
        out_shape=shapes,
        compiler_params=params(),
        cost_estimate=cost(12),
        name="grad_up_out",
    )(me, low1, grad_pre, context, grad_attn)


def grad_qkv(me, x, dq, dk, dv, sums, up_sums, bias_sums, fsdp):
    w = 3 * D // 2
    per, per_up = D // fsdp, FF // fsdp
    tall = per + 16

    def kernel(me_ref, x_ref, q_ref, k_ref, v_ref, s_ref, u_ref, b_ref, send_ref, keep_ref):
        core, _ = bits_of(me_ref)

        def put(o_ref, lo, val):
            val = val.astype(BF)
            for d in range(fsdp):
                o_ref[d, :per, lo : lo + val.shape[1]] = val[d * per : (d + 1) * per]

        def fill(o_ref, b):
            @pl.when(b == 0)
            def _():
                put(o_ref, 0, tn(x_ref[...], q_ref[...]))
                put(o_ref, D, tn(x_ref[...], k_ref[:, : D // 2]))

            @pl.when(b == 1)
            def _():
                put(o_ref, 0, tn(x_ref[...], k_ref[:, D // 2 :]))
                put(o_ref, D // 2, tn(x_ref[...], v_ref[...]))

            rows = jnp.concatenate([s_ref[0:6], b_ref[0:2]], 0)
            for d in range(fsdp):
                o_ref[d, per:, :] = jnp.zeros((16, w), BF)
                o_ref[d, per : per + 8, :per] = rows[:, d * per : (d + 1) * per].astype(BF)
                o_ref[d, per + 8 : per + 9, :per_up] = u_ref[0:1, d * per_up : (d + 1) * per_up].astype(BF)

        pl.when(pl.program_id(0) == 0)(lambda: fill(send_ref, 1 - core))
        pl.when(pl.program_id(0) == 1)(lambda: fill(keep_ref, core))

    rows = x.shape[0]
    full = lambda s: pl.BlockSpec(s, lambda i, me: (0, 0))
    return pl.pallas_call(
        kernel,
        grid_spec=pltpu.PrefetchScalarGridSpec(
            num_scalar_prefetch=1, grid=(2,),
            in_specs=[full((rows, D))] * 4 + [full((8, D)), full((8, FF)), full((8, D))],
            out_specs=[pl.BlockSpec((fsdp, tall, w), lambda i, me: (0, 0, 0))] * 2),
        out_shape=[jax.ShapeDtypeStruct((fsdp, tall, w), BF)] * 2,
        compiler_params=params(),
        cost_estimate=cost(9),
        name="grad_qkv",
    )(me, x, dq, dk, dv, sums, up_sums, bias_sums)


def grad_in(me, dq, dk, dv, res1, weight):
    kind, refs = weight
    n = 3 * D
    count = copy_count(weight)

    def kernel(me_ref, q_ref, k_ref, v_ref, r_ref, *rest):
        w_refs, o_refs, (w_ref, sems) = rest[: len(refs)], rest[len(refs) : -2], rest[-2:]

        @pl.when(pl.program_id(0) == 0)
        def _():
            copies = weight_copies(kind, w_refs, (0, n // 2), (0, n), w_ref, sems, bits_of(me_ref))
            start_all(copies)
            wait_all(copies)

        total = r_ref[...] + nt(q_ref[...], w_ref[:, :D])
        total = total + nt(k_ref[...], w_ref[:, D : 2 * D])
        total = total + nt(v_ref[...], w_ref[:, 2 * D :])
        put_block(o_refs, pl.program_id(0), total.astype(BF))

    rows = dq.shape[0]
    blocks = rows // ROWS
    blk = pl.BlockSpec((ROWS, D), lambda i, me: (i, 0))
    return pl.pallas_call(
        kernel,
        grid_spec=pltpu.PrefetchScalarGridSpec(
            num_scalar_prefetch=1, grid=(rows // ROWS,),
            in_specs=[blk] * 4 + [ANY] * len(refs),
            out_specs=[pl.BlockSpec((ROWS, D), lambda i, me: (0, 0))] * blocks,
            scratch_shapes=[pltpu.VMEM((D, n), BF), pltpu.SemaphoreType.DMA((count,))]),
        out_shape=[jax.ShapeDtypeStruct((ROWS, D), BF)] * blocks,
        compiler_params=params(),
        cost_estimate=cost(9),
        name="grad_in",
    )(me, dq, dk, dv, res1, *refs)


def local(hidden_in, doc_starts, w_qkv, query_bias, value_bias, w_out, out_bias, norm1_gain,
          norm1_bias, w_up, up_bias, w_down, down_bias, norm2_gain, norm2_bias, cotangent):
    fsdp, sp = lax.axis_size("fsdp"), lax.axis_size("sp")
    seqs, span, _ = hidden_in.shape
    assert sp == 4 and seqs == sp and span * sp == SEQ and span == ROWS
    me = lax.axis_index("sp").astype(jnp.int32)
    core = me & 1
    row = lax.axis_index("fsdp").astype(jnp.int32)
    xb, zs = row & 1, fsdp // 2
    me1 = jnp.stack([me, xb])
    rows_d, rows_f = D // fsdp, FF // fsdp
    split = in_pieces(fsdp)

    def partner(v, bit):
        return lax.ppermute(v, "sp", [(i, i ^ bit) for i in range(sp)])

    def across(v):
        return lax.ppermute(v, "fsdp", [(i, i ^ 1) for i in range(fsdp)])

    lines = [[2 * z + b for z in range(zs)] for b in range(2)]

    def along(v):
        return lax.all_to_all(v, "fsdp", 0, 0, axis_index_groups=lines, tiled=True)

    def swap(parts):
        return [parts[0]] + [partner(parts[r], r) for r in (2, 3, 1)]

    def fetch(v):
        own, two, three, one = swap(deal(me1, v))
        return jnp.concatenate([own, one, two, three], 0)

    def deliver(parts):
        own, two, three, one = swap(parts)
        return place(me1, [own, one, two, three])

    def each(v):
        return jnp.broadcast_to(v[None], (zs,) + v.shape)

    def half_cols(w):
        return lax.dynamic_slice(w, (0, core * (w.shape[1] // 2)), (w.shape[0], w.shape[1] // 2))

    def spread(v):
        a = along(v)
        a = jnp.stack([a, across(a)])
        return a, partner(a, 1)

    small = [out_bias, norm1_gain, norm1_bias, down_bias, norm2_gain, norm2_bias, query_bias,
             value_bias, up_bias]
    x = fetch(hidden_in)
    if split:
        a1 = spread(pack(me1, w_qkv, small, zs))
        every = a1[0][:, :, rows_d:, :rows_f]
        every = jnp.where(xb == 0, every, every[::-1]).transpose(2, 1, 0, 3)
        every = every.astype(F32).reshape(16, fsdp, rows_f)
        table = every[:8, :, :rows_d].reshape(8, D)
        full_up_bias = every[8].reshape(1, FF)
        weight1 = ("cols", a1)
        weight2 = ("cols", spread(each(jnp.concatenate([half_cols(w_out), half_cols(w_up)], 1))))
        down = lax.dynamic_slice(w_down, (core * (rows_f // 2), 0), (rows_f // 2, D))
        weight3 = ("rows", spread(each(down)))
    else:
        every = lax.all_gather(jnp.concatenate(small), "fsdp", axis=0).astype(F32)
        table = every[:, : 8 * rows_d].reshape(fsdp, 8, rows_d).transpose(1, 0, 2).reshape(8, D)
        full_up_bias = every[:, 8 * rows_d :].reshape(1, FF)
        gather = lambda w: lax.all_gather(w, "fsdp", axis=0, tiled=True)
        weight1 = ("whole", (gather(w_qkv),))
        weight2 = ("whole", (gather(jnp.concatenate([w_out, w_up], 1)),))
        weight3 = ("whole", (gather(w_down),))
    g = fetch(cotangent)
    bias_row = jnp.concatenate([table[6:7], jnp.zeros((1, D), F32), table[7:8]], 1)

    starts = lax.dynamic_slice(doc_starts, (me, 0), (1, doc_starts.shape[1]))
    order = jnp.arange(SEQ, dtype=jnp.int32)
    position = ((order // span) ^ me) * span + order % span
    seg = jnp.sum((position[:, None] >= starts).astype(jnp.int32), -1)
    seg_col, seg_row = seg[:, None], seg[None, :]

    qkv = project(me1, x, weight1, bias_row)
    context = ()
    per = PAIRS // PARTS
    for i in range(PARTS):
        context = attend(qkv, seg_col, seg_row, i * per, per, context)
    context, lse = context
    (*out, act, gpre, low1, gffn, gattn, res1, gctx, sums, up_sums) = middle(
        me1, context, x, g, table, full_up_bias, weight2, weight3)
    layer_out = deliver(out)

    def add(a, b):
        return (a.astype(F32) + b.astype(F32)).astype(BF)

    def join(mine, other, axis):
        return jnp.where(core == 0, jnp.concatenate([mine, other], axis),
                         jnp.concatenate([other, mine], axis))

    def reduce_part(send, keep):
        other = partner(send, 1)
        cut = lambda v, b: lax.dynamic_index_in_dim(v.reshape((zs, 2) + v.shape[1:]), b, 1, False)
        theirs = add(cut(keep, 1 - xb), cut(other, 1 - xb))
        mine = add(add(cut(keep, xb), cut(other, xb)), across(theirs))
        total = jnp.sum(along(mine).astype(F32), 0).astype(BF)
        total = add(total, partner(total, 2))
        return total, partner(total, 1)

    def scatter(v):
        part = lax.psum_scatter(v, "fsdp", scatter_dimension=0, tiled=True)
        return lax.psum(part, "sp").astype(F32)

    down_parts = grad_down(me1, act, gffn, fsdp)
    wide_parts = grad_up_out(me1, low1, gpre, context, gattn)
    if split:
        down = reduce_part(*down_parts)
        wide = reduce_part(*[v.reshape(fsdp, rows_d, -1) for v in wide_parts])
    grads = ()
    for i in range(PARTS):
        grads = attend_back(qkv, context, gctx, lse, seg_col, seg_row, i * per, per, grads)
    dq, dk, dv, bias_sums = grads
    qkv_parts = grad_qkv(me1, x, dq, dk, dv, sums, up_sums, bias_sums, fsdp)
    if split:
        qkv_sum = reduce_part(*qkv_parts)
    dx = grad_in(me1, dq, dk, dv, res1, weight1)
    grad_input = deliver(dx)

    if split:
        both = lambda pair, axis: join(pair[0], pair[1], axis).astype(F32)
        grad_down_w = both(down, 0)
        w1 = D // 2
        grad_out = both([v[:, :w1] for v in wide], 1)
        grad_up = both([v[:, w1:] for v in wide], 1)
        grad_q = both([v[:rows_d] for v in qkv_sum], 1)
        tail = qkv_sum[0][rows_d:].astype(F32)
        g2, b2, db, g1, b1, ob, qb, vb = [tail[i, :rows_d] for i in range(8)]
        ub = tail[8, :rows_f]
    else:
        grad_down_w = scatter(join(*down_parts[::-1], 1).reshape(FF, D).astype(F32))
        wide = scatter(join(*wide_parts[::-1], 1).astype(F32))
        w1, w2 = D // 2, FF // 2
        grad_out = jnp.concatenate([wide[:, :w1], wide[:, w1 + w2 : 2 * w1 + w2]], 1)
        grad_up = jnp.concatenate([wide[:, w1 : w1 + w2], wide[:, 2 * w1 + w2 :]], 1)
        grad_q = scatter(join(*[v[:, :rows_d] for v in qkv_parts[::-1]], 2).reshape(D, 3 * D).astype(F32))
        by_dest = jnp.concatenate([sums[:6], bias_sums[:2]], 0).reshape(8, fsdp, rows_d)
        by_dest = by_dest.transpose(1, 0, 2).reshape(fsdp, 8 * rows_d)
        extra = jnp.concatenate([by_dest, up_sums[0].reshape(fsdp, rows_f)], 1)
        tail = scatter(extra).reshape(-1)
        g2, b2, db, g1, b1, ob, qb, vb = [tail[i * rows_d : (i + 1) * rows_d] for i in range(8)]
        ub = tail[8 * rows_d :]
    return (layer_out, grad_input, grad_q, qb, vb, grad_out, ob, g1, b1, grad_up, ub, grad_down_w,
            db, g2, b2)


PARTS = 3


def in_pieces(fsdp):
    return D // fsdp % 32 == 0 and FF // fsdp % 32 == 0


def solution(mesh):
    tok = P("fsdp", "sp", None)
    mat, vec = P("fsdp", None), P("fsdp")
    in_specs = (tok, mat, mat, vec, vec, mat, vec, vec, vec, mat, vec, mat, vec, vec, vec, tok)
    out_specs = (tok, tok, mat, vec, vec, mat, vec, vec, vec, mat, vec, mat, vec, vec, vec)

    return jax.shard_map(local, mesh=mesh, in_specs=in_specs, out_specs=out_specs, check_vma=False)
```

profile of v0, /device:TPU:0, one launch (start us, length us, event | category | flops | bytes accessed | tf_op | source)
XLA Modules:
  0.0 694.6 jit_solution(8235956586754012817)
XLA Ops:
  1.3 2.8 pack.1
  4.0 6.5 all-to-all-start
  10.6 25.3 %all-to-all-done = bf16[4,112,1152]{2,1,0:T(8,128)(2,1)S(1)} async-done(((bf16[4,112,1152]{2,1,0:T(8,128)(2,1)}), bf16[4,112,1152]{2,1,0:T(8,128)(2,1)S(1)}, u32[]{:S(2)}, u32[]{:S(2)}) %all-to-all-start) | async-done | bytes 1032224 | tf_op jit(solution)/shard_map/all_to_all | solution.py:645
  37.1 3.6 all-to-all-start.1
  43.2 31.8 %all-to-all-done.1 = bf16[4,96,1920]{2,1,0:T(8,128)(2,1)S(1)} async-done(((bf16[4,96,1920]{2,1,0:T(8,128)(2,1)}), bf16[4,96,1920]{2,1,0:T(8,128)(2,1)S(1)}, u32[]{:S(2)}, u32[]{:S(2)}) %all-to-all-start.1) | async-done | bytes 1474592 | tf_op jit(solution)/shard_map/all_to_all | solution.py:645
  76.1 4.3 all-to-all-start.2
  80.4 49.5 %deal.2 = (bf16[256,768]{1,0:T(8,128)(2,1)}, bf16[256,768]{1,0:T(8,128)(2,1)}, bf16[256,768]{1,0:T(8,128)(2,1)}, bf16[256,768]{1,0:T(8,128)(2,1)}) custom-call(s32[2]{0:T(128)} %pad_add_fusion.me_ref, bf16[4,256,768]{2,1,0:T(8,128)(2,1)} %v_ref.2), custom_call_target="tpu_custom_call" | custom-call | flops 2000000000 | bytes 1048576 | tf_op jit(solution)/shard_map/deal/pallas_call | solution.py:184
  130.0 1.6 collective-permute-start.1
  131.8 49.4 %deal.3 = (bf16[256,768]{1,0:T(8,128)(2,1)}, bf16[256,768]{1,0:T(8,128)(2,1)}, bf16[256,768]{1,0:T(8,128)(2,1)}, bf16[256,768]{1,0:T(8,128)(2,1)}) custom-call(s32[2]{0:T(128)} %pad_add_fusion.me_ref, bf16[4,256,768]{2,1,0:T(8,128)(2,1)} %v_ref.3), custom_call_target="tpu_custom_call" | custom-call | flops 2000000000 | bytes 1048576 | tf_op jit(solution)/shard_map/deal/pallas_call | solution.py:184
  181.7 2.8 pad_maximum_fusion.2.rest_0_
  190.5 1.8 constant_dynamic-update-slice_fusion.2
  192.9 1.8 constant_dynamic-update-slice_fusion.1
  194.6 1.8 constant_dynamic-update-slice_fusion.x_ref
  196.4 2.1 collective-permute-done.6
  198.4 7.2 %collective-permute-done.7 = bf16[256,768]{1,0:T(8,128)(2,1)} collective-permute-done((bf16[256,768]{1,0:T(8,128)(2,1)}, bf16[256,768]{1,0:T(8,128)(2,1)}, u32[]{:S(2)}, u32[]{:S(2)}) %collective-permute-start.7) | collective-permute-done | bytes 393248 | tf_op jit(solution)/shard_map/ppermute | solution.py:637
  205.6 2.4 pad_maximum_fusion.3.g_ref
  211.0 38.0 %collective-permute-done.10 = bf16[4,192,768]{2,1,0:T(8,128)(2,1)} collective-permute-done((bf16[4,192,768]{2,1,0:T(8,128)(2,1)}, bf16[4,192,768]{2,1,0:T(8,128)(2,1)}, u32[]{:S(2)}, u32[]{:S(2)}) %collective-permute-start.10) | collective-permute-done | bytes 1179680 | tf_op jit(solution)/shard_map/ppermute | solution.py:640
  249.1 3.3 pad_maximum_fusion.1.rest_2_
  252.4 1.7 pad_maximum_fusion.rest_0_
  254.7 9.5 %project.1.q_ref.k_ref.v_ref = bf16[1024,2304]{1,0:T(8,128)(2,1)} custom-call(s32[2]{0:T(128)} %pad_add_fusion.me_ref, bf16[1024,768]{1,0:T(8,128)(2,1)} %constant_dynamic-update-slice_fusion.x_ref, f32[1,2304]{1,0:T(1,128)} %fusion.14.b_ref, bf16[2,4,112,1152]{3,2,1,0:T(8,128)(2,1)} %pad_maximum_fusion.2.rest_0_, ...), custom_call_target="tpu_custom_call" | custom-call | flops 8999999488 | bytes 1048576 | tf_op jit(solution)/shard_map/project/pallas_call | solution.py:236
  264.2 13.6 %attend.3 = (bf16[1024,768]{1,0:T(8,128)(2,1)}, f32[6,8,1024]{2,1,0:T(8,128)}) custom-call(bf16[1024,2304]{1,0:T(8,128)(2,1)} %project.1.q_ref.k_ref.v_ref, bf16[1024,2304]{1,0:T(8,128)(2,1)} %project.1.q_ref.k_ref.v_ref, bf16[1024,2304]{1,0:T(8,128)(2,1)} %project.1.q_ref.k_ref.v_ref, s32[1024,1]{1,0:T(8,128)} %copy.67.sc_ref, s32[1,1024]{1,0:T(1,128)} %bitcast.83), custom_call_target="tpu_custom_call" | custom-call | flops 12000000000 | bytes 1048576 | tf_op jit(solution)/shard_map/attend/pallas_call | solution.py:284
  277.7 14.0 %attend.4 = (bf16[1024,768]{1,0:T(8,128)(2,1)}, f32[6,8,1024]{2,1,0:T(8,128)}) custom-call(bf16[1024,2304]{1,0:T(8,128)(2,1)} %project.1.q_ref.k_ref.v_ref, bf16[1024,2304]{1,0:T(8,128)(2,1)} %project.1.q_ref.k_ref.v_ref, bf16[1024,2304]{1,0:T(8,128)(2,1)} %project.1.q_ref.k_ref.v_ref, ...), custom_call_target="tpu_custom_call", output_to_operand_aliasing={{0}: (5, {}), {1}: (6, {})} | custom-call | flops 12000000000 | bytes 1048576 | tf_op jit(solution)/shard_map/attend/pallas_call | solution.py:284
  291.7 13.5 %attend.5 = (bf16[1024,768]{1,0:T(8,128)(2,1)}, f32[6,8,1024]{2,1,0:T(8,128)}) custom-call(bf16[1024,2304]{1,0:T(8,128)(2,1)} %project.1.q_ref.k_ref.v_ref, bf16[1024,2304]{1,0:T(8,128)(2,1)} %project.1.q_ref.k_ref.v_ref, bf16[1024,2304]{1,0:T(8,128)(2,1)} %project.1.q_ref.k_ref.v_ref, ...), custom_call_target="tpu_custom_call", output_to_operand_aliasing={{0}: (5, {}), {1}: (6, {})} | custom-call | flops 12000000000 | bytes 1048576 | tf_op jit(solution)/shard_map/attend/pallas_call | solution.py:284
  306.9 49.0 %middle.1 = (bf16[256,768]{1,0:T(8,128)(2,1)}, bf16[256,768]{1,0:T(8,128)(2,1)}, bf16[256,768]{1,0:T(8,128)(2,1)}, bf16[256,768]{1,0:T(8,128)(2,1)}, bf16[1024,3...) custom-call(s32[2]{0:T(128)} %pad_add_fusion.me_ref, ...), custom_call_target="tpu_custom_call" | custom-call | flops 48000000000 | bytes 1048576 | tf_op jit(solution)/shard_map/middle/pallas_call | solution.py:439
  355.9 15.0 %attend_back.3 = (bf16[1024,768]{1,0:T(8,128)(2,1)}, bf16[1024,768]{1,0:T(8,128)(2,1)}, bf16[1024,768]{1,0:T(8,128)(2,1)}, f32[8,768]{1,0:T(8,128)}) custom-call(bf16[1024,2304]{1,0:T(8,128)(2,1)} %project.1.q_ref.k_ref.v_ref, bf16[1024,2304]{1,0:T(8,128)(2,1)} %project.1.q_ref.k_ref.v_ref, bf16[1024,2304]{1,0:T(8,128)(2,1)} %project.1.q_ref.k_ref.v_ref, ...), custom_call_target="tpu_custom_call" | custom-call | flops 12000000000 | bytes 1048576 | tf_op jit(solution)/shard_map/attend_back/pallas_call | solution.py:344
  370.9 14.8 %attend_back.4 = (bf16[1024,768]{1,0:T(8,128)(2,1)}, bf16[1024,768]{1,0:T(8,128)(2,1)}, bf16[1024,768]{1,0:T(8,128)(2,1)}, f32[8,768]{1,0:T(8,128)}) custom-call(bf16[1024,2304]{1,0:T(8,128)(2,1)} %project.1.q_ref.k_ref.v_ref, ...), custom_call_target="tpu_custom_call", output_to_operand_aliasing={{0}: (8, {}), {1}: (9, {}), {2}: (10, {}), {3}: (11, {})} | custom-call | flops 12000000000 | bytes 1048576 | tf_op jit(solution)/shard_map/attend_back/pallas_call | solution.py:344
  385.7 15.3 %attend_back.5 = (bf16[1024,768]{1,0:T(8,128)(2,1)}, bf16[1024,768]{1,0:T(8,128)(2,1)}, bf16[1024,768]{1,0:T(8,128)(2,1)}, f32[8,768]{1,0:T(8,128)}) custom-call(bf16[1024,2304]{1,0:T(8,128)(2,1)} %project.1.q_ref.k_ref.v_ref, ...), custom_call_target="tpu_custom_call", output_to_operand_aliasing={{0}: (8, {}), {1}: (9, {}), {2}: (10, {}), {3}: (11, {})} | custom-call | flops 12000000000 | bytes 1048576 | tf_op jit(solution)/shard_map/attend_back/pallas_call | solution.py:344
  401.0 10.2 %grad_qkv.1 = (bf16[8,112,1152]{2,1,0:T(8,128)(2,1)}, bf16[8,112,1152]{2,1,0:T(8,128)(2,1)}) custom-call(s32[2]{0:T(128)} %pad_add_fusion.me_ref, bf16[1024,768]{1,0:T(8,128)(2,1)} %constant_dynamic-update-slice_fusion.x_ref, bf16[1024,768]{1,0:T(8,128)(2,1)} %get-tuple-element.91.q_ref, bf16[1024,768]{1,0:T(8,128)(2,1)} %get-tuple-element.92.k_ref, ...), custom_call_target="tpu_custom_call" | custom-call | flops 8999999488 | bytes 1048576 | tf_op jit(solution)/shard_map/grad_qkv/pallas_call | solution.py:574
  411.4 12.5 %grad_down.1 = (bf16[8,192,768]{2,1,0:T(8,128)(2,1)}, bf16[8,192,768]{2,1,0:T(8,128)(2,1)}) custom-call(s32[2]{0:T(128)} %pad_add_fusion.me_ref, bf16[1024,3072]{1,0:T(8,128)(2,1)} %get-tuple-element.109.a_ref, bf16[1024,768]{1,0:T(8,128)(2,1)} %get-tuple-element.110.g_ref), custom_call_target="tpu_custom_call" | custom-call | flops 12000000000 | bytes 1048576 | tf_op jit(solution)/shard_map/grad_down/pallas_call | solution.py:482
  424.1 13.5 %grad_up_out.1 = (bf16[768,1920]{1,0:T(8,128)(2,1)}, bf16[768,1920]{1,0:T(8,128)(2,1)}) custom-call(s32[2]{0:T(128)} %pad_add_fusion.me_ref, bf16[1024,768]{1,0:T(8,128)(2,1)} %get-tuple-element.104.l_ref, bf16[1024,3072]{1,0:T(8,128)(2,1)} %get-tuple-element.105.p_ref, bf16[1024,768]{1,0:T(8,128)(2,1)} %get-tuple-element.72.c_ref.o_ref, ...), custom_call_target="tpu_custom_call" | custom-call | flops 12000000000 | bytes 1048576 | tf_op jit(solution)/shard_map/grad_up_out/pallas_call | solution.py:527
  440.9 23.5 %collective-permute-done.19 = bf16[4,112,1152]{2,1,0:T(8,128)(2,1)S(1)} collective-permute-done((bf16[4,112,1152]{2,1,0:T(8,128)(2,1)S(1)}, bf16[4,112,1152]{2,1,0:T(8,128)(2,1)S(1)}, u32[]{:S(2)}, u32[]{:S(2)}) %collective-permute-start.19) | collective-permute-done | bytes 1032224 | tf_op jit(solution)/shard_map/ppermute | solution.py:640
  464.4 3.0 fusion.2
  467.4 5.0 all-to-all-start.3
  472.5 1.7 fusion.6
  475.8 2.8 fusion.4
  479.1 23.9 %collective-permute-done.27 = bf16[4,192,768]{2,1,0:T(8,128)(2,1)S(1)} collective-permute-done((bf16[4,192,768]{2,1,0:T(8,128)(2,1)S(1)}, bf16[4,192,768]{2,1,0:T(8,128)(2,1)S(1)}, u32[]{:S(2)}, u32[]{:S(2)}) %collective-permute-start.27) | collective-permute-done | bytes 1179680 | tf_op jit(solution)/shard_map/ppermute | solution.py:640
  503.1 2.7 fusion.1
  505.8 5.1 all-to-all-start.5
  510.9 22.0 %collective-permute-done.23 = bf16[4,96,1920]{2,1,0:T(8,128)(2,1)} collective-permute-done((bf16[4,96,1920]{2,1,0:T(8,128)(2,1)}, bf16[4,96,1920]{2,1,0:T(8,128)(2,1)}, u32[]{:S(2)}, u32[]{:S(2)}) %collective-permute-start.23) | collective-permute-done | bytes 1474592 | tf_op jit(solution)/shard_map/ppermute | solution.py:640
  532.9 3.9 fusion
  536.9 4.8 all-to-all-start.4
  541.7 10.6 %grad_in.1 = (bf16[256,768]{1,0:T(8,128)(2,1)}, bf16[256,768]{1,0:T(8,128)(2,1)}, bf16[256,768]{1,0:T(8,128)(2,1)}, bf16[256,768]{1,0:T(8,128)(2,1)}) custom-call(s32[2]{0:T(128)} %pad_add_fusion.me_ref, bf16[1024,768]{1,0:T(8,128)(2,1)} %get-tuple-element.91.q_ref, bf16[1024,768]{1,0:T(8,128)(2,1)} %get-tuple-element.92.k_ref, ...), custom_call_target="tpu_custom_call" | custom-call | flops 8999999488 | bytes 1048576 | tf_op jit(solution)/shard_map/grad_in/pallas_call | solution.py:609
  557.5 7.2 %collective-permute-done.16.rest_2_ = bf16[256,768]{1,0:T(8,128)(2,1)} collective-permute-done((bf16[256,768]{1,0:T(8,128)(2,1)}, bf16[256,768]{1,0:T(8,128)(2,1)}, u32[]{:S(2)}, u32[]{:S(2)}) %collective-permute-start.16) | collective-permute-done | bytes 393248 | tf_op jit(solution)/shard_map/ppermute | solution.py:637
  566.3 5.9 collective-permute-done.17.rest_3_
  572.2 49.4 %place.3 = bf16[4,256,768]{2,1,0:T(8,128)(2,1)} custom-call(s32[2]{0:T(128)} %pad_add_fusion.me_ref, bf16[256,768]{1,0:T(8,128)(2,1)} %get-tuple-element.95.rest_0_, bf16[256,768]{1,0:T(8,128)(2,1)} %collective-permute-done.15.rest_1_, bf16[256,768]{1,0:T(8,128)(2,1)} %collective-permute-done.16.rest_2_, bf16[256,768]{1,0:T(8,128)(2,1)} %collective-permute-done.17.rest_3_), custom_call_target="tpu_custom_call" | custom-call | flops 2000000000 | bytes 1048576 | tf_op jit(solution)/shard_map/place/pallas_call | solution.py:204
  621.7 49.5 %place.2 = bf16[4,256,768]{2,1,0:T(8,128)(2,1)} custom-call(s32[2]{0:T(128)} %pad_add_fusion.me_ref, bf16[256,768]{1,0:T(8,128)(2,1)} %get-tuple-element.77.rest_0_, bf16[256,768]{1,0:T(8,128)(2,1)} %collective-permute-done.12.rest_1_, bf16[256,768]{1,0:T(8,128)(2,1)} %collective-permute-done.13.rest_2_, bf16[256,768]{1,0:T(8,128)(2,1)} %collective-permute-done.14.rest_3_), custom_call_target="tpu_custom_call" | custom-call | flops 2000000000 | bytes 1048576 | tf_op jit(solution)/shard_map/place/pallas_call | solution.py:204
  679.4 3.7 collective-permute-done.28
  683.3 6.8 collective-permute-done.24
  (124 shorter events, 43.2 us)
Async XLA Ops:
  0.6 9.9 %copy-start = (bf16[96,3072]{1,0:T(8,128)(2,1)S(1)}, bf16[96,3072]{1,0:T(8,128)(2,1)}, u32[]{:S(2)}) copy-start(bf16[96,3072]{1,0:T(8,128)(2,1)} %param.25) | copy-start | bytes 1769476
  4.0 6.5 copy-start.9
  4.0 31.9 %all-to-all-start = ((bf16[4,112,1152]{2,1,0:T(8,128)(2,1)}), bf16[4,112,1152]{2,1,0:T(8,128)(2,1)S(1)}, u32[]{:S(2)}, u32[]{:S(2)}) async-start(bf16[4,112,1152]{2,1,0:T(8,128)(2,1)} %pack.1), calls=%async_computation | async-start | bytes 2064384 | tf_op jit(solution)/shard_map/all_to_all | solution.py:645
  37.1 37.9 %all-to-all-start.1 = ((bf16[4,96,1920]{2,1,0:T(8,128)(2,1)}), bf16[4,96,1920]{2,1,0:T(8,128)(2,1)S(1)}, u32[]{:S(2)}, u32[]{:S(2)}) async-start(bf16[4,96,1920]{2,1,0:T(8,128)(2,1)} %broadcast_in_dim.25), calls=%async_computation.1 | async-start | bytes 2949120 | tf_op jit(solution)/shard_map/all_to_all | solution.py:645
  40.6 141.0 %collective-permute-start.3 = (bf16[4,112,1152]{2,1,0:T(8,128)(2,1)S(1)}, bf16[4,112,1152]{2,1,0:T(8,128)(2,1)}, u32[]{:S(2)}, u32[]{:S(2)}) collective-permute-start(bf16[4,112,1152]{2,1,0:T(8,128)(2,1)S(1)} %all-to-all-done), channel_id=1, source_target_pairs={{0,4},{4,0},{8,12},{12,8},{16,20},{20,16},{24,28},{28,24},{1,5},{5... | collective-permute-start | bytes 3096584 | tf_op jit(solution)/shard_map/ppermute | solution.py:640
  76.1 116.2 %all-to-all-start.2 = ((bf16[4,192,768]{2,1,0:T(8,128)(2,1)}), bf16[4,192,768]{2,1,0:T(8,128)(2,1)}, u32[]{:S(2)}, u32[]{:S(2)}) async-start(bf16[4,192,768]{2,1,0:T(8,128)(2,1)} %broadcast_in_dim.26), calls=%async_computation.2 | async-start | bytes 2359296 | tf_op jit(solution)/shard_map/all_to_all | solution.py:645
  129.9 56.3 %collective-permute-start = (bf16[256,768]{1,0:T(8,128)(2,1)}, bf16[256,768]{1,0:T(8,128)(2,1)}, u32[]{:S(2)}, u32[]{:S(2)}) collective-permute-start(bf16[256,768]{1,0:T(8,128)(2,1)} %get-tuple-element.65), channel_id=1, source_target_pairs={{0,1},{1,0},{2,3},{3,2},{4,5},{5,4},{6,7},{7,6},{8,9},{9,8},{10,11... | collective-permute-start | bytes 1179656 | tf_op jit(solution)/shard_map/ppermute | solution.py:637
  130.0 57.7 %collective-permute-start.1 = (bf16[256,768]{1,0:T(8,128)(2,1)}, bf16[256,768]{1,0:T(8,128)(2,1)}, u32[]{:S(2)}, u32[]{:S(2)}) collective-permute-start(bf16[256,768]{1,0:T(8,128)(2,1)} %get-tuple-element.66), channel_id=1, source_target_pairs={{0,2},{1,3},{2,0},{3,1},{4,6},{5,7},{6,4},{7,5},{8,10},{9,11},{10,... | collective-permute-start | bytes 1179656 | tf_op jit(solution)/shard_map/ppermute | solution.py:637
  131.5 57.4 %collective-permute-start.2 = (bf16[256,768]{1,0:T(8,128)(2,1)}, bf16[256,768]{1,0:T(8,128)(2,1)}, u32[]{:S(2)}, u32[]{:S(2)}) collective-permute-start(bf16[256,768]{1,0:T(8,128)(2,1)} %get-tuple-element.67), channel_id=1, source_target_pairs={{0,3},{1,2},{2,1},{3,0},{4,7},{5,6},{6,5},{7,4},{8,11},{9,10},{10,... | collective-permute-start | bytes 1179656 | tf_op jit(solution)/shard_map/ppermute | solution.py:637
  181.3 11.1 %collective-permute-start.5 = (bf16[256,768]{1,0:T(8,128)(2,1)}, bf16[256,768]{1,0:T(8,128)(2,1)S(1)}, u32[]{:S(2)}, u32[]{:S(2)}) collective-permute-start(bf16[256,768]{1,0:T(8,128)(2,1)} %get-tuple-element.74), channel_id=1, source_target_pairs={{0,1},{1,0},{2,3},{3,2},{4,5},{5,4},{6,7},{7,6},{8,9},{9,8},{10,11... | collective-permute-start | bytes 1179656 | tf_op jit(solution)/shard_map/ppermute | solution.py:637
  181.7 3.7 copy-start.8
  184.5 70.2 %collective-permute-start.4 = (bf16[2,4,112,1152]{3,2,1,0:T(8,128)(2,1)}, bf16[2,4,112,1152]{3,2,1,0:T(8,128)(2,1)}, u32[]{:S(2)}, u32[]{:S(2)}) collective-permute-start(bf16[2,4,112,1152]{3,2,1,0:T(8,128)(2,1)} %pad_maximum_fusion.2.rest_0_), channel_id=1, source_target_pairs={{0,1},{1,0},{2,3},{3,2},{4,5},{5,4},{6,7},{7,6},{8,9},{9,8},{10,11... | collective-permute-start | bytes 6193160 | tf_op jit(solution)/shard_map/ppermute | solution.py:637
  186.1 19.5 %copy-start.7 = (bf16[256,768]{1,0:T(8,128)(2,1)S(1)}, bf16[256,768]{1,0:T(8,128)(2,1)}, u32[]{:S(2)}) copy-start(bf16[256,768]{1,0:T(8,128)(2,1)} %get-tuple-element.73) | copy-start | bytes 1179652
  186.1 12.3 %collective-permute-start.6 = (bf16[256,768]{1,0:T(8,128)(2,1)}, bf16[256,768]{1,0:T(8,128)(2,1)}, u32[]{:S(2)}, u32[]{:S(2)}) collective-permute-start(bf16[256,768]{1,0:T(8,128)(2,1)} %get-tuple-element.75), channel_id=1, source_target_pairs={{0,2},{1,3},{2,0},{3,1},{4,6},{5,7},{6,4},{7,5},{8,10},{9,11},{10,... | collective-permute-start | bytes 1179656 | tf_op jit(solution)/shard_map/ppermute | solution.py:637
  187.7 18.0 %collective-permute-start.7 = (bf16[256,768]{1,0:T(8,128)(2,1)}, bf16[256,768]{1,0:T(8,128)(2,1)}, u32[]{:S(2)}, u32[]{:S(2)}) collective-permute-start(bf16[256,768]{1,0:T(8,128)(2,1)} %get-tuple-element.76), channel_id=1, source_target_pairs={{0,3},{1,2},{2,1},{3,0},{4,7},{5,6},{6,5},{7,4},{8,11},{9,10},{10,... | collective-permute-start | bytes 1179656 | tf_op jit(solution)/shard_map/ppermute | solution.py:637
  187.9 20.1 %copy-start.10 = (s32[1024]{0:T(1024)}, s32[1024]{0:T(1024)S(1)}, u32[]{:S(2)}) copy-start(s32[1024]{0:T(1024)S(1)} %convert_reduce_fusion) | copy-start | bytes 12292
  189.0 63.4 %collective-permute-start.8 = (bf16[4,96,1920]{2,1,0:T(8,128)(2,1)S(1)}, bf16[4,96,1920]{2,1,0:T(8,128)(2,1)}, u32[]{:S(2)}, u32[]{:S(2)}) collective-permute-start(bf16[4,96,1920]{2,1,0:T(8,128)(2,1)S(1)} %all-to-all-done.1), channel_id=1, source_target_pairs={{0,4},{4,0},{8,12},{12,8},{16,20},{20,16},{24,28},{28,24},{1,5},{5... | collective-permute-start | bytes 4423688 | tf_op jit(solution)/shard_map/ppermute | solution.py:640
  192.3 56.7 %collective-permute-start.10 = (bf16[4,192,768]{2,1,0:T(8,128)(2,1)}, bf16[4,192,768]{2,1,0:T(8,128)(2,1)}, u32[]{:S(2)}, u32[]{:S(2)}) collective-permute-start(bf16[4,192,768]{2,1,0:T(8,128)(2,1)} %all-to-all-done.2), channel_id=1, source_target_pairs={{0,4},{4,0},{8,12},{12,8},{16,20},{20,16},{24,28},{28,24},{1,5},{5... | collective-permute-start | bytes 3538952 | tf_op jit(solution)/shard_map/ppermute | solution.py:640
  252.4 52.9 %collective-permute-start.11 = (bf16[2,4,192,768]{3,2,1,0:T(8,128)(2,1)}, bf16[2,4,192,768]{3,2,1,0:T(8,128)(2,1)}, u32[]{:S(2)}, u32[]{:S(2)}) collective-permute-start(bf16[2,4,192,768]{3,2,1,0:T(8,128)(2,1)} %pad_maximum_fusion.1.rest_2_), channel_id=1, source_target_pairs={{0,1},{1,0},{2,3},{3,2},{4,5},{5,4},{6,7},{7,6},{8,9},{9,8},{10,11... | collective-permute-start | bytes 7077896 | tf_op jit(solution)/shard_map/ppermute | solution.py:637
  254.1 10.1 %copy-start.4 = (bf16[2,4,96,1920]{3,2,1,0:T(8,128)(2,1)}, bf16[2,4,96,1920]{3,2,1,0:T(8,128)(2,1)S(1)}, u32[]{:S(2)}) copy-start(bf16[2,4,96,1920]{3,2,1,0:T(8,128)(2,1)S(1)} %pad_maximum_fusion.rest_0_) | copy-start | bytes 8847364
  254.1 51.2 %collective-permute-start.9 = (bf16[2,4,96,1920]{3,2,1,0:T(8,128)(2,1)S(1)}, bf16[2,4,96,1920]{3,2,1,0:T(8,128)(2,1)S(1)}, u32[]{:S(2)}, u32[]{:S(2)}) collective-permute-start(bf16[2,4,96,1920]{3,2,1,0:T(8,128)(2,1)S(1)} %pad_maximum_fusion.rest_0_), channel_id=1, source_target_pairs={{0,1},{1,0},{2,3},{3,2},{4,5},{5,4},{6,7},{7,6},{8,9},{9,8},{10,11... | collective-permute-start | bytes 8847368 | tf_op jit(solution)/shard_map/ppermute | solution.py:637
  305.3 1.6 copy-start.11
  411.1 26.8 %collective-permute-start.18 = (bf16[8,112,1152]{2,1,0:T(8,128)(2,1)}, bf16[8,112,1152]{2,1,0:T(8,128)(2,1)}, u32[]{:S(2)}, u32[]{:S(2)}) collective-permute-start(bf16[8,112,1152]{2,1,0:T(8,128)(2,1)} %get-tuple-element.103), channel_id=1, source_target_pairs={{0,1},{1,0},{2,3},{3,2},{4,5},{5,4},{6,7},{7,6},{8,9},{9,8},{10,11... | collective-permute-start | bytes 6193160 | tf_op jit(solution)/shard_map/ppermute | solution.py:637
  423.9 48.6 %collective-permute-start.26 = (bf16[8,192,768]{2,1,0:T(8,128)(2,1)}, bf16[8,192,768]{2,1,0:T(8,128)(2,1)}, u32[]{:S(2)}, u32[]{:S(2)}) collective-permute-start(bf16[8,192,768]{2,1,0:T(8,128)(2,1)} %get-tuple-element.112), channel_id=1, source_target_pairs={{0,1},{1,0},{2,3},{3,2},{4,5},{5,4},{6,7},{7,6},{8,9},{9,8},{10,11... | collective-permute-start | bytes 7077896 | tf_op jit(solution)/shard_map/ppermute | solution.py:637
  424.1 13.8 %copy-start.6 = (bf16[8,112,1152]{2,1,0:T(8,128)(2,1)S(1)}, bf16[8,112,1152]{2,1,0:T(8,128)(2,1)}, u32[]{:S(2)}) copy-start(bf16[8,112,1152]{2,1,0:T(8,128)(2,1)} %get-tuple-element.102) | copy-start | bytes 6193156
  437.6 38.1 %collective-permute-start.22 = (bf16[8,96,1920]{2,1,0:T(8,128)(2,1)}, bf16[8,96,1920]{2,1,0:T(8,128)(2,1)}, u32[]{:S(2)}, u32[]{:S(2)}) collective-permute-start(bf16[8,96,1920]{2,1,0:T(8,128)(2,1)} %bitcast.89), channel_id=1, source_target_pairs={{0,1},{1,0},{2,3},{3,2},{4,5},{5,4},{6,7},{7,6},{8,9},{9,8},{10,11... | collective-permute-start | bytes 8847368 | tf_op jit(solution)/shard_map/ppermute | solution.py:637
  439.4 25.0 %collective-permute-start.19 = (bf16[4,112,1152]{2,1,0:T(8,128)(2,1)S(1)}, bf16[4,112,1152]{2,1,0:T(8,128)(2,1)S(1)}, u32[]{:S(2)}, u32[]{:S(2)}) collective-permute-start(bf16[4,112,1152]{2,1,0:T(8,128)(2,1)S(1)} %fusion.8), channel_id=1, source_target_pairs={{0,4},{4,0},{8,12},{12,8},{16,20},{20,16},{24,28},{28,24},{1,5},{5... | collective-permute-start | bytes 3096584 | tf_op jit(solution)/shard_map/ppermute | solution.py:640
  464.4 8.1 %copy-start.5 = (bf16[8,192,768]{2,1,0:T(8,128)(2,1)S(1)}, bf16[8,192,768]{2,1,0:T(8,128)(2,1)}, u32[]{:S(2)}) copy-start(bf16[8,192,768]{2,1,0:T(8,128)(2,1)} %get-tuple-element.111) | copy-start | bytes 7077892
  467.4 38.4 %all-to-all-start.3 = ((bf16[4,112,1152]{2,1,0:T(8,128)(2,1)}), bf16[4,112,1152]{2,1,0:T(8,128)(2,1)S(1)}, u32[]{:S(2)}, u32[]{:S(2)}) async-start(bf16[4,112,1152]{2,1,0:T(8,128)(2,1)} %fusion.2), calls=%async_computation.3 | async-start | bytes 2064384 | tf_op jit(solution)/shard_map/all_to_all | solution.py:645
  472.5 3.3 copy-start.3
  474.2 28.9 %collective-permute-start.27 = (bf16[4,192,768]{2,1,0:T(8,128)(2,1)S(1)}, bf16[4,192,768]{2,1,0:T(8,128)(2,1)S(1)}, u32[]{:S(2)}, u32[]{:S(2)}) collective-permute-start(bf16[4,192,768]{2,1,0:T(8,128)(2,1)S(1)} %fusion.6), channel_id=1, source_target_pairs={{0,4},{4,0},{8,12},{12,8},{16,20},{20,16},{24,28},{28,24},{1,5},{5... | collective-permute-start | bytes 3538952 | tf_op jit(solution)/shard_map/ppermute | solution.py:640
  478.6 54.4 %collective-permute-start.23 = (bf16[4,96,1920]{2,1,0:T(8,128)(2,1)}, bf16[4,96,1920]{2,1,0:T(8,128)(2,1)}, u32[]{:S(2)}, u32[]{:S(2)}) collective-permute-start(bf16[4,96,1920]{2,1,0:T(8,128)(2,1)} %fusion.4), channel_id=1, source_target_pairs={{0,4},{4,0},{8,12},{12,8},{16,20},{20,16},{24,28},{28,24},{1,5},{5... | collective-permute-start | bytes 4423688 | tf_op jit(solution)/shard_map/ppermute | solution.py:640
  505.8 31.0 %copy-start.2 = (bf16[4,112,1152]{2,1,0:T(8,128)(2,1)}, bf16[4,112,1152]{2,1,0:T(8,128)(2,1)S(1)}, u32[]{:S(2)}) copy-start(bf16[4,112,1152]{2,1,0:T(8,128)(2,1)S(1)} %all-to-all-done.3) | copy-start | bytes 3096580
  505.8 31.0 %all-to-all-start.5 = ((bf16[4,192,768]{2,1,0:T(8,128)(2,1)}), bf16[4,192,768]{2,1,0:T(8,128)(2,1)S(1)}, u32[]{:S(2)}, u32[]{:S(2)}) async-start(bf16[4,192,768]{2,1,0:T(8,128)(2,1)} %fusion.1), calls=%async_computation.5 | async-start | bytes 2359296 | tf_op jit(solution)/shard_map/all_to_all | solution.py:645
  536.9 137.9 %all-to-all-start.4 = ((bf16[4,96,1920]{2,1,0:T(8,128)(2,1)}), bf16[4,96,1920]{2,1,0:T(8,128)(2,1)S(1)}, u32[]{:S(2)}, u32[]{:S(2)}) async-start(bf16[4,96,1920]{2,1,0:T(8,128)(2,1)} %fusion), calls=%async_computation.4 | async-start | bytes 2949120 | tf_op jit(solution)/shard_map/all_to_all | solution.py:645
  552.3 3.8 collective-permute-start.15
  552.4 12.4 %collective-permute-start.16 = (bf16[256,768]{1,0:T(8,128)(2,1)}, bf16[256,768]{1,0:T(8,128)(2,1)}, u32[]{:S(2)}, u32[]{:S(2)}) collective-permute-start(bf16[256,768]{1,0:T(8,128)(2,1)} %get-tuple-element.97), channel_id=1, source_target_pairs={{0,2},{1,3},{2,0},{3,1},{4,6},{5,7},{6,4},{7,5},{8,10},{9,11},{10,... | collective-permute-start | bytes 1179656 | tf_op jit(solution)/shard_map/ppermute | solution.py:637
  554.0 18.2 %collective-permute-start.17 = (bf16[256,768]{1,0:T(8,128)(2,1)}, bf16[256,768]{1,0:T(8,128)(2,1)}, u32[]{:S(2)}, u32[]{:S(2)}) collective-permute-start(bf16[256,768]{1,0:T(8,128)(2,1)} %get-tuple-element.98), channel_id=1, source_target_pairs={{0,3},{1,2},{2,1},{3,0},{4,7},{5,6},{6,5},{7,4},{8,11},{9,10},{10,... | collective-permute-start | bytes 1179656 | tf_op jit(solution)/shard_map/ppermute | solution.py:637
  554.2 67.4 %collective-permute-start.12 = (bf16[256,768]{1,0:T(8,128)(2,1)}, bf16[256,768]{1,0:T(8,128)(2,1)}, u32[]{:S(2)}, u32[]{:S(2)}) collective-permute-start(bf16[256,768]{1,0:T(8,128)(2,1)} %get-tuple-element.78), channel_id=1, source_target_pairs={{0,1},{1,0},{2,3},{3,2},{4,5},{5,4},{6,7},{7,6},{8,9},{9,8},{10,11... | collective-permute-start | bytes 1179656 | tf_op jit(solution)/shard_map/ppermute | solution.py:637
  554.6 67.1 %collective-permute-start.13 = (bf16[256,768]{1,0:T(8,128)(2,1)}, bf16[256,768]{1,0:T(8,128)(2,1)}, u32[]{:S(2)}, u32[]{:S(2)}) collective-permute-start(bf16[256,768]{1,0:T(8,128)(2,1)} %get-tuple-element.79), channel_id=1, source_target_pairs={{0,2},{1,3},{2,0},{3,1},{4,6},{5,7},{6,4},{7,5},{8,10},{9,11},{10,... | collective-permute-start | bytes 1179656 | tf_op jit(solution)/shard_map/ppermute | solution.py:637
  556.1 65.6 %collective-permute-start.14 = (bf16[256,768]{1,0:T(8,128)(2,1)}, bf16[256,768]{1,0:T(8,128)(2,1)}, u32[]{:S(2)}, u32[]{:S(2)}) collective-permute-start(bf16[256,768]{1,0:T(8,128)(2,1)} %get-tuple-element.80), channel_id=1, source_target_pairs={{0,3},{1,2},{2,1},{3,0},{4,7},{5,6},{6,5},{7,4},{8,11},{9,10},{10,... | collective-permute-start | bytes 1179656 | tf_op jit(solution)/shard_map/ppermute | solution.py:637
  564.7 106.4 %collective-permute-start.20 = (bf16[112,1152]{1,0:T(8,128)(2,1)S(1)}, bf16[112,1152]{1,0:T(8,128)(2,1)S(1)}, u32[]{:S(2)}, u32[]{:S(2)}) collective-permute-start(bf16[112,1152]{1,0:T(8,128)(2,1)S(1)} %reduce_sum.46), channel_id=1, source_target_pairs={{0,2},{1,3},{2,0},{3,1},{4,6},{5,7},{6,4},{7,5},{8,10},{9,11},{10,... | collective-permute-start | bytes 774152 | tf_op jit(solution)/shard_map/ppermute | solution.py:637
  671.2 7.2 %collective-permute-start.21 = (bf16[112,1152]{1,0:T(8,128)(2,1)S(1)}, bf16[112,1152]{1,0:T(8,128)(2,1)}, u32[]{:S(2)}, u32[]{:S(2)}) collective-permute-start(bf16[112,1152]{1,0:T(8,128)(2,1)S(1)} %add_convert_fusion.8), channel_id=1, source_target_pairs={{0,1},{1,0},{2,3},{3,2},{4,5},{5,4},{6,7},{7,6},{8,9},{9,8},{10,11... | collective-permute-start | bytes 774152 | tf_op jit(solution)/shard_map/ppermute | solution.py:637
  673.2 9.9 %collective-permute-start.28 = (bf16[192,768]{1,0:T(8,128)(2,1)S(1)}, bf16[192,768]{1,0:T(8,128)(2,1)S(1)}, u32[]{:S(2)}, u32[]{:S(2)}) collective-permute-start(bf16[192,768]{1,0:T(8,128)(2,1)S(1)} %reduce_sum.48), channel_id=1, source_target_pairs={{0,2},{1,3},{2,0},{3,1},{4,6},{5,7},{6,4},{7,5},{8,10},{9,11},{10,... | collective-permute-start | bytes 884744 | tf_op jit(solution)/shard_map/ppermute | solution.py:637
  675.0 15.1 %collective-permute-start.24 = (bf16[96,1920]{1,0:T(8,128)(2,1)S(1)}, bf16[96,1920]{1,0:T(8,128)(2,1)S(1)}, u32[]{:S(2)}, u32[]{:S(2)}) collective-permute-start(bf16[96,1920]{1,0:T(8,128)(2,1)S(1)} %reduce_sum.47), channel_id=1, source_target_pairs={{0,2},{1,3},{2,0},{3,1},{4,6},{5,7},{6,4},{7,5},{8,10},{9,11},{10,... | collective-permute-start | bytes 1105928 | tf_op jit(solution)/shard_map/ppermute | solution.py:637
  683.2 8.0 %collective-permute-start.29 = (bf16[192,768]{1,0:T(8,128)(2,1)S(1)}, bf16[192,768]{1,0:T(8,128)(2,1)S(1)}, u32[]{:S(2)}, u32[]{:S(2)}) collective-permute-start(bf16[192,768]{1,0:T(8,128)(2,1)S(1)} %add_convert_fusion.7), channel_id=1, source_target_pairs={{0,1},{1,0},{2,3},{3,2},{4,5},{5,4},{6,7},{7,6},{8,9},{9,8},{10,11... | collective-permute-start | bytes 884744 | tf_op jit(solution)/shard_map/ppermute | solution.py:637
  690.2 2.3 collective-permute-start.25
  692.4 2.0 copy-start.1
where the time goes:
time: 703 us; the launch traced here: 695 us
  Pallas kernels  392 us (56%)
  waiting for transfers between devices  198 us (28%)
  starting transfers between devices  50.8 us (7%)
  other arithmetic  34.8 us (5%)
  local copies, waits for them, and re-layouts  18.1 us (3%)
    ppermute x6, waiting for transfers between devices, across(): return lax.ppermute(v, 'fsdp', [(i, i ^ 1) for i in range(fsdp)])  107 us
    pallas_call x2, Pallas kernels, deal(): pl.pallas_call(kernel, in_specs=[pl.BlockSpec(memory_space=pltpu.SMEM), A...  98.9 us
    pallas_call x2, Pallas kernels, place(): pl.pallas_call(kernel, in_specs=[pl.BlockSpec(memory_space=pltpu.SMEM)] +...  98.9 us
    all_to_all x6, waiting for transfers between devices, along(): return lax.all_to_all(v, 'fsdp', 0, 0, axis_index_groups=lines, tiled=True)  57.1 us
    pallas_call x1, Pallas kernels, middle(): pl.pallas_call(kernel, grid_spec=pltpu.PrefetchScalarGridSpec(num_scalar_...  49 us
    pallas_call x3, Pallas kernels, attend_back(): pl.pallas_call(kernel, grid=(count,), in_specs=[spec(0), spec(PAIRS), spe...  45.1 us
    pallas_call x3, Pallas kernels, attend(): pl.pallas_call(kernel, grid=(count,), in_specs=[spec(0), spec(PAIRS), spe...  41.1 us
    ppermute x24, waiting for transfers between devices, partner(): return lax.ppermute(v, 'sp', [(i, i ^ bit) for i in range(sp)])  33 us
  transfers between devices with their start and end apart: 36, of which 12 were waited for; matrix products, arithmetic and copies ran while one was open for 7% of the time, Pallas kernels for 41%

commit v1 on v0

--- a/solution.py
+++ b/solution.py
@@ -172,53 +172,77 @@
     )(me, w, *vectors)
 
 
+def block_at(r):
+    return pl.BlockSpec((None, ROWS, D), lambda i, me: (lax.bitwise_xor(me[0], r), 0, 0))
+
+
+WHOLE = pl.BlockSpec((ROWS, D), lambda i, me: (0, 0))
+
+
 def deal(me, v):
-    def kernel(me_ref, v_ref, *rest):
-        o_refs, sems = rest[:-1], rest[-1]
-        copies = [pltpu.make_async_copy(v_ref.at[lax.bitwise_xor(me_ref[0], r)], o, sems.at[r])
-                  for r, o in enumerate(o_refs)]
-        start_all(copies)
-        wait_all(copies)
-
-    n = v.shape[0]
-    return pl.pallas_call(
-        kernel,
-        in_specs=[pl.BlockSpec(memory_space=pltpu.SMEM), ANY],
-        out_specs=[ANY] * n,
-        out_shape=[jax.ShapeDtypeStruct(v.shape[1:], v.dtype)] * n,
-        scratch_shapes=[pltpu.SemaphoreType.DMA((n,))],
+    away = v.shape[0] - 1
+
+    def kernel(me_ref, *refs):
+        for r in range(away):
+            refs[away + r][...] = refs[r][...]
+
+    return pl.pallas_call(
+        kernel,
+        grid_spec=pltpu.PrefetchScalarGridSpec(
+            num_scalar_prefetch=1, grid=(1,),
+            in_specs=[block_at(r + 1) for r in range(away)],
+            out_specs=[WHOLE] * away),
+        out_shape=[jax.ShapeDtypeStruct((ROWS, D), v.dtype)] * away,
+        compiler_params=params(),
         cost_estimate=cost(2),
         name="deal",
-    )(me, v)
+    )(me, *([v] * away))
 
 
 def place(me, parts):
-    def kernel(me_ref, *rest):
-        p_refs, (o_ref, sems) = rest[:-2], rest[-2:]
-        copies = [pltpu.make_async_copy(p, o_ref.at[lax.bitwise_xor(me_ref[0], r)], sems.at[r])
-                  for r, p in enumerate(p_refs)]
-        start_all(copies)
-        wait_all(copies)
-
     n = len(parts)
-    return pl.pallas_call(
-        kernel,
-        in_specs=[pl.BlockSpec(memory_space=pltpu.SMEM)] + [ANY] * n,
-        out_specs=ANY,
-        out_shape=jax.ShapeDtypeStruct((n,) + parts[0].shape, parts[0].dtype),
-        scratch_shapes=[pltpu.SemaphoreType.DMA((n,))],
+
+    def kernel(me_ref, *refs):
+        for r in range(n):
+            @pl.when(pl.program_id(0) == r)
+            def _():
+                refs[n][...] = refs[r][...]
+
+    return pl.pallas_call(
+        kernel,
+        grid_spec=pltpu.PrefetchScalarGridSpec(
+            num_scalar_prefetch=1, grid=(n,),
+            in_specs=[WHOLE] * n,
+            out_specs=pl.BlockSpec((None, ROWS, D), lambda i, me: (lax.bitwise_xor(me[0], i), 0, 0))),
+        out_shape=jax.ShapeDtypeStruct((n, ROWS, D), parts[0].dtype),
+        compiler_params=params(),
         cost_estimate=cost(2),
         name="place",
     )(me, *parts)
 
 
-def project(me, x, weight, bias_row):
+def own_and_near(v, parts):
+    return [v] + list(parts), [block_at(0)] + [WHOLE] * len(parts)
+
+
+def get_block(refs, step, into):
+    for r, ref in enumerate(refs):
+        @pl.when(step == r)
+        def _():
+            into[...] = ref[...]
+
+
+def project(me, x_own, x_near, weight, bias_row):
     kind, refs = weight
     n = 3 * D
     count = copy_count(weight)
 
-    def kernel(me_ref, x_ref, b_ref, *rest):
-        w_refs, (o_ref, w_ref, sems) = rest[:-3], rest[-3:]
+    x_args, x_specs = own_and_near(x_own, x_near)
+    blocks = len(x_args)
+
+    def kernel(me_ref, b_ref, *rest):
+        x_refs, w_refs, (o_ref, x_ref, w_ref, sems) = rest[:blocks], rest[blocks:-4], rest[-4:]
+        get_block(x_refs, pl.program_id(0), x_ref)
 
         @pl.when(pl.program_id(0) == 0)
         def _():
@@ -232,25 +256,22 @@
                 nn(xv, w_ref[:, lo : lo + D]) + b_ref[:, lo : lo + D]
             ).astype(BF)
 
-    rows = x.shape[0]
+    rows = ROWS * blocks
     return pl.pallas_call(
         kernel,
         grid_spec=pltpu.PrefetchScalarGridSpec(
             num_scalar_prefetch=1,
-            grid=(rows // ROWS,),
-            in_specs=[
-                pl.BlockSpec((ROWS, D), lambda i, me: (i, 0)),
-                pl.BlockSpec((1, n), lambda i, me: (0, 0)),
-            ]
-            + [ANY] * len(refs),
-            out_specs=pl.BlockSpec((ROWS, n), lambda i, me: (i, 0)),
+            grid=(blocks,),
+            in_specs=[pl.BlockSpec((1, n), lambda i, me: (0, 0))] + x_specs + [ANY] * len(refs),
+            out_specs=[pl.BlockSpec((ROWS, n), lambda i, me: (i, 0)),
+                       pl.BlockSpec((ROWS, D), lambda i, me: (i, 0))],
             scratch_shapes=[pltpu.VMEM((D, n), BF), pltpu.SemaphoreType.DMA((count,))],
         ),
-        out_shape=jax.ShapeDtypeStruct((rows, n), BF),
+        out_shape=[jax.ShapeDtypeStruct((rows, n), BF), jax.ShapeDtypeStruct((rows, D), BF)],
         compiler_params=params(),
         cost_estimate=cost(9),
         name="project",
-    )(me, x, bias_row, *refs)
+    )(me, bias_row, *x_args, *refs)
 
 
 def attend(qkv, seg_col, seg_row, first, count, before):
@@ -357,18 +378,22 @@
     )(qkv, qkv, qkv, context, grad_context, lse, seg_col, seg_row, *before)
 
 
-def middle(me, context, x, g, vectors, up_bias, weight2, weight3):
+def middle(me, context, x, g_own, g_near, vectors, up_bias, weight2, weight3):
     kind2, refs2 = weight2
     kind3, refs3 = weight3
     count = copy_count(weight2)
     blocks = x.shape[0] // ROWS
 
-    def kernel(me_ref, c_ref, x_ref, g_ref, vec_ref, ub_ref, *rest):
+    g_args, g_specs = own_and_near(g_own, g_near)
+
+    def kernel(me_ref, c_ref, x_ref, vec_ref, ub_ref, *rest):
+        g_refs, rest = rest[:blocks], rest[blocks:]
         w2, w3 = rest[: len(refs2)], rest[len(refs2) : len(refs2) + len(refs3)]
         o_refs = rest[len(refs2) + len(refs3) :][:blocks]
         (act_ref, gpre_ref, n1_ref, gffn_ref, gattn_ref, gres_ref, gctx_ref,
-         sum_ref, usum_ref, wo, wu, wd, slope, s_o, s_u, s_d) = rest[len(refs2) + len(refs3) + blocks :]
+         sum_ref, usum_ref, wo, wu, wd, slope, g_ref, s_o, s_u, s_d) = rest[len(refs2) + len(refs3) + blocks :]
         step = pl.program_id(0)
+        get_block(g_refs, step, g_ref)
         bits = bits_of(me_ref)
         co = weight_copies(kind2, w2, (0, D // 2), (0, D), wo, s_o, bits)
         cu = weight_copies(kind2, w2, (D // 2, FF // 2), (D, FF), wu, s_u, bits)
@@ -441,13 +466,13 @@
         grid_spec=pltpu.PrefetchScalarGridSpec(
             num_scalar_prefetch=1,
             grid=(rows // ROWS,),
-            in_specs=[blk(D), blk(D), blk(D), full((8, D)), full((1, FF))]
+            in_specs=[blk(D), blk(D), full((8, D)), full((1, FF))] + g_specs
             + [ANY] * (len(refs2) + len(refs3)),
             out_specs=[full((ROWS, D))] * blocks + [blk(FF), blk(FF), blk(D), blk(D), blk(D), blk(D), blk(D),
                        full((8, D)), full((8, FF))],
             scratch_shapes=[
                 pltpu.VMEM((D, D), BF), pltpu.VMEM((D, FF), BF), pltpu.VMEM((FF, D), BF),
-                pltpu.VMEM((ROWS, FF), F32),
+                pltpu.VMEM((ROWS, FF), F32), pltpu.VMEM((ROWS, D), BF),
                 pltpu.SemaphoreType.DMA((count,)), pltpu.SemaphoreType.DMA((count,)),
                 pltpu.SemaphoreType.DMA((count,)),
             ],
@@ -458,7 +483,7 @@
         compiler_params=params(),
         cost_estimate=cost(48),
         name="middle",
-    )(me, context, x, g, vectors, up_bias, *refs2, *refs3)
+    )(me, context, x, vectors, up_bias, *g_args, *refs2, *refs3)
 
 
 def grad_down(me, act, grad_ffn, fsdp):
@@ -645,15 +670,14 @@
         return lax.all_to_all(v, "fsdp", 0, 0, axis_index_groups=lines, tiled=True)
 
     def swap(parts):
-        return [parts[0]] + [partner(parts[r], r) for r in (2, 3, 1)]
+        two, three, one = [partner(parts[r - 1], r) for r in (2, 3, 1)]
+        return [one, two, three]
 
     def fetch(v):
-        own, two, three, one = swap(deal(me1, v))
-        return jnp.concatenate([own, one, two, three], 0)
+        return swap(deal(me1, v))
 
     def deliver(parts):
-        own, two, three, one = swap(parts)
-        return place(me1, [own, one, two, three])
+        return place(me1, [parts[0]] + swap(parts[1:]))
 
     def each(v):
         return jnp.broadcast_to(v[None], (zs,) + v.shape)
@@ -668,7 +692,7 @@
 
     small = [out_bias, norm1_gain, norm1_bias, down_bias, norm2_gain, norm2_bias, query_bias,
              value_bias, up_bias]
-    x = fetch(hidden_in)
+    x_near = fetch(hidden_in)
     if split:
         a1 = spread(pack(me1, w_qkv, small, zs))
         every = a1[0][:, :, rows_d:, :rows_f]
@@ -688,7 +712,7 @@
         weight1 = ("whole", (gather(w_qkv),))
         weight2 = ("whole", (gather(jnp.concatenate([w_out, w_up], 1)),))
         weight3 = ("whole", (gather(w_down),))
-    g = fetch(cotangent)
+    g_near = fetch(cotangent)
     bias_row = jnp.concatenate([table[6:7], jnp.zeros((1, D), F32), table[7:8]], 1)
 
     starts = lax.dynamic_slice(doc_starts, (me, 0), (1, doc_starts.shape[1]))
@@ -697,14 +721,14 @@
     seg = jnp.sum((position[:, None] >= starts).astype(jnp.int32), -1)
     seg_col, seg_row = seg[:, None], seg[None, :]
 
-    qkv = project(me1, x, weight1, bias_row)
+    qkv, x = project(me1, hidden_in, x_near, weight1, bias_row)
     context = ()
     per = PAIRS // PARTS
     for i in range(PARTS):
         context = attend(qkv, seg_col, seg_row, i * per, per, context)
     context, lse = context
     (*out, act, gpre, low1, gffn, gattn, res1, gctx, sums, up_sums) = middle(
-        me1, context, x, g, table, full_up_bias, weight2, weight3)
+        me1, context, x, cotangent, g_near, table, full_up_bias, weight2, weight3)
     layer_out = deliver(out)
 
     def add(a, b):

time: 703 us -> 556 us (0.79)
  Pallas kernels: 392 us -> 209 us
  waiting for transfers between devices: 198 us -> 243 us
    pallas_call x4, Pallas kernels: 198 us -> 13.5 us  [the longest x2 7.47 us: place(): pl.pallas_call(kernel, grid_spec=pltpu.PrefetchScalarGridSpec(num_scalar_...]
    ppermute x6, waiting for transfers between devices: 107 us -> 140 us  [across(): return lax.ppermute(v, 'fsdp', [(i, i ^ 1) for i in range(fsdp)])]
    ppermute x24, waiting for transfers between devices: 33 us -> 44.1 us  [partner(): return lax.ppermute(v, 'sp', [(i, i ^ bit) for i in range(sp)])]
  transfers between devices with their start and end apart: 36 -> 36, of which waited for: 12 -> 15; matrix products, arithmetic and copies ran while one was open for 7% -> 7% of each run, Pallas kernels for 41% -> 18%
where the time goes in v1:
time: 556 us; the launch traced here: 548 us
  waiting for transfers between devices  243 us (44%)
  Pallas kernels  209 us (38%)
  starting transfers between devices  48.6 us (9%)
  other arithmetic  32.4 us (6%)
  local copies, waits for them, and re-layouts  13.7 us (2%)
    ppermute x6, waiting for transfers between devices, across(): return lax.ppermute(v, 'fsdp', [(i, i ^ 1) for i in range(fsdp)])  140 us
    all_to_all x6, waiting for transfers between devices, along(): return lax.all_to_all(v, 'fsdp', 0, 0, axis_index_groups=lines, tiled=True)  58.7 us
    pallas_call x1, Pallas kernels, middle(): pl.pallas_call(kernel, grid_spec=pltpu.PrefetchScalarGridSpec(num_scalar_...  49.4 us
    pallas_call x3, Pallas kernels, attend_back(): pl.pallas_call(kernel, grid=(count,), in_specs=[spec(0), spec(PAIRS), spe...  45.1 us
    ppermute x24, waiting for transfers between devices, partner(): return lax.ppermute(v, 'sp', [(i, i ^ bit) for i in range(sp)])  44.1 us
    pallas_call x3, Pallas kernels, attend(): pl.pallas_call(kernel, grid=(count,), in_specs=[spec(0), spec(PAIRS), spe...  41.1 us
    all_to_all x6, starting transfers between devices, along(): return lax.all_to_all(v, 'fsdp', 0, 0, axis_index_groups=lines, tiled=True)  28.9 us
    convert_element_type x9, other arithmetic, add(): return (a.astype(F32) + b.astype(F32)).astype(BF)  17.5 us
  transfers between devices with their start and end apart: 36, of which 15 were waited for; matrix products, arithmetic and copies ran while one was open for 7% of the time, Pallas kernels for 18%

profile of v1, /device:TPU:0, one launch (start us, length us, event | category | flops | bytes accessed | tf_op | source)
XLA Modules:
  0.0 547.6 jit_solution(17404322783717200620)
XLA Ops:
  1.3 2.8 pack.1
  4.0 6.5 %all-to-all-start = ((bf16[4,112,1152]{2,1,0:T(8,128)(2,1)}), bf16[4,112,1152]{2,1,0:T(8,128)(2,1)S(1)}, u32[]{:S(2)}, u32[]{:S(2)}) async-start(bf16[4,112,1152]{2,1,0:T(8,128)(2,1)} %pack.1), calls=%async_computation | async-start | bytes 2064384 | tf_op jit(solution)/shard_map/all_to_all | solution.py:670
  10.6 25.3 %all-to-all-done = bf16[4,112,1152]{2,1,0:T(8,128)(2,1)S(1)} async-done(((bf16[4,112,1152]{2,1,0:T(8,128)(2,1)}), bf16[4,112,1152]{2,1,0:T(8,128)(2,1)S(1)}, u32[]{:S(2)}, u32[]{:S(2)}) %all-to-all-start) | async-done | bytes 1032224 | tf_op jit(solution)/shard_map/all_to_all | solution.py:670
  37.1 3.6 all-to-all-start.1
  41.6 33.4 %all-to-all-done.1 = bf16[4,96,1920]{2,1,0:T(8,128)(2,1)S(1)} async-done(((bf16[4,96,1920]{2,1,0:T(8,128)(2,1)}), bf16[4,96,1920]{2,1,0:T(8,128)(2,1)S(1)}, u32[]{:S(2)}, u32[]{:S(2)}) %all-to-all-start.1) | async-done | bytes 1474592 | tf_op jit(solution)/shard_map/all_to_all | solution.py:670
  76.1 4.3 all-to-all-start.2
  81.9 22.3 %collective-permute-done = bf16[4,112,1152]{2,1,0:T(8,128)(2,1)S(1)} collective-permute-done((bf16[4,112,1152]{2,1,0:T(8,128)(2,1)S(1)}, bf16[4,112,1152]{2,1,0:T(8,128)(2,1)S(1)}, u32[]{:S(2)}, u32[]{:S(2)}) %collective-permute-start) | collective-permute-done | bytes 1032224 | tf_op jit(solution)/shard_map/ppermute | solution.py:665
  104.3 1.7 pad_maximum_fusion.2.rest_4_.rest_0_
  106.0 2.9 deal.2
  114.8 3.1 deal.3
  120.2 50.0 %collective-permute-done.10 = bf16[4,192,768]{2,1,0:T(8,128)(2,1)} collective-permute-done((bf16[4,192,768]{2,1,0:T(8,128)(2,1)}, bf16[4,192,768]{2,1,0:T(8,128)(2,1)}, u32[]{:S(2)}, u32[]{:S(2)}) %collective-permute-start.10) | collective-permute-done | bytes 1179680 | tf_op jit(solution)/shard_map/ppermute | solution.py:665
  170.2 1.8 pad_maximum_fusion.1.rest_6_
  172.8 3.4 pad_maximum_fusion.rest_4_
  178.2 3.6 collective-permute-done.3.rest_3_
  182.6 9.9 %project.1 = (bf16[1024,2304]{1,0:T(8,128)(2,1)}, bf16[1024,768]{1,0:T(8,128)(2,1)}) custom-call(s32[2]{0:T(128)} %pad_add_fusion.me_ref, f32[1,2304]{1,0:T(1,128)} %fusion.14.b_ref, bf16[4,256,768]{2,1,0:T(8,128)(2,1)} %rest_0_.4, bf16[256,768]{1,0:T(8,128)(2,1)} %copy-done.13, bf16[256,768]{1,0:T(8,128)(2,1)} %collective-permute-done.2.rest_2_, ...), custom_call_target="tpu_custom_call" | custom-call | flops 8999999488 | bytes 1048576 | tf_op jit(solution)/shard_map/project/pallas_call | solution.py:260
  192.5 13.6 %attend.3 = (bf16[1024,768]{1,0:T(8,128)(2,1)}, f32[6,8,1024]{2,1,0:T(8,128)}) custom-call(bf16[1024,2304]{1,0:T(8,128)(2,1)} %get-tuple-element.67.q_ref.k_ref.v_ref, bf16[1024,2304]{1,0:T(8,128)(2,1)} %get-tuple-element.67.q_ref.k_ref.v_ref, bf16[1024,2304]{1,0:T(8,128)(2,1)} %get-tuple-element.67.q_ref.k_ref.v_ref, s32[1024,1]{1,0:T(8,128)} %copy.67.sc_ref, ...), custom_call_target="tpu_custom_call" | custom-call | flops 12000000000 | bytes 1048576 | tf_op jit(solution)/shard_map/attend/pallas_call | solution.py:305
  206.1 14.0 %attend.4 = (bf16[1024,768]{1,0:T(8,128)(2,1)}, f32[6,8,1024]{2,1,0:T(8,128)}) custom-call(bf16[1024,2304]{1,0:T(8,128)(2,1)} %get-tuple-element.67.q_ref.k_ref.v_ref, bf16[1024,2304]{1,0:T(8,128)(2,1)} %get-tuple-element.67.q_ref.k_ref.v_ref, bf16[1024,2304]{1,0:T(8,128)(2,1)} %get-tuple-element.67.q_ref.k_ref.v_ref, ...), custom_call_target="tpu_custom_call", output_to_operand_aliasing={{0}: (5, {}), {1}: (6, {})} | custom-call | flops 12000000000 | bytes 1048576 | tf_op jit(solution)/shard_map/attend/pallas_call | solution.py:305
  220.1 13.5 %attend.5 = (bf16[1024,768]{1,0:T(8,128)(2,1)}, f32[6,8,1024]{2,1,0:T(8,128)}) custom-call(bf16[1024,2304]{1,0:T(8,128)(2,1)} %get-tuple-element.67.q_ref.k_ref.v_ref, bf16[1024,2304]{1,0:T(8,128)(2,1)} %get-tuple-element.67.q_ref.k_ref.v_ref, bf16[1024,2304]{1,0:T(8,128)(2,1)} %get-tuple-element.67.q_ref.k_ref.v_ref, ...), custom_call_target="tpu_custom_call", output_to_operand_aliasing={{0}: (5, {}), {1}: (6, {})} | custom-call | flops 12000000000 | bytes 1048576 | tf_op jit(solution)/shard_map/attend/pallas_call | solution.py:305
  235.2 49.4 %middle.1 = (bf16[256,768]{1,0:T(8,128)(2,1)}, bf16[256,768]{1,0:T(8,128)(2,1)}, bf16[256,768]{1,0:T(8,128)(2,1)}, bf16[256,768]{1,0:T(8,128)(2,1)}, bf16[1024,3...) custom-call(s32[2]{0:T(128)} %pad_add_fusion.me_ref, ...), custom_call_target="tpu_custom_call" | custom-call | flops 48000000000 | bytes 1048576 | tf_op jit(solution)/shard_map/middle/pallas_call | solution.py:464
  284.6 15.0 %attend_back.3 = (bf16[1024,768]{1,0:T(8,128)(2,1)}, bf16[1024,768]{1,0:T(8,128)(2,1)}, bf16[1024,768]{1,0:T(8,128)(2,1)}, f32[8,768]{1,0:T(8,128)}) custom-call(bf16[1024,2304]{1,0:T(8,128)(2,1)} %get-tuple-element.67.q_ref.k_ref.v_ref, bf16[1024,2304]{1,0:T(8,128)(2,1)} %get-tuple-element.67.q_ref.k_ref.v_ref, ...), custom_call_target="tpu_custom_call" | custom-call | flops 12000000000 | bytes 1048576 | tf_op jit(solution)/shard_map/attend_back/pallas_call | solution.py:365
  299.6 14.8 %attend_back.4 = (bf16[1024,768]{1,0:T(8,128)(2,1)}, bf16[1024,768]{1,0:T(8,128)(2,1)}, bf16[1024,768]{1,0:T(8,128)(2,1)}, f32[8,768]{1,0:T(8,128)}) custom-call(bf16[1024,2304]{1,0:T(8,128)(2,1)} %get-tuple-element.67.q_ref.k_ref.v_ref, ...), custom_call_target="tpu_custom_call", output_to_operand_aliasing={{0}: (8, {}), {1}: (9, {}), {2}: (10, {}), {3}: (11, {})} | custom-call | flops 12000000000 | bytes 1048576 | tf_op jit(solution)/shard_map/attend_back/pallas_call | solution.py:365
  314.4 15.3 %attend_back.5 = (bf16[1024,768]{1,0:T(8,128)(2,1)}, bf16[1024,768]{1,0:T(8,128)(2,1)}, bf16[1024,768]{1,0:T(8,128)(2,1)}, f32[8,768]{1,0:T(8,128)}) custom-call(bf16[1024,2304]{1,0:T(8,128)(2,1)} %get-tuple-element.67.q_ref.k_ref.v_ref, ...), custom_call_target="tpu_custom_call", output_to_operand_aliasing={{0}: (8, {}), {1}: (9, {}), {2}: (10, {}), {3}: (11, {})} | custom-call | flops 12000000000 | bytes 1048576 | tf_op jit(solution)/shard_map/attend_back/pallas_call | solution.py:365
  329.7 10.2 %grad_qkv.1 = (bf16[8,112,1152]{2,1,0:T(8,128)(2,1)}, bf16[8,112,1152]{2,1,0:T(8,128)(2,1)}) custom-call(s32[2]{0:T(128)} %pad_add_fusion.me_ref, bf16[1024,768]{1,0:T(8,128)(2,1)} %get-tuple-element.73.x_ref, bf16[1024,768]{1,0:T(8,128)(2,1)} %get-tuple-element.91.q_ref, bf16[1024,768]{1,0:T(8,128)(2,1)} %get-tuple-element.92.k_ref, ...), custom_call_target="tpu_custom_call" | custom-call | flops 8999999488 | bytes 1048576 | tf_op jit(solution)/shard_map/grad_qkv/pallas_call | solution.py:599
  340.4 12.4 %grad_down.1 = (bf16[8,192,768]{2,1,0:T(8,128)(2,1)}, bf16[8,192,768]{2,1,0:T(8,128)(2,1)}) custom-call(s32[2]{0:T(128)} %pad_add_fusion.me_ref, bf16[1024,3072]{1,0:T(8,128)(2,1)} %get-tuple-element.109.a_ref, bf16[1024,768]{1,0:T(8,128)(2,1)} %get-tuple-element.110.g_ref), custom_call_target="tpu_custom_call" | custom-call | flops 12000000000 | bytes 1048576 | tf_op jit(solution)/shard_map/grad_down/pallas_call | solution.py:507
  352.8 13.5 %grad_up_out.1 = (bf16[768,1920]{1,0:T(8,128)(2,1)}, bf16[768,1920]{1,0:T(8,128)(2,1)}) custom-call(s32[2]{0:T(128)} %pad_add_fusion.me_ref, bf16[1024,768]{1,0:T(8,128)(2,1)} %get-tuple-element.104.l_ref, bf16[1024,3072]{1,0:T(8,128)(2,1)} %get-tuple-element.105.p_ref, bf16[1024,768]{1,0:T(8,128)(2,1)} %get-tuple-element.72.c_ref.o_ref, ...), custom_call_target="tpu_custom_call" | custom-call | flops 12000000000 | bytes 1048576 | tf_op jit(solution)/shard_map/grad_up_out/pallas_call | solution.py:552
  366.8 2.4 fusion.8
  370.8 23.6 %collective-permute-done.19 = bf16[4,112,1152]{2,1,0:T(8,128)(2,1)} collective-permute-done((bf16[4,112,1152]{2,1,0:T(8,128)(2,1)}, bf16[4,112,1152]{2,1,0:T(8,128)(2,1)}, u32[]{:S(2)}, u32[]{:S(2)}) %collective-permute-start.19) | collective-permute-done | bytes 1032224 | tf_op jit(solution)/shard_map/ppermute | solution.py:665
  394.3 2.9 fusion.2
  397.2 4.7 all-to-all-start.3
  401.9 2.1 fusion.6
  403.9 1.6 collective-permute-start.27
  405.5 3.0 fusion.4
  409.1 23.8 %collective-permute-done.27 = bf16[4,192,768]{2,1,0:T(8,128)(2,1)S(1)} collective-permute-done((bf16[4,192,768]{2,1,0:T(8,128)(2,1)S(1)}, bf16[4,192,768]{2,1,0:T(8,128)(2,1)S(1)}, u32[]{:S(2)}, u32[]{:S(2)}) %collective-permute-start.27) | collective-permute-done | bytes 1179680 | tf_op jit(solution)/shard_map/ppermute | solution.py:665
  432.9 2.8 fusion.1
  436.6 5.1 all-to-all-start.5
  441.7 20.7 %collective-permute-done.23 = bf16[4,96,1920]{2,1,0:T(8,128)(2,1)S(1)} collective-permute-done((bf16[4,96,1920]{2,1,0:T(8,128)(2,1)}, bf16[4,96,1920]{2,1,0:T(8,128)(2,1)S(1)}, u32[]{:S(2)}, u32[]{:S(2)}) %collective-permute-start.23) | collective-permute-done | bytes 1474592 | tf_op jit(solution)/shard_map/ppermute | solution.py:665
  462.4 3.5 fusion
  465.8 4.8 all-to-all-start.4
  470.6 10.6 %grad_in.1 = (bf16[256,768]{1,0:T(8,128)(2,1)}, bf16[256,768]{1,0:T(8,128)(2,1)}, bf16[256,768]{1,0:T(8,128)(2,1)}, bf16[256,768]{1,0:T(8,128)(2,1)}) custom-call(s32[2]{0:T(128)} %pad_add_fusion.me_ref, bf16[1024,768]{1,0:T(8,128)(2,1)} %get-tuple-element.91.q_ref, bf16[1024,768]{1,0:T(8,128)(2,1)} %get-tuple-element.92.k_ref, ...), custom_call_target="tpu_custom_call" | custom-call | flops 8999999488 | bytes 1048576 | tf_op jit(solution)/shard_map/grad_in/pallas_call | solution.py:634
  486.5 7.3 %collective-permute-done.16.refs_2_ = bf16[256,768]{1,0:T(8,128)(2,1)} collective-permute-done((bf16[256,768]{1,0:T(8,128)(2,1)}, bf16[256,768]{1,0:T(8,128)(2,1)}, u32[]{:S(2)}, u32[]{:S(2)}) %collective-permute-start.16) | collective-permute-done | bytes 393248 | tf_op jit(solution)/shard_map/ppermute | solution.py:662
  494.3 6.7 %collective-permute-done.17.refs_3_ = bf16[256,768]{1,0:T(8,128)(2,1)} collective-permute-done((bf16[256,768]{1,0:T(8,128)(2,1)}, bf16[256,768]{1,0:T(8,128)(2,1)}, u32[]{:S(2)}, u32[]{:S(2)}) %collective-permute-start.17) | collective-permute-done | bytes 393248 | tf_op jit(solution)/shard_map/ppermute | solution.py:662
  501.1 3.7 place.3
  504.8 5.8 %collective-permute-done.13.refs_2_ = bf16[256,768]{1,0:T(8,128)(2,1)} collective-permute-done((bf16[256,768]{1,0:T(8,128)(2,1)}, bf16[256,768]{1,0:T(8,128)(2,1)}, u32[]{:S(2)}, u32[]{:S(2)}) %collective-permute-start.13) | collective-permute-done | bytes 393248 | tf_op jit(solution)/shard_map/ppermute | solution.py:662
  510.6 7.3 %collective-permute-done.14.refs_3_ = bf16[256,768]{1,0:T(8,128)(2,1)} collective-permute-done((bf16[256,768]{1,0:T(8,128)(2,1)}, bf16[256,768]{1,0:T(8,128)(2,1)}, u32[]{:S(2)}, u32[]{:S(2)}) %collective-permute-start.14) | collective-permute-done | bytes 393248 | tf_op jit(solution)/shard_map/ppermute | solution.py:662
  517.9 3.7 place.2
  521.7 2.2 collective-permute-done.20
  531.9 3.8 collective-permute-done.28
  535.8 7.3 %collective-permute-done.24 = bf16[96,1920]{1,0:T(8,128)(2,1)S(1)} collective-permute-done((bf16[96,1920]{1,0:T(8,128)(2,1)S(1)}, bf16[96,1920]{1,0:T(8,128)(2,1)S(1)}, u32[]{:S(2)}, u32[]{:S(2)}) %collective-permute-start.24) | collective-permute-done | bytes 368672 | tf_op jit(solution)/shard_map/ppermute | solution.py:662
  (129 shorter events, 40.9 us)
Async XLA Ops:
  0.6 9.9 %copy-start = (bf16[96,3072]{1,0:T(8,128)(2,1)S(1)}, bf16[96,3072]{1,0:T(8,128)(2,1)}, u32[]{:S(2)}) copy-start(bf16[96,3072]{1,0:T(8,128)(2,1)} %param.25) | copy-start | bytes 1769476
  4.0 6.5 %copy-start.10 = (bf16[96,768]{1,0:T(8,128)(2,1)S(1)}, bf16[96,768]{1,0:T(8,128)(2,1)}, u32[]{:S(2)}) copy-start(bf16[96,768]{1,0:T(8,128)(2,1)} %param.21) | copy-start | bytes 442372
  4.0 31.9 %all-to-all-start = ((bf16[4,112,1152]{2,1,0:T(8,128)(2,1)}), bf16[4,112,1152]{2,1,0:T(8,128)(2,1)S(1)}, u32[]{:S(2)}, u32[]{:S(2)}) async-start(bf16[4,112,1152]{2,1,0:T(8,128)(2,1)} %pack.1), calls=%async_computation | async-start | bytes 2064384 | tf_op jit(solution)/shard_map/all_to_all | solution.py:670
  37.1 37.9 %all-to-all-start.1 = ((bf16[4,96,1920]{2,1,0:T(8,128)(2,1)}), bf16[4,96,1920]{2,1,0:T(8,128)(2,1)S(1)}, u32[]{:S(2)}, u32[]{:S(2)}) async-start(bf16[4,96,1920]{2,1,0:T(8,128)(2,1)} %broadcast_in_dim.25), calls=%async_computation.1 | async-start | bytes 2949120 | tf_op jit(solution)/shard_map/all_to_all | solution.py:670
  76.1 36.3 %all-to-all-start.2 = ((bf16[4,192,768]{2,1,0:T(8,128)(2,1)}), bf16[4,192,768]{2,1,0:T(8,128)(2,1)}, u32[]{:S(2)}, u32[]{:S(2)}) async-start(bf16[4,192,768]{2,1,0:T(8,128)(2,1)} %broadcast_in_dim.26), calls=%async_computation.2 | async-start | bytes 2359296 | tf_op jit(solution)/shard_map/all_to_all | solution.py:670
  80.4 23.9 %collective-permute-start = (bf16[4,112,1152]{2,1,0:T(8,128)(2,1)S(1)}, bf16[4,112,1152]{2,1,0:T(8,128)(2,1)S(1)}, u32[]{:S(2)}, u32[]{:S(2)}) collective-permute-start(bf16[4,112,1152]{2,1,0:T(8,128)(2,1)S(1)} %all-to-all-done), channel_id=1, source_target_pairs={{0,4},{4,0},{8,12},{12,8},{16,20},{20,16},{24,28},{28,24},{1,5},{5... | collective-permute-start | bytes 3096584 | tf_op jit(solution)/shard_map/ppermute | solution.py:665
  105.9 76.6 %collective-permute-start.4 = (bf16[2,4,112,1152]{3,2,1,0:T(8,128)(2,1)}, bf16[2,4,112,1152]{3,2,1,0:T(8,128)(2,1)}, u32[]{:S(2)}, u32[]{:S(2)}) collective-permute-start(bf16[2,4,112,1152]{3,2,1,0:T(8,128)(2,1)} %pad_maximum_fusion.2.rest_4_.rest_0_), channel_id=1, source_target_pairs={{0,1},{1,0},{2,3},{3,2},{4,5},{5,4},{6,7},{7,6},{8,9},{9,8},{10,11... | collective-permute-start | bytes 6193160 | tf_op jit(solution)/shard_map/ppermute | solution.py:662
  108.9 67.3 %collective-permute-start.1 = (bf16[256,768]{1,0:T(8,128)(2,1)}, bf16[256,768]{1,0:T(8,128)(2,1)S(1)}, u32[]{:S(2)}, u32[]{:S(2)}) collective-permute-start(bf16[256,768]{1,0:T(8,128)(2,1)} %get-tuple-element.64), channel_id=1, source_target_pairs={{0,1},{1,0},{2,3},{3,2},{4,5},{5,4},{6,7},{7,6},{8,9},{9,8},{10,11... | collective-permute-start | bytes 1179656 | tf_op jit(solution)/shard_map/ppermute | solution.py:662
  109.4 68.2 %collective-permute-start.2 = (bf16[256,768]{1,0:T(8,128)(2,1)}, bf16[256,768]{1,0:T(8,128)(2,1)}, u32[]{:S(2)}, u32[]{:S(2)}) collective-permute-start(bf16[256,768]{1,0:T(8,128)(2,1)} %get-tuple-element.65), channel_id=1, source_target_pairs={{0,2},{1,3},{2,0},{3,1},{4,6},{5,7},{6,4},{7,5},{8,10},{9,11},{10,... | collective-permute-start | bytes 1179656 | tf_op jit(solution)/shard_map/ppermute | solution.py:662
  110.9 61.2 %collective-permute-start.8 = (bf16[4,96,1920]{2,1,0:T(8,128)(2,1)S(1)}, bf16[4,96,1920]{2,1,0:T(8,128)(2,1)}, u32[]{:S(2)}, u32[]{:S(2)}) collective-permute-start(bf16[4,96,1920]{2,1,0:T(8,128)(2,1)S(1)} %all-to-all-done.1), channel_id=1, source_target_pairs={{0,4},{4,0},{8,12},{12,8},{16,20},{20,16},{24,28},{28,24},{1,5},{5... | collective-permute-start | bytes 4423688 | tf_op jit(solution)/shard_map/ppermute | solution.py:665
  112.4 57.8 %collective-permute-start.10 = (bf16[4,192,768]{2,1,0:T(8,128)(2,1)}, bf16[4,192,768]{2,1,0:T(8,128)(2,1)}, u32[]{:S(2)}, u32[]{:S(2)}) collective-permute-start(bf16[4,192,768]{2,1,0:T(8,128)(2,1)} %all-to-all-done.2), channel_id=1, source_target_pairs={{0,4},{4,0},{8,12},{12,8},{16,20},{20,16},{24,28},{28,24},{1,5},{5... | collective-permute-start | bytes 3538952 | tf_op jit(solution)/shard_map/ppermute | solution.py:665
  113.8 4.2 copy-start.11
  114.8 3.1 copy-start.4
  170.2 11.6 %collective-permute-start.3 = (bf16[256,768]{1,0:T(8,128)(2,1)}, bf16[256,768]{1,0:T(8,128)(2,1)S(1)}, u32[]{:S(2)}, u32[]{:S(2)}) collective-permute-start(bf16[256,768]{1,0:T(8,128)(2,1)} %get-tuple-element.66), channel_id=1, source_target_pairs={{0,3},{1,2},{2,1},{3,0},{4,7},{5,6},{6,5},{7,4},{8,11},{9,10},{10,... | collective-permute-start | bytes 1179656 | tf_op jit(solution)/shard_map/ppermute | solution.py:662
  172.1 9.8 %copy-start.6 = (bf16[2,4,192,768]{3,2,1,0:T(8,128)(2,1)}, bf16[2,4,192,768]{3,2,1,0:T(8,128)(2,1)S(1)}, u32[]{:S(2)}) copy-start(bf16[2,4,192,768]{3,2,1,0:T(8,128)(2,1)S(1)} %pad_maximum_fusion.1.rest_6_) | copy-start | bytes 7077892
  172.1 61.6 %collective-permute-start.5 = (bf16[256,768]{1,0:T(8,128)(2,1)}, bf16[256,768]{1,0:T(8,128)(2,1)}, u32[]{:S(2)}, u32[]{:S(2)}) collective-permute-start(bf16[256,768]{1,0:T(8,128)(2,1)} %get-tuple-element.74), channel_id=1, source_target_pairs={{0,1},{1,0},{2,3},{3,2},{4,5},{5,4},{6,7},{7,6},{8,9},{9,8},{10,11... | collective-permute-start | bytes 1179656 | tf_op jit(solution)/shard_map/ppermute | solution.py:662
  172.8 4.8 copy-start.14
  176.2 5.7 %copy-start.13 = (bf16[256,768]{1,0:T(8,128)(2,1)}, bf16[256,768]{1,0:T(8,128)(2,1)S(1)}, u32[]{:S(2)}) copy-start(bf16[256,768]{1,0:T(8,128)(2,1)S(1)} %collective-permute-done.1.rest_1_) | copy-start | bytes 1179652
  176.2 57.5 %collective-permute-start.6 = (bf16[256,768]{1,0:T(8,128)(2,1)}, bf16[256,768]{1,0:T(8,128)(2,1)}, u32[]{:S(2)}, u32[]{:S(2)}) collective-permute-start(bf16[256,768]{1,0:T(8,128)(2,1)} %get-tuple-element.75), channel_id=1, source_target_pairs={{0,2},{1,3},{2,0},{3,1},{4,6},{5,7},{6,4},{7,5},{8,10},{9,11},{10,... | collective-permute-start | bytes 1179656 | tf_op jit(solution)/shard_map/ppermute | solution.py:662
  177.6 56.0 %collective-permute-start.7 = (bf16[256,768]{1,0:T(8,128)(2,1)S(1)}, bf16[256,768]{1,0:T(8,128)(2,1)}, u32[]{:S(2)}, u32[]{:S(2)}) collective-permute-start(bf16[256,768]{1,0:T(8,128)(2,1)S(1)} %copy-done.14), channel_id=1, source_target_pairs={{0,3},{1,2},{2,1},{3,0},{4,7},{5,6},{6,5},{7,4},{8,11},{9,10},{10,... | collective-permute-start | bytes 1179656 | tf_op jit(solution)/shard_map/ppermute | solution.py:662
  181.8 51.8 %collective-permute-start.11 = (bf16[2,4,192,768]{3,2,1,0:T(8,128)(2,1)S(1)}, bf16[2,4,192,768]{3,2,1,0:T(8,128)(2,1)}, u32[]{:S(2)}, u32[]{:S(2)}) collective-permute-start(bf16[2,4,192,768]{3,2,1,0:T(8,128)(2,1)S(1)} %pad_maximum_fusion.1.rest_6_), channel_id=1, source_target_pairs={{0,1},{1,0},{2,3},{3,2},{4,5},{5,4},{6,7},{7,6},{8,9},{9,8},{10,11... | collective-permute-start | bytes 7077896 | tf_op jit(solution)/shard_map/ppermute | solution.py:662
  182.6 51.1 %collective-permute-start.9 = (bf16[2,4,96,1920]{3,2,1,0:T(8,128)(2,1)}, bf16[2,4,96,1920]{3,2,1,0:T(8,128)(2,1)S(1)}, u32[]{:S(2)}, u32[]{:S(2)}) collective-permute-start(bf16[2,4,96,1920]{3,2,1,0:T(8,128)(2,1)} %pad_maximum_fusion.rest_4_), channel_id=1, source_target_pairs={{0,1},{1,0},{2,3},{3,2},{4,5},{5,4},{6,7},{7,6},{8,9},{9,8},{10,11... | collective-permute-start | bytes 8847368 | tf_op jit(solution)/shard_map/ppermute | solution.py:662
  339.9 27.0 %collective-permute-start.18 = (bf16[8,112,1152]{2,1,0:T(8,128)(2,1)}, bf16[8,112,1152]{2,1,0:T(8,128)(2,1)}, u32[]{:S(2)}, u32[]{:S(2)}) collective-permute-start(bf16[8,112,1152]{2,1,0:T(8,128)(2,1)} %get-tuple-element.103), channel_id=1, source_target_pairs={{0,1},{1,0},{2,3},{3,2},{4,5},{5,4},{6,7},{7,6},{8,9},{9,8},{10,11... | collective-permute-start | bytes 6193160 | tf_op jit(solution)/shard_map/ppermute | solution.py:662
  352.8 49.1 %collective-permute-start.26 = (bf16[8,192,768]{2,1,0:T(8,128)(2,1)}, bf16[8,192,768]{2,1,0:T(8,128)(2,1)}, u32[]{:S(2)}, u32[]{:S(2)}) collective-permute-start(bf16[8,192,768]{2,1,0:T(8,128)(2,1)} %get-tuple-element.112), channel_id=1, source_target_pairs={{0,1},{1,0},{2,3},{3,2},{4,5},{5,4},{6,7},{7,6},{8,9},{9,8},{10,11... | collective-permute-start | bytes 7077896 | tf_op jit(solution)/shard_map/ppermute | solution.py:662
  352.8 14.0 %copy-start.8 = (bf16[8,112,1152]{2,1,0:T(8,128)(2,1)S(1)}, bf16[8,112,1152]{2,1,0:T(8,128)(2,1)}, u32[]{:S(2)}) copy-start(bf16[8,112,1152]{2,1,0:T(8,128)(2,1)} %get-tuple-element.102) | copy-start | bytes 6193156
  366.3 39.2 %collective-permute-start.22 = (bf16[8,96,1920]{2,1,0:T(8,128)(2,1)}, bf16[8,96,1920]{2,1,0:T(8,128)(2,1)}, u32[]{:S(2)}, u32[]{:S(2)}) collective-permute-start(bf16[8,96,1920]{2,1,0:T(8,128)(2,1)} %bitcast.91), channel_id=1, source_target_pairs={{0,1},{1,0},{2,3},{3,2},{4,5},{5,4},{6,7},{7,6},{8,9},{9,8},{10,11... | collective-permute-start | bytes 8847368 | tf_op jit(solution)/shard_map/ppermute | solution.py:662
  369.3 25.0 %collective-permute-start.19 = (bf16[4,112,1152]{2,1,0:T(8,128)(2,1)}, bf16[4,112,1152]{2,1,0:T(8,128)(2,1)}, u32[]{:S(2)}, u32[]{:S(2)}) collective-permute-start(bf16[4,112,1152]{2,1,0:T(8,128)(2,1)} %fusion.8), channel_id=1, source_target_pairs={{0,4},{4,0},{8,12},{12,8},{16,20},{20,16},{24,28},{28,24},{1,5},{5... | collective-permute-start | bytes 3096584 | tf_op jit(solution)/shard_map/ppermute | solution.py:665
  397.2 38.4 %all-to-all-start.3 = ((bf16[4,112,1152]{2,1,0:T(8,128)(2,1)}), bf16[4,112,1152]{2,1,0:T(8,128)(2,1)S(1)}, u32[]{:S(2)}, u32[]{:S(2)}) async-start(bf16[4,112,1152]{2,1,0:T(8,128)(2,1)} %fusion.2), calls=%async_computation.3 | async-start | bytes 2064384 | tf_op jit(solution)/shard_map/all_to_all | solution.py:670
  401.9 3.6 copy-start.5
  403.9 28.9 %collective-permute-start.27 = (bf16[4,192,768]{2,1,0:T(8,128)(2,1)S(1)}, bf16[4,192,768]{2,1,0:T(8,128)(2,1)S(1)}, u32[]{:S(2)}, u32[]{:S(2)}) collective-permute-start(bf16[4,192,768]{2,1,0:T(8,128)(2,1)S(1)} %fusion.6), channel_id=1, source_target_pairs={{0,4},{4,0},{8,12},{12,8},{16,20},{20,16},{24,28},{28,24},{1,5},{5... | collective-permute-start | bytes 3538952 | tf_op jit(solution)/shard_map/ppermute | solution.py:665
  405.5 27.3 %copy-start.7 = (bf16[8,192,768]{2,1,0:T(8,128)(2,1)S(1)}, bf16[8,192,768]{2,1,0:T(8,128)(2,1)}, u32[]{:S(2)}) copy-start(bf16[8,192,768]{2,1,0:T(8,128)(2,1)} %get-tuple-element.111) | copy-start | bytes 7077892
  408.5 53.9 %collective-permute-start.23 = (bf16[4,96,1920]{2,1,0:T(8,128)(2,1)}, bf16[4,96,1920]{2,1,0:T(8,128)(2,1)S(1)}, u32[]{:S(2)}, u32[]{:S(2)}) collective-permute-start(bf16[4,96,1920]{2,1,0:T(8,128)(2,1)} %fusion.4), channel_id=1, source_target_pairs={{0,4},{4,0},{8,12},{12,8},{16,20},{20,16},{24,28},{28,24},{1,5},{5... | collective-permute-start | bytes 4423688 | tf_op jit(solution)/shard_map/ppermute | solution.py:665
  436.6 29.2 %all-to-all-start.5 = ((bf16[4,192,768]{2,1,0:T(8,128)(2,1)}), bf16[4,192,768]{2,1,0:T(8,128)(2,1)S(1)}, u32[]{:S(2)}, u32[]{:S(2)}) async-start(bf16[4,192,768]{2,1,0:T(8,128)(2,1)} %fusion.1), calls=%async_computation.5 | async-start | bytes 2359296 | tf_op jit(solution)/shard_map/all_to_all | solution.py:670
  465.8 60.6 %all-to-all-start.4 = ((bf16[4,96,1920]{2,1,0:T(8,128)(2,1)}), bf16[4,96,1920]{2,1,0:T(8,128)(2,1)S(1)}, u32[]{:S(2)}, u32[]{:S(2)}) async-start(bf16[4,96,1920]{2,1,0:T(8,128)(2,1)} %fusion), calls=%async_computation.4 | async-start | bytes 2949120 | tf_op jit(solution)/shard_map/all_to_all | solution.py:670
  481.3 2.9 collective-permute-start.15
  481.3 12.4 %collective-permute-start.16 = (bf16[256,768]{1,0:T(8,128)(2,1)}, bf16[256,768]{1,0:T(8,128)(2,1)}, u32[]{:S(2)}, u32[]{:S(2)}) collective-permute-start(bf16[256,768]{1,0:T(8,128)(2,1)} %get-tuple-element.97), channel_id=1, source_target_pairs={{0,2},{1,3},{2,0},{3,1},{4,6},{5,7},{6,4},{7,5},{8,10},{9,11},{10,... | collective-permute-start | bytes 1179656 | tf_op jit(solution)/shard_map/ppermute | solution.py:662
  482.0 19.0 %collective-permute-start.17 = (bf16[256,768]{1,0:T(8,128)(2,1)}, bf16[256,768]{1,0:T(8,128)(2,1)}, u32[]{:S(2)}, u32[]{:S(2)}) collective-permute-start(bf16[256,768]{1,0:T(8,128)(2,1)} %get-tuple-element.98), channel_id=1, source_target_pairs={{0,3},{1,2},{2,1},{3,0},{4,7},{5,6},{6,5},{7,4},{8,11},{9,10},{10,... | collective-permute-start | bytes 1179656 | tf_op jit(solution)/shard_map/ppermute | solution.py:662
  483.2 21.6 %collective-permute-start.12 = (bf16[256,768]{1,0:T(8,128)(2,1)}, bf16[256,768]{1,0:T(8,128)(2,1)}, u32[]{:S(2)}, u32[]{:S(2)}) collective-permute-start(bf16[256,768]{1,0:T(8,128)(2,1)} %get-tuple-element.78), channel_id=1, source_target_pairs={{0,1},{1,0},{2,3},{3,2},{4,5},{5,4},{6,7},{7,6},{8,9},{9,8},{10,11... | collective-permute-start | bytes 1179656 | tf_op jit(solution)/shard_map/ppermute | solution.py:662
  483.6 27.0 %collective-permute-start.13 = (bf16[256,768]{1,0:T(8,128)(2,1)}, bf16[256,768]{1,0:T(8,128)(2,1)}, u32[]{:S(2)}, u32[]{:S(2)}) collective-permute-start(bf16[256,768]{1,0:T(8,128)(2,1)} %get-tuple-element.79), channel_id=1, source_target_pairs={{0,2},{1,3},{2,0},{3,1},{4,6},{5,7},{6,4},{7,5},{8,10},{9,11},{10,... | collective-permute-start | bytes 1179656 | tf_op jit(solution)/shard_map/ppermute | solution.py:662
  484.2 33.7 %collective-permute-start.14 = (bf16[256,768]{1,0:T(8,128)(2,1)}, bf16[256,768]{1,0:T(8,128)(2,1)}, u32[]{:S(2)}, u32[]{:S(2)}) collective-permute-start(bf16[256,768]{1,0:T(8,128)(2,1)} %get-tuple-element.80), channel_id=1, source_target_pairs={{0,3},{1,2},{2,1},{3,0},{4,7},{5,6},{6,5},{7,4},{8,11},{9,10},{10,... | collective-permute-start | bytes 1179656 | tf_op jit(solution)/shard_map/ppermute | solution.py:662
  493.7 30.2 %collective-permute-start.20 = (bf16[112,1152]{1,0:T(8,128)(2,1)S(1)}, bf16[112,1152]{1,0:T(8,128)(2,1)S(1)}, u32[]{:S(2)}, u32[]{:S(2)}) collective-permute-start(bf16[112,1152]{1,0:T(8,128)(2,1)S(1)} %reduce_sum.46), channel_id=1, source_target_pairs={{0,2},{1,3},{2,0},{3,1},{4,6},{5,7},{6,4},{7,5},{8,10},{9,11},{10,... | collective-permute-start | bytes 774152 | tf_op jit(solution)/shard_map/ppermute | solution.py:662
  524.6 6.3 %collective-permute-start.21 = (bf16[112,1152]{1,0:T(8,128)(2,1)}, bf16[112,1152]{1,0:T(8,128)(2,1)}, u32[]{:S(2)}, u32[]{:S(2)}) collective-permute-start(bf16[112,1152]{1,0:T(8,128)(2,1)} %add_convert_fusion.8), channel_id=1, source_target_pairs={{0,1},{1,0},{2,3},{3,2},{4,5},{5,4},{6,7},{7,6},{8,9},{9,8},{10,11... | collective-permute-start | bytes 774152 | tf_op jit(solution)/shard_map/ppermute | solution.py:662
  525.4 2.7 copy-start.9
  525.7 9.9 %collective-permute-start.28 = (bf16[192,768]{1,0:T(8,128)(2,1)S(1)}, bf16[192,768]{1,0:T(8,128)(2,1)S(1)}, u32[]{:S(2)}, u32[]{:S(2)}) collective-permute-start(bf16[192,768]{1,0:T(8,128)(2,1)S(1)} %reduce_sum.48), channel_id=1, source_target_pairs={{0,2},{1,3},{2,0},{3,1},{4,6},{5,7},{6,4},{7,5},{8,10},{9,11},{10,... | collective-permute-start | bytes 884744 | tf_op jit(solution)/shard_map/ppermute | solution.py:662
  526.6 16.5 %collective-permute-start.24 = (bf16[96,1920]{1,0:T(8,128)(2,1)S(1)}, bf16[96,1920]{1,0:T(8,128)(2,1)S(1)}, u32[]{:S(2)}, u32[]{:S(2)}) collective-permute-start(bf16[96,1920]{1,0:T(8,128)(2,1)S(1)} %reduce_sum.47), channel_id=1, source_target_pairs={{0,2},{1,3},{2,0},{3,1},{4,6},{5,7},{6,4},{7,5},{8,10},{9,11},{10,... | collective-permute-start | bytes 1105928 | tf_op jit(solution)/shard_map/ppermute | solution.py:662
  535.7 8.6 %collective-permute-start.29 = (bf16[192,768]{1,0:T(8,128)(2,1)S(1)}, bf16[192,768]{1,0:T(8,128)(2,1)S(1)}, u32[]{:S(2)}, u32[]{:S(2)}) collective-permute-start(bf16[192,768]{1,0:T(8,128)(2,1)S(1)} %add_convert_fusion.7), channel_id=1, source_target_pairs={{0,1},{1,0},{2,3},{3,2},{4,5},{5,4},{6,7},{7,6},{8,9},{9,8},{10,11... | collective-permute-start | bytes 884744 | tf_op jit(solution)/shard_map/ppermute | solution.py:662
  543.2 2.3 collective-permute-start.25
  545.4 2.0 copy-start.1
  (5 other events, 5.8 us)

commit v2 on v1

--- a/solution.py
+++ b/solution.py
@@ -19,6 +19,7 @@
 F32 = jnp.float32
 ROWS = 256
 MIB = 1 << 20
+SMALL = 16
 
 
 ERFC = (
@@ -68,26 +69,26 @@
     return rstd * (a - jnp.mean(a, -1, keepdims=True) - xhat * jnp.mean(a * xhat, -1, keepdims=True))
 
 
-def piece_copies(pieces, by_rows, cols, dst, sems, core, x_bit):
+def piece_copies(pieces, by_rows, rows, cols, dst, sems, bits):
+    core, x_bit, z_at = bits
+    lo, nc = cols
+    zs = len(pieces) // 4 if len(pieces[0].shape) == 2 else pieces[0].shape[0]
     copies = []
-    lo, nc = cols
-    for rc, ref in enumerate(pieces):
-        _, count, nr, _ = ref.shape
-        nr -= nr % (D // 8 // 2) if not by_rows else 0
-        row0 = nr * lax.bitwise_xor(core, rc) if by_rows else 0
-        col0 = 0 if by_rows else nc * lax.bitwise_xor(core, rc)
-        stride = nr * (2 if by_rows else 1)
+    for rc in range(2):
+        row0 = rows * lax.bitwise_xor(core, rc) if by_rows else 0
+        col0 = 0 if by_rows else pl.multiple_of(nc * lax.bitwise_xor(core, rc), nc)
         for rx in range(2):
-            for z in range(count):
-                row = row0 + stride * (2 * z + lax.bitwise_xor(x_bit, rx))
+            for z in range(zs):
+                if len(pieces[0].shape) == 2:
+                    src, at = pieces[(rc * 2 + rx) * zs + z], lax.bitwise_xor(z_at, z)
+                else:
+                    src, at = pieces[rc * 2 + rx].at[z], z
+                row = row0 + rows * (2 if by_rows else 1) * (2 * at + lax.bitwise_xor(x_bit, rx))
                 copies.append(
                     pltpu.make_async_copy(
-                        ref.at[rx, z, pl.ds(0, nr), pl.ds(lo, nc)],
-                        dst.at[
-                            pl.ds(pl.multiple_of(row, nr), nr),
-                            pl.ds(0 if by_rows else pl.multiple_of(col0, nc), nc),
-                        ],
-                        sems.at[(rc * 2 + rx) * count + z],
+                        src.at[pl.ds(0, rows), pl.ds(lo, nc)],
+                        dst.at[pl.ds(pl.multiple_of(row, rows), rows), pl.ds(col0, nc)],
+                        sems.at[(rc * 2 + rx) * zs + z],
                     )
                 )
     return copies
@@ -98,15 +99,18 @@
     return [pltpu.make_async_copy(ref.at[:, pl.ds(lo, nc)], dst, sems.at[0])]
 
 
-def weight_copies(kind, refs, cols, full_cols, dst, sems, bits):
+def weight_copies(weight, refs, rows, cols, full_cols, dst, sems, bits):
+    kind = weight[0]
     if kind == "whole":
         return whole_copies(refs[0], full_cols, dst, sems)
-    return piece_copies(refs, kind == "rows", full_cols if kind == "rows" else cols, dst, sems, *bits)
+    return piece_copies(refs, kind == "rows", rows, full_cols if kind == "rows" else cols, dst, sems, bits)
 
 
 def copy_count(weight):
     kind, refs = weight
-    return 1 if kind == "whole" else 4 * refs[0].shape[1]
+    if kind == "whole":
+        return 1
+    return len(refs) if len(refs[0].shape) == 2 else 4 * refs[0].shape[0]
 
 
 def put_block(refs, step, value):
@@ -140,20 +144,18 @@
 
 
 def bits_of(me_ref):
-    return lax.bitwise_and(me_ref[0], 1), me_ref[1]
-
-
-def pack(me, w, vectors, copies):
+    return lax.bitwise_and(me_ref[0], 1), me_ref[1], me_ref[2]
+
+
+def pack(me, w, vectors):
     rows, width = w.shape[0], w.shape[1] // 2
 
     def kernel(me_ref, w_ref, *rest):
         v_refs, o_ref = rest[:-1], rest[-1]
-        for z in range(copies):
-            o_ref[z, :rows, :] = w_ref[...]
-            o_ref[z, rows:, :] = jnp.zeros((16, width), BF)
+        o_ref[:rows, :] = w_ref[...]
+        o_ref[rows:, :] = jnp.zeros((SMALL, width), BF)
         for i, v in enumerate(v_refs):
-            for z in range(copies):
-                o_ref[z, rows + i : rows + i + 1, : v.shape[0]] = v[...].reshape(1, -1)
+            o_ref[rows + i : rows + i + 1, : v.shape[0]] = v[...].reshape(1, -1)
 
     one = lambda v: pl.BlockSpec(v.shape, lambda i, me: (0,))
     return pl.pallas_call(
@@ -163,9 +165,9 @@
             grid=(1,),
             in_specs=[pl.BlockSpec((rows, width), lambda i, me: (0, lax.bitwise_and(me[0], 1)))]
             + [one(v) for v in vectors],
-            out_specs=pl.BlockSpec((copies, rows + 16, width), lambda i, me: (0, 0, 0)),
+            out_specs=pl.BlockSpec((rows + SMALL, width), lambda i, me: (0, 0)),
         ),
-        out_shape=jax.ShapeDtypeStruct((copies, rows + 16, width), BF),
+        out_shape=jax.ShapeDtypeStruct((rows + SMALL, width), BF),
         compiler_params=params(),
         cost_estimate=cost(2),
         name="pack",
@@ -232,46 +234,65 @@
             into[...] = ref[...]
 
 
-def project(me, x_own, x_near, weight, bias_row):
-    kind, refs = weight
+def project(me, x_own, x_near, weight, table, fsdp):
+    _, refs = weight
     n = 3 * D
     count = copy_count(weight)
-
+    per, per_up = D // fsdp, FF // fsdp
     x_args, x_specs = own_and_near(x_own, x_near)
     blocks = len(x_args)
-
-    def kernel(me_ref, b_ref, *rest):
-        x_refs, w_refs, (o_ref, x_ref, w_ref, sems) = rest[:blocks], rest[blocks:-4], rest[-4:]
+    given = [] if table is None else list(table)
+
+    def kernel(me_ref, *rest):
+        x_refs, t_refs, w_refs = rest[:blocks], rest[blocks : blocks + len(given)], rest[blocks + len(given) : -8]
+        o_ref, x_ref, tab_ref, up_ref, w_ref, sm_ref, sems, ssems = rest[-8:]
         get_block(x_refs, pl.program_id(0), x_ref)
 
         @pl.when(pl.program_id(0) == 0)
         def _():
-            copies = weight_copies(kind, w_refs, (0, n // 2), (0, n), w_ref, sems, bits_of(me_ref))
+            bits = bits_of(me_ref)
+            copies = weight_copies(weight, w_refs, per, (0, n // 2), (0, n), w_ref, sems, bits)
             start_all(copies)
+            if given:
+                tab_ref[...] = t_refs[0][...]
+                up_ref[...] = t_refs[1][...]
+            else:
+                zs = fsdp // 2
+                vector_rows = [pltpu.make_async_copy(
+                    w_refs[rx * zs + z].at[pl.ds(per, SMALL), pl.ds(0, per_up)],
+                    sm_ref.at[2 * lax.bitwise_xor(bits[2], z) + lax.bitwise_xor(bits[1], rx)],
+                    ssems.at[rx * zs + z]) for rx in range(2) for z in range(zs)]
+                start_all(vector_rows)
+                wait_all(vector_rows)
+                for d in range(fsdp):
+                    tab_ref[:, d * per : (d + 1) * per] = sm_ref[d, 0:8, :per].astype(F32)
+                    up_ref[:, d * per_up : (d + 1) * per_up] = sm_ref[d, 8:16, :].astype(F32)
             wait_all(copies)
 
         xv = x_ref[...]
-        for lo in range(0, n, D):
-            o_ref[:, lo : lo + D] = (
-                nn(xv, w_ref[:, lo : lo + D]) + b_ref[:, lo : lo + D]
-            ).astype(BF)
+        o_ref[:, :D] = (nn(xv, w_ref[:, :D]) + tab_ref[6:7, :]).astype(BF)
+        o_ref[:, D : 2 * D] = nn(xv, w_ref[:, D : 2 * D]).astype(BF)
+        o_ref[:, 2 * D :] = (nn(xv, w_ref[:, 2 * D :]) + tab_ref[7:8, :]).astype(BF)
 
     rows = ROWS * blocks
+    full = lambda s: pl.BlockSpec(s, lambda i, me: (0, 0))
+    sd = jax.ShapeDtypeStruct
     return pl.pallas_call(
         kernel,
         grid_spec=pltpu.PrefetchScalarGridSpec(
             num_scalar_prefetch=1,
             grid=(blocks,),
-            in_specs=[pl.BlockSpec((1, n), lambda i, me: (0, 0))] + x_specs + [ANY] * len(refs),
+            in_specs=x_specs + [full((8, D)), full((8, FF))][: len(given)] + [ANY] * len(refs),
             out_specs=[pl.BlockSpec((ROWS, n), lambda i, me: (i, 0)),
-                       pl.BlockSpec((ROWS, D), lambda i, me: (i, 0))],
-            scratch_shapes=[pltpu.VMEM((D, n), BF), pltpu.SemaphoreType.DMA((count,))],
+                       pl.BlockSpec((ROWS, D), lambda i, me: (i, 0)), full((8, D)), full((8, FF))],
+            scratch_shapes=[pltpu.VMEM((D, n), BF), pltpu.VMEM((fsdp, SMALL, per_up), BF),
+                            pltpu.SemaphoreType.DMA((count,)), pltpu.SemaphoreType.DMA((fsdp,))],
         ),
-        out_shape=[jax.ShapeDtypeStruct((rows, n), BF), jax.ShapeDtypeStruct((rows, D), BF)],
+        out_shape=[sd((rows, n), BF), sd((rows, D), BF), sd((8, D), F32), sd((8, FF), F32)],
         compiler_params=params(),
         cost_estimate=cost(9),
         name="project",
-    )(me, bias_row, *x_args, *refs)
+    )(me, *x_args, *given, *refs)
 
 
 def attend(qkv, seg_col, seg_row, first, count, before):
@@ -283,6 +304,7 @@
         k = k_ref[...]
         vt = v_ref[...].T
         seg_k = sc_ref[...]
+
         for c in range(SEQ // chunk):
             at = pl.ds(c * chunk, chunk)
             q = q_ref[at, :] * jnp.asarray(SCALE, BF)
@@ -336,7 +358,8 @@
         seg_q = sr_ref[...]
         kt_ref[...] = k_ref[...].T
         acc_ref[...] = jnp.zeros_like(acc_ref)
-        dv_total = jnp.zeros((1, 2 * HD), F32)
+        sum_ref[1:2, :] = jnp.zeros((1, 2 * HD), F32)
+
         for c in range(SEQ // chunk):
             at = pl.ds(c * chunk, chunk)
             k = k_ref[at, :]
@@ -354,11 +377,11 @@
             dk_ref[at, :] = jnp.where(first, dks[0], dks[1]).astype(BF)
             dv = jnp.where(first, dvs[0], dvs[1]).astype(BF)
             dv_ref[at, :] = dv
-            dv_total += jnp.sum(dv.astype(F32), 0, keepdims=True)
+            sum_ref[1:2, :] += jnp.sum(dv.astype(F32), 0, keepdims=True)
+
         dq = (acc_ref[...].T * SCALE).astype(BF)
         dq_ref[...] = dq
         sum_ref[0:1, :] = jnp.sum(dq.astype(F32), 0, keepdims=True)
-        sum_ref[1:2, :] = dv_total
 
     spec = lambda off: pl.BlockSpec((SEQ, 2 * HD), lambda i: (0, i + off + start))
     full = lambda s: pl.BlockSpec(s, lambda i: (0,) * len(s))
@@ -378,9 +401,9 @@
     )(qkv, qkv, qkv, context, grad_context, lse, seg_col, seg_row, *before)
 
 
-def middle(me, context, x, g_own, g_near, vectors, up_bias, weight2, weight3):
-    kind2, refs2 = weight2
-    kind3, refs3 = weight3
+def middle(me, context, x, g_own, g_near, vectors, up_bias, weight2, weight3, fsdp):
+    _, refs2 = weight2
+    _, refs3 = weight3
     count = copy_count(weight2)
     blocks = x.shape[0] // ROWS
 
@@ -395,9 +418,9 @@
         step = pl.program_id(0)
         get_block(g_refs, step, g_ref)
         bits = bits_of(me_ref)
-        co = weight_copies(kind2, w2, (0, D // 2), (0, D), wo, s_o, bits)
-        cu = weight_copies(kind2, w2, (D // 2, FF // 2), (D, FF), wu, s_u, bits)
-        cd = weight_copies(kind3, w3, None, (0, D), wd, s_d, bits)
+        co = weight_copies(weight2, w2, D // fsdp, (0, D // 2), (0, D), wo, s_o, bits)
+        cu = weight_copies(weight2, w2, D // fsdp, (D // 2, FF // 2), (D, FF), wu, s_u, bits)
+        cd = weight_copies(weight3, w3, FF // fsdp // 2, None, (0, D), wd, s_d, bits)
 
         @pl.when(step == 0)
         def _():
@@ -424,7 +447,7 @@
         ffn = jnp.zeros((ROWS, D), F32)
         for lo in range(0, FF, D):
             at = slice(lo, lo + D)
-            pre = nn(low1, wu[:, at]) + ub_ref[:, at]
+            pre = nn(low1, wu[:, at]) + ub_ref[0:1, at]
             act, sl = gelu_with_slope(pre)
             act = act.astype(BF)
             act_ref[:, at] = act
@@ -466,7 +489,7 @@
         grid_spec=pltpu.PrefetchScalarGridSpec(
             num_scalar_prefetch=1,
             grid=(rows // ROWS,),
-            in_specs=[blk(D), blk(D), full((8, D)), full((1, FF))] + g_specs
+            in_specs=[blk(D), blk(D), full((8, D)), full((8, FF))] + g_specs
             + [ANY] * (len(refs2) + len(refs3)),
             out_specs=[full((ROWS, D))] * blocks + [blk(FF), blk(FF), blk(D), blk(D), blk(D), blk(D), blk(D),
                        full((8, D)), full((8, FF))],
@@ -493,7 +516,7 @@
     inner = width // per
 
     def kernel(me_ref, a_ref, g_ref, send_ref, keep_ref, acc_ref):
-        core, _ = bits_of(me_ref)
+        core, _, _ = bits_of(me_ref)
         acc_ref[...] = tn(a_ref[...], g_ref[...])
         n = per // 2
         for i in range(inner):
@@ -521,10 +544,16 @@
     )(me, act, grad_ffn)
 
 
-def halves_out(rows, width):
-    specs = [pl.BlockSpec((rows, width), lambda i, me: (0, 0))] * 2
-    shapes = [jax.ShapeDtypeStruct((rows, width), BF)] * 2
-    return specs, shapes
+def write_half(step, slots, send_ref, keep_ref, sems):
+    sending = pltpu.make_async_copy(slots.at[0], send_ref, sems.at[0])
+    keeping = pltpu.make_async_copy(slots.at[1], keep_ref, sems.at[1])
+    pl.when(step == 0)(sending.start)
+
+    @pl.when(step == 1)
+    def _():
+        keeping.start()
+        sending.wait()
+        keeping.wait()
 
 
 def half_of(i, core):
@@ -534,27 +563,25 @@
 def grad_up_out(me, low1, grad_pre, context, grad_attn):
     wu, wo = FF // 2, D // 2
 
-    def kernel(me_ref, l_ref, p_ref, c_ref, a_ref, send_ref, keep_ref):
-        def fill(o_ref):
-            o_ref[:, :wo] = tn(c_ref[...], a_ref[...]).astype(BF)
-            low = l_ref[...]
-            for lo in range(0, wu, D):
-                o_ref[:, wo + lo : wo + lo + D] = tn(low, p_ref[:, lo : lo + D]).astype(BF)
-
-        pl.when(pl.program_id(0) == 0)(lambda: fill(send_ref))
-        pl.when(pl.program_id(0) == 1)(lambda: fill(keep_ref))
+    def kernel(me_ref, l_ref, p_ref, c_ref, a_ref, send_ref, keep_ref, slots, sems):
+        step = pl.program_id(0)
+        slots[step, :, :wo] = tn(c_ref[...], a_ref[...]).astype(BF)
+        low = l_ref[...]
+        for lo in range(0, wu, D):
+            slots[step, :, wo + lo : wo + lo + D] = tn(low, p_ref[:, lo : lo + D]).astype(BF)
+        write_half(step, slots, send_ref, keep_ref, sems)
 
     rows = low1.shape[0]
     half = lambda n: pl.BlockSpec(
         (rows, n), lambda i, me: (0, half_of(i, lax.bitwise_and(me[0], 1))))
     full = pl.BlockSpec((rows, D), lambda i, me: (0, 0))
-    specs, shapes = halves_out(D, wu + wo)
     return pl.pallas_call(
         kernel,
         grid_spec=pltpu.PrefetchScalarGridSpec(
             num_scalar_prefetch=1, grid=(2,),
-            in_specs=[full, half(wu), full, half(wo)], out_specs=specs),
-        out_shape=shapes,
+            in_specs=[full, half(wu), full, half(wo)], out_specs=[ANY] * 2,
+            scratch_shapes=[pltpu.VMEM((2, D, wu + wo), BF), pltpu.SemaphoreType.DMA((2,))]),
+        out_shape=[jax.ShapeDtypeStruct((D, wu + wo), BF)] * 2,
         compiler_params=params(),
         cost_estimate=cost(12),
         name="grad_up_out",
@@ -564,35 +591,34 @@
 def grad_qkv(me, x, dq, dk, dv, sums, up_sums, bias_sums, fsdp):
     w = 3 * D // 2
     per, per_up = D // fsdp, FF // fsdp
-    tall = per + 16
-
-    def kernel(me_ref, x_ref, q_ref, k_ref, v_ref, s_ref, u_ref, b_ref, send_ref, keep_ref):
-        core, _ = bits_of(me_ref)
-
-        def put(o_ref, lo, val):
+    tall = per + SMALL
+
+    def kernel(me_ref, x_ref, q_ref, k_ref, v_ref, s_ref, u_ref, b_ref, send_ref, keep_ref, slots, sems):
+        core, _, _ = bits_of(me_ref)
+        step = pl.program_id(0)
+        b = half_of(step, core)
+
+        def put(lo, val):
             val = val.astype(BF)
             for d in range(fsdp):
-                o_ref[d, :per, lo : lo + val.shape[1]] = val[d * per : (d + 1) * per]
-
-        def fill(o_ref, b):
-            @pl.when(b == 0)
-            def _():
-                put(o_ref, 0, tn(x_ref[...], q_ref[...]))
-                put(o_ref, D, tn(x_ref[...], k_ref[:, : D // 2]))
-
-            @pl.when(b == 1)
-            def _():
-                put(o_ref, 0, tn(x_ref[...], k_ref[:, D // 2 :]))
-                put(o_ref, D // 2, tn(x_ref[...], v_ref[...]))
-
-            rows = jnp.concatenate([s_ref[0:6], b_ref[0:2]], 0)
-            for d in range(fsdp):
-                o_ref[d, per:, :] = jnp.zeros((16, w), BF)
-                o_ref[d, per : per + 8, :per] = rows[:, d * per : (d + 1) * per].astype(BF)
-                o_ref[d, per + 8 : per + 9, :per_up] = u_ref[0:1, d * per_up : (d + 1) * per_up].astype(BF)
-
-        pl.when(pl.program_id(0) == 0)(lambda: fill(send_ref, 1 - core))
-        pl.when(pl.program_id(0) == 1)(lambda: fill(keep_ref, core))
+                slots[step, d, :per, lo : lo + val.shape[1]] = val[d * per : (d + 1) * per]
+
+        @pl.when(b == 0)
+        def _():
+            put(0, tn(x_ref[...], q_ref[...]))
+            put(D, tn(x_ref[...], k_ref[:, : D // 2]))
+
+        @pl.when(b == 1)
+        def _():
+            put(0, tn(x_ref[...], k_ref[:, D // 2 :]))
+            put(D // 2, tn(x_ref[...], v_ref[...]))
+
+        rows = jnp.concatenate([s_ref[0:6], b_ref[0:2]], 0)
+        for d in range(fsdp):
+            slots[step, d, per:, :] = jnp.zeros((SMALL, w), BF)
+            slots[step, d, per : per + 8, :per] = rows[:, d * per : (d + 1) * per].astype(BF)
+            slots[step, d, per + 8 : per + 9, :per_up] = u_ref[0:1, d * per_up : (d + 1) * per_up].astype(BF)
+        write_half(step, slots, send_ref, keep_ref, sems)
 
     rows = x.shape[0]
     full = lambda s: pl.BlockSpec(s, lambda i, me: (0, 0))
@@ -601,7 +627,8 @@
         grid_spec=pltpu.PrefetchScalarGridSpec(
             num_scalar_prefetch=1, grid=(2,),
             in_specs=[full((rows, D))] * 4 + [full((8, D)), full((8, FF)), full((8, D))],
-            out_specs=[pl.BlockSpec((fsdp, tall, w), lambda i, me: (0, 0, 0))] * 2),
+            out_specs=[ANY] * 2,
+            scratch_shapes=[pltpu.VMEM((2, fsdp, tall, w), BF), pltpu.SemaphoreType.DMA((2,))]),
         out_shape=[jax.ShapeDtypeStruct((fsdp, tall, w), BF)] * 2,
         compiler_params=params(),
         cost_estimate=cost(9),
@@ -609,8 +636,8 @@
     )(me, x, dq, dk, dv, sums, up_sums, bias_sums)
 
 
-def grad_in(me, dq, dk, dv, res1, weight):
-    kind, refs = weight
+def grad_in(me, dq, dk, dv, res1, weight, fsdp):
+    _, refs = weight
     n = 3 * D
     count = copy_count(weight)
 
@@ -619,7 +646,7 @@
 
         @pl.when(pl.program_id(0) == 0)
         def _():
-            copies = weight_copies(kind, w_refs, (0, n // 2), (0, n), w_ref, sems, bits_of(me_ref))
+            copies = weight_copies(weight, w_refs, D // fsdp, (0, n // 2), (0, n), w_ref, sems, bits_of(me_ref))
             start_all(copies)
             wait_all(copies)
 
@@ -654,15 +681,19 @@
     core = me & 1
     row = lax.axis_index("fsdp").astype(jnp.int32)
     xb, zs = row & 1, fsdp // 2
-    me1 = jnp.stack([me, xb])
+    me1 = jnp.stack([me, xb, row >> 1])
+    high = me >> 1
     rows_d, rows_f = D // fsdp, FF // fsdp
     split = in_pieces(fsdp)
 
     def partner(v, bit):
         return lax.ppermute(v, "sp", [(i, i ^ bit) for i in range(sp)])
 
+    def away(v, bits):
+        return lax.ppermute(v, "fsdp", [(i, i ^ bits) for i in range(fsdp)])
+
     def across(v):
-        return lax.ppermute(v, "fsdp", [(i, i ^ 1) for i in range(fsdp)])
+        return away(v, 1)
 
     lines = [[2 * z + b for z in range(zs)] for b in range(2)]
 
@@ -686,34 +717,34 @@
         return lax.dynamic_slice(w, (0, core * (w.shape[1] // 2)), (w.shape[0], w.shape[1] // 2))
 
     def spread(v):
-        a = along(v)
-        a = jnp.stack([a, across(a)])
-        return a, partner(a, 1)
+        a = along(each(v))
+        b = across(a)
+        return a, b, partner(a, 1), partner(b, 1)
+
+    def spread_apart(v):
+        line = [v] + [away(v, 2 * z) for z in range(1, zs)]
+        line += [across(a) for a in line]
+        return line + [partner(a, 1) for a in line]
 
     small = [out_bias, norm1_gain, norm1_bias, down_bias, norm2_gain, norm2_bias, query_bias,
              value_bias, up_bias]
     x_near = fetch(hidden_in)
     if split:
-        a1 = spread(pack(me1, w_qkv, small, zs))
-        every = a1[0][:, :, rows_d:, :rows_f]
-        every = jnp.where(xb == 0, every, every[::-1]).transpose(2, 1, 0, 3)
-        every = every.astype(F32).reshape(16, fsdp, rows_f)
-        table = every[:8, :, :rows_d].reshape(8, D)
-        full_up_bias = every[8].reshape(1, FF)
-        weight1 = ("cols", a1)
-        weight2 = ("cols", spread(each(jnp.concatenate([half_cols(w_out), half_cols(w_up)], 1))))
+        weight1 = ("cols", spread_apart(pack(me1, w_qkv, small)))
+        table = None
+        weight2 = ("cols", spread(jnp.concatenate([half_cols(w_out), half_cols(w_up)], 1)))
         down = lax.dynamic_slice(w_down, (core * (rows_f // 2), 0), (rows_f // 2, D))
-        weight3 = ("rows", spread(each(down)))
+        weight3 = ("rows", spread(down))
     else:
         every = lax.all_gather(jnp.concatenate(small), "fsdp", axis=0).astype(F32)
         table = every[:, : 8 * rows_d].reshape(fsdp, 8, rows_d).transpose(1, 0, 2).reshape(8, D)
-        full_up_bias = every[:, 8 * rows_d :].reshape(1, FF)
+        full_up_bias = jnp.broadcast_to(every[:, 8 * rows_d :].reshape(1, FF), (8, FF))
+        table = (table, full_up_bias)
         gather = lambda w: lax.all_gather(w, "fsdp", axis=0, tiled=True)
         weight1 = ("whole", (gather(w_qkv),))
         weight2 = ("whole", (gather(jnp.concatenate([w_out, w_up], 1)),))
         weight3 = ("whole", (gather(w_down),))
     g_near = fetch(cotangent)
-    bias_row = jnp.concatenate([table[6:7], jnp.zeros((1, D), F32), table[7:8]], 1)
 
     starts = lax.dynamic_slice(doc_starts, (me, 0), (1, doc_starts.shape[1]))
     order = jnp.arange(SEQ, dtype=jnp.int32)
@@ -721,30 +752,42 @@
     seg = jnp.sum((position[:, None] >= starts).astype(jnp.int32), -1)
     seg_col, seg_row = seg[:, None], seg[None, :]
 
-    qkv, x = project(me1, hidden_in, x_near, weight1, bias_row)
+    qkv, x, table, full_up_bias = project(me1, hidden_in, x_near, weight1, table, fsdp)
     context = ()
     per = PAIRS // PARTS
     for i in range(PARTS):
         context = attend(qkv, seg_col, seg_row, i * per, per, context)
     context, lse = context
     (*out, act, gpre, low1, gffn, gattn, res1, gctx, sums, up_sums) = middle(
-        me1, context, x, cotangent, g_near, table, full_up_bias, weight2, weight3)
+        me1, context, x, cotangent, g_near, table, full_up_bias, weight2, weight3, fsdp)
     layer_out = deliver(out)
 
     def add(a, b):
         return (a.astype(F32) + b.astype(F32)).astype(BF)
 
-    def join(mine, other, axis):
-        return jnp.where(core == 0, jnp.concatenate([mine, other], axis),
+    def join(mine, other, axis, bit=core):
+        return jnp.where(bit == 0, jnp.concatenate([mine, other], axis),
                          jnp.concatenate([other, mine], axis))
 
+    def pick(v, bit):
+        return lax.dynamic_index_in_dim(v, bit, 1, False)
+
+    def over_rows(v):
+        v = v.reshape((zs, 2) + v.shape[1:])
+        v = add(pick(v, xb), across(pick(v, 1 - xb)))
+        return jnp.sum(along(v).astype(F32), 0).astype(BF)
+
     def reduce_part(send, keep):
-        other = partner(send, 1)
-        cut = lambda v, b: lax.dynamic_index_in_dim(v.reshape((zs, 2) + v.shape[1:]), b, 1, False)
-        theirs = add(cut(keep, 1 - xb), cut(other, 1 - xb))
-        mine = add(add(cut(keep, xb), cut(other, xb)), across(theirs))
-        total = jnp.sum(along(mine).astype(F32), 0).astype(BF)
+        total = over_rows(add(keep, partner(send, 1)))
         total = add(total, partner(total, 2))
+        return total, partner(total, 1)
+
+    def reduce_by_high(send, keep):
+        v = add(keep, partner(send, 1))
+        v = v.reshape(fsdp, 2, v.shape[1] // 2, v.shape[2])
+        v = add(pick(v, high), partner(pick(v, 1 - high), 2))
+        total = over_rows(v)
+        total = join(total, partner(total, 2), 0, high)
         return total, partner(total, 1)
 
     def scatter(v):
@@ -755,7 +798,7 @@
     wide_parts = grad_up_out(me1, low1, gpre, context, gattn)
     if split:
         down = reduce_part(*down_parts)
-        wide = reduce_part(*[v.reshape(fsdp, rows_d, -1) for v in wide_parts])
+        wide = reduce_by_high(*[v.reshape(fsdp, rows_d, -1) for v in wide_parts])
     grads = ()
     for i in range(PARTS):
         grads = attend_back(qkv, context, gctx, lse, seg_col, seg_row, i * per, per, grads)
@@ -763,7 +806,7 @@
     qkv_parts = grad_qkv(me1, x, dq, dk, dv, sums, up_sums, bias_sums, fsdp)
     if split:
         qkv_sum = reduce_part(*qkv_parts)
-    dx = grad_in(me1, dq, dk, dv, res1, weight1)
+    dx = grad_in(me1, dq, dk, dv, res1, weight1, fsdp)
     grad_input = deliver(dx)
 
     if split:

time: 556 us -> 490 us (0.88)
  waiting for transfers between devices: 243 us -> 178 us
  other arithmetic: 32.4 us -> 24.7 us
  starting transfers between devices: 48.6 us -> 56.2 us
    ppermute x6 -> x12, waiting for transfers between devices: 140 us -> 116 us  [away(): return lax.ppermute(v, 'fsdp', [(i, i ^ bits) for i in range(fsdp)])]
    ppermute x24 -> x34, waiting for transfers between devices: 44.1 us -> 20.6 us  [partner(): return lax.ppermute(v, 'sp', [(i, i ^ bit) for i in range(sp)])]
    all_to_all x6 -> x5, waiting for transfers between devices: 58.7 us -> 41.4 us  [along(): return lax.all_to_all(v, 'fsdp', 0, 0, axis_index_groups=lines, tiled=True)]
    ppermute x6 -> x12, starting transfers between devices: 7.26 us -> 16.2 us  [away(): return lax.ppermute(v, 'fsdp', [(i, i ^ bits) for i in range(fsdp)])]
    another operation x5 -> x1, other arithmetic: 7.49 us -> 0.59 us  [local(): me1 = jnp.stack([me, xb, row >> 1])]
    all_to_all x6 -> x5, starting transfers between devices: 28.9 us -> 24.1 us  [along(): return lax.all_to_all(v, 'fsdp', 0, 0, axis_index_groups=lines, tiled=True)]
    ppermute x24 -> x34, starting transfers between devices: 12.4 us -> 15.8 us  [partner(): return lax.ppermute(v, 'sp', [(i, i ^ bit) for i in range(sp)])]
  transfers between devices with their start and end apart: 36 -> 51, of which waited for: 15 -> 17; matrix products, arithmetic and copies ran while one was open for 7% -> 6% of each run, Pallas kernels for 18% -> 30%
where the time goes in v2:
time: 490 us; the launch traced here: 482 us
  Pallas kernels  207 us (42%)
  waiting for transfers between devices  178 us (36%)
  starting transfers between devices  56.2 us (11%)
  other arithmetic  24.7 us (5%)
  local copies, waits for them, and re-layouts  14.8 us (3%)
    ppermute x12, waiting for transfers between devices, away(): return lax.ppermute(v, 'fsdp', [(i, i ^ bits) for i in range(fsdp)])  116 us
    pallas_call x1, Pallas kernels, middle(): pl.pallas_call(kernel, grid_spec=pltpu.PrefetchScalarGridSpec(num_scalar_...  49.6 us
    pallas_call x3, Pallas kernels, attend_back(): pl.pallas_call(kernel, grid=(count,), in_specs=[spec(0), spec(PAIRS), spe...  44.4 us
    all_to_all x5, waiting for transfers between devices, along(): return lax.all_to_all(v, 'fsdp', 0, 0, axis_index_groups=lines, tiled=True)  41.4 us
    pallas_call x3, Pallas kernels, attend(): pl.pallas_call(kernel, grid=(count,), in_specs=[spec(0), spec(PAIRS), spe...  41.1 us
    all_to_all x5, starting transfers between devices, along(): return lax.all_to_all(v, 'fsdp', 0, 0, axis_index_groups=lines, tiled=True)  24.1 us
    ppermute x34, waiting for transfers between devices, partner(): return lax.ppermute(v, 'sp', [(i, i ^ bit) for i in range(sp)])  20.6 us
    convert_element_type x9, other arithmetic, add(): return (a.astype(F32) + b.astype(F32)).astype(BF)  16.8 us
  transfers between devices with their start and end apart: 51, of which 17 were waited for; matrix products, arithmetic and copies ran while one was open for 6% of the time, Pallas kernels for 30%

profile of v2, /device:TPU:0, one launch (start us, length us, event | category | flops | bytes accessed | tf_op | source)
XLA Modules:
  0.0 481.7 jit_solution(7549586408514463889)
XLA Ops:
  2.8 6.5 %all-to-all-start.1 = ((bf16[4,192,768]{2,1,0:T(8,128)(2,1)}), bf16[4,192,768]{2,1,0:T(8,128)(2,1)S(1)}, u32[]{:S(2)}, u32[]{:S(2)}) async-start(bf16[4,192,768]{2,1,0:T(8,128)(2,1)} %broadcast_in_dim.22), calls=%async_computation.1 | async-start | bytes 2359296 | tf_op jit(solution)/shard_map/all_to_all | solution.py:701
  9.4 28.4 %all-to-all-done.1.rest_8_ = bf16[4,192,768]{2,1,0:T(8,128)(2,1)S(1)} async-done(((bf16[4,192,768]{2,1,0:T(8,128)(2,1)}), bf16[4,192,768]{2,1,0:T(8,128)(2,1)S(1)}, u32[]{:S(2)}, u32[]{:S(2)}) %all-to-all-start.1) | async-done | bytes 1179680 | tf_op jit(solution)/shard_map/all_to_all | solution.py:701
  39.2 3.6 all-to-all-start
  43.3 2.4 pack.1.rest_4_.rest_0_
  45.8 2.0 collective-permute-start.3
  47.7 2.4 collective-permute-start.4
  50.2 2.9 deal.2
  54.6 18.8 %collective-permute-done.3.rest_5_.rest_1_ = bf16[112,1152]{1,0:T(8,128)(2,1)} collective-permute-done((bf16[112,1152]{1,0:T(8,128)(2,1)}, bf16[112,1152]{1,0:T(8,128)(2,1)}, u32[]{:S(2)}, u32[]{:S(2)}) %collective-permute-start.3) | collective-permute-done | bytes 258080 | tf_op jit(solution)/shard_map/ppermute | solution.py:693
  73.4 21.4 %collective-permute-done.4.rest_6_.rest_2_ = bf16[112,1152]{1,0:T(8,128)(2,1)} collective-permute-done((bf16[112,1152]{1,0:T(8,128)(2,1)}, bf16[112,1152]{1,0:T(8,128)(2,1)}, u32[]{:S(2)}, u32[]{:S(2)}) %collective-permute-start.4) | collective-permute-done | bytes 258080 | tf_op jit(solution)/shard_map/ppermute | solution.py:693
  96.3 5.1 %collective-permute-done.6.rest_8_.rest_4_ = bf16[112,1152]{1,0:T(8,128)(2,1)S(1)} collective-permute-done((bf16[112,1152]{1,0:T(8,128)(2,1)S(1)}, bf16[112,1152]{1,0:T(8,128)(2,1)S(1)}, u32[]{:S(2)}, u32[]{:S(2)}) %collective-permute-start.6) | collective-permute-done | bytes 258080 | tf_op jit(solution)/shard_map/ppermute | solution.py:693
  106.2 4.6 collective-permute-done.7.rest_9_.rest_5_
  110.8 4.2 collective-permute-done.8.rest_10_.rest_6_
  115.0 2.9 collective-permute-done.9.rest_11_.rest_7_
  119.5 2.9 deal.3
  126.6 10.1 %project.1 = (bf16[1024,2304]{1,0:T(8,128)(2,1)}, bf16[1024,768]{1,0:T(8,128)(2,1)}, f32[8,768]{1,0:T(8,128)}, f32[8,3072]{1,0:T(8,128)}) custom-call(s32[3]{0:T(128)} %pad_add_fusion.me_ref, bf16[4,256,768]{2,1,0:T(8,128)(2,1)} %rest_0_.4, bf16[256,768]{1,0:T(8,128)(2,1)} %copy-done.16, bf16[256,768]{1,0:T(8,128)(2,1)} %collective-permute-done.1.rest_2_, ...), custom_call_target="tpu_custom_call" | custom-call | flops 8999999488 | bytes 1048576 | tf_op jit(solution)/shard_map/project/pallas_call | solution.py:280
  136.7 13.6 %attend.3 = (bf16[1024,768]{1,0:T(8,128)(2,1)}, f32[6,8,1024]{2,1,0:T(8,128)}) custom-call(bf16[1024,2304]{1,0:T(8,128)(2,1)} %get-tuple-element.69.q_ref.k_ref.v_ref, bf16[1024,2304]{1,0:T(8,128)(2,1)} %get-tuple-element.69.q_ref.k_ref.v_ref, bf16[1024,2304]{1,0:T(8,128)(2,1)} %get-tuple-element.69.q_ref.k_ref.v_ref, s32[1024,1]{1,0:T(8,128)} %copy.51.sc_ref, ...), custom_call_target="tpu_custom_call" | custom-call | flops 12000000000 | bytes 1048576 | tf_op jit(solution)/shard_map/attend/pallas_call | solution.py:327
  150.9 2.6 collective-permute-done.24.rest_9_
  153.5 30.3 %collective-permute-done.21.rest_5_ = bf16[4,96,1920]{2,1,0:T(8,128)(2,1)S(1)} collective-permute-done((bf16[4,96,1920]{2,1,0:T(8,128)(2,1)S(1)}, bf16[4,96,1920]{2,1,0:T(8,128)(2,1)S(1)}, u32[]{:S(2)}, u32[]{:S(2)}) %collective-permute-start.21) | collective-permute-done | bytes 1474592 | tf_op jit(solution)/shard_map/ppermute | solution.py:693
  183.8 14.0 %attend.4 = (bf16[1024,768]{1,0:T(8,128)(2,1)}, f32[6,8,1024]{2,1,0:T(8,128)}) custom-call(bf16[1024,2304]{1,0:T(8,128)(2,1)} %get-tuple-element.69.q_ref.k_ref.v_ref, bf16[1024,2304]{1,0:T(8,128)(2,1)} %get-tuple-element.69.q_ref.k_ref.v_ref, bf16[1024,2304]{1,0:T(8,128)(2,1)} %get-tuple-element.69.q_ref.k_ref.v_ref, ...), custom_call_target="tpu_custom_call", output_to_operand_aliasing={{0}: (5, {}), {1}: (6, {})} | custom-call | flops 12000000000 | bytes 1048576 | tf_op jit(solution)/shard_map/attend/pallas_call | solution.py:327
  198.3 13.5 %attend.5 = (bf16[1024,768]{1,0:T(8,128)(2,1)}, f32[6,8,1024]{2,1,0:T(8,128)}) custom-call(bf16[1024,2304]{1,0:T(8,128)(2,1)} %get-tuple-element.69.q_ref.k_ref.v_ref, bf16[1024,2304]{1,0:T(8,128)(2,1)} %get-tuple-element.69.q_ref.k_ref.v_ref, bf16[1024,2304]{1,0:T(8,128)(2,1)} %get-tuple-element.69.q_ref.k_ref.v_ref, ...), custom_call_target="tpu_custom_call", output_to_operand_aliasing={{0}: (5, {}), {1}: (6, {})} | custom-call | flops 12000000000 | bytes 1048576 | tf_op jit(solution)/shard_map/attend/pallas_call | solution.py:327
  212.9 49.6 %middle.1 = (bf16[256,768]{1,0:T(8,128)(2,1)}, bf16[256,768]{1,0:T(8,128)(2,1)}, bf16[256,768]{1,0:T(8,128)(2,1)}, bf16[256,768]{1,0:T(8,128)(2,1)}, bf16[1024,3...) custom-call(s32[3]{0:T(128)} %pad_add_fusion.me_ref, ...), custom_call_target="tpu_custom_call" | custom-call | flops 48000000000 | bytes 1048576 | tf_op jit(solution)/shard_map/middle/pallas_call | solution.py:487
  262.5 12.4 %grad_up_out.1 = (bf16[768,1920]{1,0:T(8,128)(2,1)}, bf16[768,1920]{1,0:T(8,128)(2,1)}) custom-call(s32[3]{0:T(128)} %pad_add_fusion.me_ref, bf16[1024,768]{1,0:T(8,128)(2,1)} %get-tuple-element.108.l_ref, bf16[1024,3072]{1,0:T(8,128)(2,1)} %get-tuple-element.109.p_ref, bf16[1024,768]{1,0:T(8,128)(2,1)} %get-tuple-element.74.c_ref.o_ref, ...), custom_call_target="tpu_custom_call" | custom-call | flops 12000000000 | bytes 1048576 | tf_op jit(solution)/shard_map/grad_up_out/pallas_call | solution.py:578
  275.3 14.8 %attend_back.3 = (bf16[1024,768]{1,0:T(8,128)(2,1)}, bf16[1024,768]{1,0:T(8,128)(2,1)}, bf16[1024,768]{1,0:T(8,128)(2,1)}, f32[8,768]{1,0:T(8,128)}) custom-call(bf16[1024,2304]{1,0:T(8,128)(2,1)} %get-tuple-element.69.q_ref.k_ref.v_ref, bf16[1024,2304]{1,0:T(8,128)(2,1)} %get-tuple-element.69.q_ref.k_ref.v_ref, ...), custom_call_target="tpu_custom_call" | custom-call | flops 12000000000 | bytes 1048576 | tf_op jit(solution)/shard_map/attend_back/pallas_call | solution.py:388
  290.1 14.9 %attend_back.4 = (bf16[1024,768]{1,0:T(8,128)(2,1)}, bf16[1024,768]{1,0:T(8,128)(2,1)}, bf16[1024,768]{1,0:T(8,128)(2,1)}, f32[8,768]{1,0:T(8,128)}) custom-call(bf16[1024,2304]{1,0:T(8,128)(2,1)} %get-tuple-element.69.q_ref.k_ref.v_ref, ...), custom_call_target="tpu_custom_call", output_to_operand_aliasing={{0}: (8, {}), {1}: (9, {}), {2}: (10, {}), {3}: (11, {})} | custom-call | flops 12000000000 | bytes 1048576 | tf_op jit(solution)/shard_map/attend_back/pallas_call | solution.py:388
  305.0 14.7 %attend_back.5 = (bf16[1024,768]{1,0:T(8,128)(2,1)}, bf16[1024,768]{1,0:T(8,128)(2,1)}, bf16[1024,768]{1,0:T(8,128)(2,1)}, f32[8,768]{1,0:T(8,128)}) custom-call(bf16[1024,2304]{1,0:T(8,128)(2,1)} %get-tuple-element.69.q_ref.k_ref.v_ref, ...), custom_call_target="tpu_custom_call", output_to_operand_aliasing={{0}: (8, {}), {1}: (9, {}), {2}: (10, {}), {3}: (11, {})} | custom-call | flops 12000000000 | bytes 1048576 | tf_op jit(solution)/shard_map/attend_back/pallas_call | solution.py:388
  319.8 9.8 %grad_qkv.1 = (bf16[8,112,1152]{2,1,0:T(8,128)(2,1)}, bf16[8,112,1152]{2,1,0:T(8,128)(2,1)}) custom-call(s32[3]{0:T(128)} %pad_add_fusion.me_ref, bf16[1024,768]{1,0:T(8,128)(2,1)} %get-tuple-element.75.x_ref, bf16[1024,768]{1,0:T(8,128)(2,1)} %get-tuple-element.95.q_ref, bf16[1024,768]{1,0:T(8,128)(2,1)} %get-tuple-element.96.k_ref, ...), custom_call_target="tpu_custom_call" | custom-call | flops 8999999488 | bytes 1048576 | tf_op jit(solution)/shard_map/grad_qkv/pallas_call | solution.py:625
  329.8 12.5 %grad_down.1 = (bf16[8,192,768]{2,1,0:T(8,128)(2,1)}, bf16[8,192,768]{2,1,0:T(8,128)(2,1)}) custom-call(s32[3]{0:T(128)} %pad_add_fusion.me_ref, bf16[1024,3072]{1,0:T(8,128)(2,1)} %get-tuple-element.113.a_ref, bf16[1024,768]{1,0:T(8,128)(2,1)} %get-tuple-element.114.g_ref), custom_call_target="tpu_custom_call" | custom-call | flops 12000000000 | bytes 1048576 | tf_op jit(solution)/shard_map/grad_down/pallas_call | solution.py:530
  342.6 2.9 add_convert_fusion.1
  347.2 3.8 add_convert_fusion
  352.5 2.5 fusion
  357.8 12.7 %collective-permute-done.34 = bf16[4,112,1152]{2,1,0:T(8,128)(2,1)S(1)} collective-permute-done((bf16[4,112,1152]{2,1,0:T(8,128)(2,1)S(1)}, bf16[4,112,1152]{2,1,0:T(8,128)(2,1)S(1)}, u32[]{:S(2)}, u32[]{:S(2)}) %collective-permute-start.34) | collective-permute-done | bytes 1032224 | tf_op jit(solution)/shard_map/ppermute | solution.py:693
  371.7 4.2 all-to-all-start.2
  376.0 2.4 dynamic-slice_bitcast_fusion.1
  379.9 10.8 %grad_in.1 = (bf16[256,768]{1,0:T(8,128)(2,1)}, bf16[256,768]{1,0:T(8,128)(2,1)}, bf16[256,768]{1,0:T(8,128)(2,1)}, bf16[256,768]{1,0:T(8,128)(2,1)}) custom-call(s32[3]{0:T(128)} %pad_add_fusion.me_ref, bf16[1024,768]{1,0:T(8,128)(2,1)} %get-tuple-element.95.q_ref, bf16[1024,768]{1,0:T(8,128)(2,1)} %get-tuple-element.96.k_ref, ...), custom_call_target="tpu_custom_call" | custom-call | flops 8999999488 | bytes 1048576 | tf_op jit(solution)/shard_map/grad_in/pallas_call | solution.py:661
  390.7 1.6 collective-permute-start.31
  392.6 13.4 %collective-permute-done.43 = bf16[4,192,768]{2,1,0:T(8,128)(2,1)} collective-permute-done((bf16[4,192,768]{2,1,0:T(8,128)(2,1)}, bf16[4,192,768]{2,1,0:T(8,128)(2,1)}, u32[]{:S(2)}, u32[]{:S(2)}) %collective-permute-start.43) | collective-permute-done | bytes 1179680 | tf_op jit(solution)/shard_map/ppermute | solution.py:693
  406.0 2.6 fusion.2
  408.6 4.8 all-to-all-start.4
  413.3 1.8 fusion.1
  419.7 3.7 place.3
  423.5 6.6 %collective-permute-done.28.refs_2_ = bf16[256,768]{1,0:T(8,128)(2,1)S(1)} collective-permute-done((bf16[256,768]{1,0:T(8,128)(2,1)}, bf16[256,768]{1,0:T(8,128)(2,1)S(1)}, u32[]{:S(2)}, u32[]{:S(2)}) %collective-permute-start.28) | collective-permute-done | bytes 393248 | tf_op jit(solution)/shard_map/ppermute | solution.py:690
  430.1 7.5 %collective-permute-done.29.refs_3_ = bf16[256,768]{1,0:T(8,128)(2,1)S(1)} collective-permute-done((bf16[256,768]{1,0:T(8,128)(2,1)S(1)}, bf16[256,768]{1,0:T(8,128)(2,1)S(1)}, u32[]{:S(2)}, u32[]{:S(2)}) %collective-permute-start.29) | collective-permute-done | bytes 393248 | tf_op jit(solution)/shard_map/ppermute | solution.py:690
  438.3 3.9 place.2
  443.6 1.6 collective-permute-start.35
  446.2 5.1 %all-to-all-start.3 = ((bf16[4,48,1920]{2,1,0:T(8,128)(2,1)}), bf16[4,48,1920]{2,1,0:T(8,128)(2,1)S(1)}, u32[]{:S(2)}, u32[]{:S(2)}) async-start(bf16[4,48,1920]{2,1,0:T(8,128)(2,1)} %fusion.4), calls=%async_computation.3 | async-start | bytes 1474560 | tf_op jit(solution)/shard_map/all_to_all | solution.py:701
  455.2 1.6 collective-permute-start.44
  458.0 13.0 %all-to-all-done.3 = bf16[4,48,1920]{2,1,0:T(8,128)(2,1)S(1)} async-done(((bf16[4,48,1920]{2,1,0:T(8,128)(2,1)}), bf16[4,48,1920]{2,1,0:T(8,128)(2,1)S(1)}, u32[]{:S(2)}, u32[]{:S(2)}) %all-to-all-start.3) | async-done | bytes 737312 | tf_op jit(solution)/shard_map/all_to_all | solution.py:701
  471.8 5.2 %collective-permute-done.40 = bf16[48,1920]{1,0:T(8,128)(2,1)S(1)} collective-permute-done((bf16[48,1920]{1,0:T(8,128)(2,1)S(1)}, bf16[48,1920]{1,0:T(8,128)(2,1)S(1)}, u32[]{:S(2)}, u32[]{:S(2)}) %collective-permute-start.40) | collective-permute-done | bytes 184352 | tf_op jit(solution)/shard_map/ppermute | solution.py:690
  (164 shorter events, 48.0 us)
Async XLA Ops:
  2.8 35.0 %all-to-all-start.1 = ((bf16[4,192,768]{2,1,0:T(8,128)(2,1)}), bf16[4,192,768]{2,1,0:T(8,128)(2,1)S(1)}, u32[]{:S(2)}, u32[]{:S(2)}) async-start(bf16[4,192,768]{2,1,0:T(8,128)(2,1)} %broadcast_in_dim.22), calls=%async_computation.1 | async-start | bytes 2359296 | tf_op jit(solution)/shard_map/all_to_all | solution.py:701
  39.2 86.9 %all-to-all-start = ((bf16[4,96,1920]{2,1,0:T(8,128)(2,1)}), bf16[4,96,1920]{2,1,0:T(8,128)(2,1)S(1)}, u32[]{:S(2)}, u32[]{:S(2)}) async-start(bf16[4,96,1920]{2,1,0:T(8,128)(2,1)} %broadcast_in_dim.10), calls=%async_computation | async-start | bytes 2949120 | tf_op jit(solution)/shard_map/all_to_all | solution.py:701
  45.8 27.6 %collective-permute-start.3 = (bf16[112,1152]{1,0:T(8,128)(2,1)}, bf16[112,1152]{1,0:T(8,128)(2,1)}, u32[]{:S(2)}, u32[]{:S(2)}) collective-permute-start(bf16[112,1152]{1,0:T(8,128)(2,1)} %pack.1.rest_4_.rest_0_), channel_id=1, source_target_pairs={{0,8},{4,12},{8,0},{12,4},{16,24},{20,28},{24,16},{28,20},{1,9},{5... | collective-permute-start | bytes 774152 | tf_op jit(solution)/shard_map/ppermute | solution.py:693
  47.7 47.1 %collective-permute-start.4 = (bf16[112,1152]{1,0:T(8,128)(2,1)}, bf16[112,1152]{1,0:T(8,128)(2,1)}, u32[]{:S(2)}, u32[]{:S(2)}) collective-permute-start(bf16[112,1152]{1,0:T(8,128)(2,1)} %pack.1.rest_4_.rest_0_), channel_id=1, source_target_pairs={{0,16},{4,20},{8,24},{12,28},{16,0},{20,4},{24,8},{28,12},{1,17},{... | collective-permute-start | bytes 774152 | tf_op jit(solution)/shard_map/ppermute | solution.py:693
  50.1 46.2 %collective-permute-start.5 = (bf16[112,1152]{1,0:T(8,128)(2,1)}, bf16[112,1152]{1,0:T(8,128)(2,1)}, u32[]{:S(2)}, u32[]{:S(2)}) collective-permute-start(bf16[112,1152]{1,0:T(8,128)(2,1)} %pack.1.rest_4_.rest_0_), channel_id=1, source_target_pairs={{0,24},{4,28},{8,16},{12,20},{16,8},{20,12},{24,0},{28,4},{1,25},{... | collective-permute-start | bytes 774152 | tf_op jit(solution)/shard_map/ppermute | solution.py:693
  53.1 50.3 %collective-permute-start = (bf16[256,768]{1,0:T(8,128)(2,1)}, bf16[256,768]{1,0:T(8,128)(2,1)S(1)}, u32[]{:S(2)}, u32[]{:S(2)}) collective-permute-start(bf16[256,768]{1,0:T(8,128)(2,1)} %get-tuple-element.66), channel_id=1, source_target_pairs={{0,1},{1,0},{2,3},{3,2},{4,5},{5,4},{6,7},{7,6},{8,9},{9,8},{10,11... | collective-permute-start | bytes 1179656 | tf_op jit(solution)/shard_map/ppermute | solution.py:690
  53.1 51.9 %collective-permute-start.1 = (bf16[256,768]{1,0:T(8,128)(2,1)}, bf16[256,768]{1,0:T(8,128)(2,1)}, u32[]{:S(2)}, u32[]{:S(2)}) collective-permute-start(bf16[256,768]{1,0:T(8,128)(2,1)} %get-tuple-element.67), channel_id=1, source_target_pairs={{0,2},{1,3},{2,0},{3,1},{4,6},{5,7},{6,4},{7,5},{8,10},{9,11},{10,... | collective-permute-start | bytes 1179656 | tf_op jit(solution)/shard_map/ppermute | solution.py:690
  73.4 31.6 %collective-permute-start.2 = (bf16[256,768]{1,0:T(8,128)(2,1)}, bf16[256,768]{1,0:T(8,128)(2,1)}, u32[]{:S(2)}, u32[]{:S(2)}) collective-permute-start(bf16[256,768]{1,0:T(8,128)(2,1)} %get-tuple-element.68), channel_id=1, source_target_pairs={{0,3},{1,2},{2,1},{3,0},{4,7},{5,6},{6,5},{7,4},{8,11},{9,10},{10,... | collective-permute-start | bytes 1179656 | tf_op jit(solution)/shard_map/ppermute | solution.py:690
  94.8 6.6 %collective-permute-start.6 = (bf16[112,1152]{1,0:T(8,128)(2,1)S(1)}, bf16[112,1152]{1,0:T(8,128)(2,1)S(1)}, u32[]{:S(2)}, u32[]{:S(2)}) collective-permute-start(bf16[112,1152]{1,0:T(8,128)(2,1)S(1)} %copy-done.22), channel_id=1, source_target_pairs={{0,4},{4,0},{8,12},{12,8},{16,20},{20,16},{24,28},{28,24},{1,5},{5... | collective-permute-start | bytes 774152 | tf_op jit(solution)/shard_map/ppermute | solution.py:693
  96.3 6.6 %collective-permute-start.10 = (bf16[112,1152]{1,0:T(8,128)(2,1)S(1)}, bf16[112,1152]{1,0:T(8,128)(2,1)S(1)}, u32[]{:S(2)}, u32[]{:S(2)}) collective-permute-start(bf16[112,1152]{1,0:T(8,128)(2,1)S(1)} %copy-done.22), channel_id=1, source_target_pairs={{0,1},{1,0},{2,3},{3,2},{4,5},{5,4},{6,7},{7,6},{8,9},{9,8},{10,11... | collective-permute-start | bytes 774152 | tf_op jit(solution)/shard_map/ppermute | solution.py:690
  101.4 9.4 %collective-permute-start.7 = (bf16[112,1152]{1,0:T(8,128)(2,1)}, bf16[112,1152]{1,0:T(8,128)(2,1)}, u32[]{:S(2)}, u32[]{:S(2)}) collective-permute-start(bf16[112,1152]{1,0:T(8,128)(2,1)} %collective-permute-done.3.rest_5_.rest_1_), channel_id=1, source_target_pairs={{0,4},{4,0},{8,12},{12,8},{16,20},{20,16},{24,28},{28,24},{1,5},{5... | collective-permute-start | bytes 774152 | tf_op jit(solution)/shard_map/ppermute | solution.py:693
  102.9 12.1 %collective-permute-start.8 = (bf16[112,1152]{1,0:T(8,128)(2,1)}, bf16[112,1152]{1,0:T(8,128)(2,1)S(1)}, u32[]{:S(2)}, u32[]{:S(2)}) collective-permute-start(bf16[112,1152]{1,0:T(8,128)(2,1)} %collective-permute-done.4.rest_6_.rest_2_), channel_id=1, source_target_pairs={{0,4},{4,0},{8,12},{12,8},{16,20},{20,16},{24,28},{28,24},{1,5},{5... | collective-permute-start | bytes 774152 | tf_op jit(solution)/shard_map/ppermute | solution.py:693
  103.4 14.4 %collective-permute-start.9 = (bf16[112,1152]{1,0:T(8,128)(2,1)}, bf16[112,1152]{1,0:T(8,128)(2,1)}, u32[]{:S(2)}, u32[]{:S(2)}) collective-permute-start(bf16[112,1152]{1,0:T(8,128)(2,1)} %collective-permute-done.5.rest_7_.rest_3_), channel_id=1, source_target_pairs={{0,4},{4,0},{8,12},{12,8},{16,20},{20,16},{24,28},{28,24},{1,5},{5... | collective-permute-start | bytes 774152 | tf_op jit(solution)/shard_map/ppermute | solution.py:693
  105.0 12.9 %collective-permute-start.11 = (bf16[112,1152]{1,0:T(8,128)(2,1)}, bf16[112,1152]{1,0:T(8,128)(2,1)}, u32[]{:S(2)}, u32[]{:S(2)}) collective-permute-start(bf16[112,1152]{1,0:T(8,128)(2,1)} %collective-permute-done.3.rest_5_.rest_1_), channel_id=1, source_target_pairs={{0,1},{1,0},{2,3},{3,2},{4,5},{5,4},{6,7},{7,6},{8,9},{9,8},{10,11... | collective-permute-start | bytes 774152 | tf_op jit(solution)/shard_map/ppermute | solution.py:690
  105.0 13.4 %collective-permute-start.12 = (bf16[112,1152]{1,0:T(8,128)(2,1)}, bf16[112,1152]{1,0:T(8,128)(2,1)}, u32[]{:S(2)}, u32[]{:S(2)}) collective-permute-start(bf16[112,1152]{1,0:T(8,128)(2,1)} %collective-permute-done.4.rest_6_.rest_2_), channel_id=1, source_target_pairs={{0,1},{1,0},{2,3},{3,2},{4,5},{5,4},{6,7},{7,6},{8,9},{9,8},{10,11... | collective-permute-start | bytes 774152 | tf_op jit(solution)/shard_map/ppermute | solution.py:690
  110.8 11.7 %collective-permute-start.13 = (bf16[112,1152]{1,0:T(8,128)(2,1)}, bf16[112,1152]{1,0:T(8,128)(2,1)}, u32[]{:S(2)}, u32[]{:S(2)}) collective-permute-start(bf16[112,1152]{1,0:T(8,128)(2,1)} %collective-permute-done.5.rest_7_.rest_3_), channel_id=1, source_target_pairs={{0,1},{1,0},{2,3},{3,2},{4,5},{5,4},{6,7},{7,6},{8,9},{9,8},{10,11... | collective-permute-start | bytes 774152 | tf_op jit(solution)/shard_map/ppermute | solution.py:690
  115.0 8.0 %collective-permute-start.14 = (bf16[112,1152]{1,0:T(8,128)(2,1)}, bf16[112,1152]{1,0:T(8,128)(2,1)}, u32[]{:S(2)}, u32[]{:S(2)}) collective-permute-start(bf16[112,1152]{1,0:T(8,128)(2,1)} %copy-done.23), channel_id=1, source_target_pairs={{0,1},{1,0},{2,3},{3,2},{4,5},{5,4},{6,7},{7,6},{8,9},{9,8},{10,11... | collective-permute-start | bytes 774152 | tf_op jit(solution)/shard_map/ppermute | solution.py:690
  117.8 6.7 %collective-permute-start.15 = (bf16[112,1152]{1,0:T(8,128)(2,1)}, bf16[112,1152]{1,0:T(8,128)(2,1)}, u32[]{:S(2)}, u32[]{:S(2)}) collective-permute-start(bf16[112,1152]{1,0:T(8,128)(2,1)} %collective-permute-done.7.rest_9_.rest_5_), channel_id=1, source_target_pairs={{0,1},{1,0},{2,3},{3,2},{4,5},{5,4},{6,7},{7,6},{8,9},{9,8},{10,11... | collective-permute-start | bytes 774152 | tf_op jit(solution)/shard_map/ppermute | solution.py:690
  117.8 8.2 %collective-permute-start.16 = (bf16[112,1152]{1,0:T(8,128)(2,1)S(1)}, bf16[112,1152]{1,0:T(8,128)(2,1)}, u32[]{:S(2)}, u32[]{:S(2)}) collective-permute-start(bf16[112,1152]{1,0:T(8,128)(2,1)S(1)} %collective-permute-done.8.rest_10_.rest_6_), channel_id=1, source_target_pairs={{0,1},{1,0},{2,3},{3,2},{4,5},{5,4},{6,7},{7,6},{8,9},{9,8},{10,11... | collective-permute-start | bytes 774152 | tf_op jit(solution)/shard_map/ppermute | solution.py:690
  118.4 8.3 %collective-permute-start.17 = (bf16[112,1152]{1,0:T(8,128)(2,1)}, bf16[112,1152]{1,0:T(8,128)(2,1)}, u32[]{:S(2)}, u32[]{:S(2)}) collective-permute-start(bf16[112,1152]{1,0:T(8,128)(2,1)} %collective-permute-done.9.rest_11_.rest_7_), channel_id=1, source_target_pairs={{0,1},{1,0},{2,3},{3,2},{4,5},{5,4},{6,7},{7,6},{8,9},{9,8},{10,11... | collective-permute-start | bytes 774152 | tf_op jit(solution)/shard_map/ppermute | solution.py:690
  122.5 27.9 %collective-permute-start.18 = (bf16[256,768]{1,0:T(8,128)(2,1)}, bf16[256,768]{1,0:T(8,128)(2,1)S(1)}, u32[]{:S(2)}, u32[]{:S(2)}) collective-permute-start(bf16[256,768]{1,0:T(8,128)(2,1)} %get-tuple-element.78), channel_id=1, source_target_pairs={{0,1},{1,0},{2,3},{3,2},{4,5},{5,4},{6,7},{7,6},{8,9},{9,8},{10,11... | collective-permute-start | bytes 1179656 | tf_op jit(solution)/shard_map/ppermute | solution.py:690
  123.0 74.9 %collective-permute-start.19 = (bf16[256,768]{1,0:T(8,128)(2,1)}, bf16[256,768]{1,0:T(8,128)(2,1)}, u32[]{:S(2)}, u32[]{:S(2)}) collective-permute-start(bf16[256,768]{1,0:T(8,128)(2,1)} %get-tuple-element.79), channel_id=1, source_target_pairs={{0,2},{1,3},{2,0},{3,1},{4,6},{5,7},{6,4},{7,5},{8,10},{9,11},{10,... | collective-permute-start | bytes 1179656 | tf_op jit(solution)/shard_map/ppermute | solution.py:690
  124.5 28.9 %collective-permute-start.24 = (bf16[4,192,768]{2,1,0:T(8,128)(2,1)S(1)}, bf16[4,192,768]{2,1,0:T(8,128)(2,1)}, u32[]{:S(2)}, u32[]{:S(2)}) collective-permute-start(bf16[4,192,768]{2,1,0:T(8,128)(2,1)S(1)} %all-to-all-done.1.rest_8_), channel_id=1, source_target_pairs={{0,4},{4,0},{8,12},{12,8},{16,20},{20,16},{24,28},{28,24},{1,5},{5... | collective-permute-start | bytes 3538952 | tf_op jit(solution)/shard_map/ppermute | solution.py:693
  126.0 57.8 %collective-permute-start.21 = (bf16[4,96,1920]{2,1,0:T(8,128)(2,1)S(1)}, bf16[4,96,1920]{2,1,0:T(8,128)(2,1)S(1)}, u32[]{:S(2)}, u32[]{:S(2)}) collective-permute-start(bf16[4,96,1920]{2,1,0:T(8,128)(2,1)S(1)} %all-to-all-done.rest_4_), channel_id=1, source_target_pairs={{0,4},{4,0},{8,12},{12,8},{16,20},{20,16},{24,28},{28,24},{1,5},{5... | collective-permute-start | bytes 4423688 | tf_op jit(solution)/shard_map/ppermute | solution.py:693
  150.3 61.5 %collective-permute-start.25 = (bf16[4,192,768]{2,1,0:T(8,128)(2,1)S(1)}, bf16[4,192,768]{2,1,0:T(8,128)(2,1)S(1)}, u32[]{:S(2)}, u32[]{:S(2)}) collective-permute-start(bf16[4,192,768]{2,1,0:T(8,128)(2,1)S(1)} %all-to-all-done.1.rest_8_), channel_id=1, source_target_pairs={{0,1},{1,0},{2,3},{3,2},{4,5},{5,4},{6,7},{7,6},{8,9},{9,8},{10,11... | collective-permute-start | bytes 3538952 | tf_op jit(solution)/shard_map/ppermute | solution.py:690
  150.4 61.4 %collective-permute-start.22 = (bf16[4,96,1920]{2,1,0:T(8,128)(2,1)S(1)}, bf16[4,96,1920]{2,1,0:T(8,128)(2,1)}, u32[]{:S(2)}, u32[]{:S(2)}) collective-permute-start(bf16[4,96,1920]{2,1,0:T(8,128)(2,1)S(1)} %all-to-all-done.rest_4_), channel_id=1, source_target_pairs={{0,1},{1,0},{2,3},{3,2},{4,5},{5,4},{6,7},{7,6},{8,9},{9,8},{10,11... | collective-permute-start | bytes 4423688 | tf_op jit(solution)/shard_map/ppermute | solution.py:690
  153.5 58.4 %collective-permute-start.26 = (bf16[4,192,768]{2,1,0:T(8,128)(2,1)}, bf16[4,192,768]{2,1,0:T(8,128)(2,1)}, u32[]{:S(2)}, u32[]{:S(2)}) collective-permute-start(bf16[4,192,768]{2,1,0:T(8,128)(2,1)} %collective-permute-done.24.rest_9_), channel_id=1, source_target_pairs={{0,1},{1,0},{2,3},{3,2},{4,5},{5,4},{6,7},{7,6},{8,9},{9,8},{10,11... | collective-permute-start | bytes 3538952 | tf_op jit(solution)/shard_map/ppermute | solution.py:690
  183.8 28.0 %collective-permute-start.23 = (bf16[4,96,1920]{2,1,0:T(8,128)(2,1)S(1)}, bf16[4,96,1920]{2,1,0:T(8,128)(2,1)}, u32[]{:S(2)}, u32[]{:S(2)}) collective-permute-start(bf16[4,96,1920]{2,1,0:T(8,128)(2,1)S(1)} %collective-permute-done.21.rest_5_), channel_id=1, source_target_pairs={{0,1},{1,0},{2,3},{3,2},{4,5},{5,4},{6,7},{7,6},{8,9},{9,8},{10,11... | collective-permute-start | bytes 4423688 | tf_op jit(solution)/shard_map/ppermute | solution.py:690
  197.9 13.9 %collective-permute-start.20 = (bf16[256,768]{1,0:T(8,128)(2,1)}, bf16[256,768]{1,0:T(8,128)(2,1)S(1)}, u32[]{:S(2)}, u32[]{:S(2)}) collective-permute-start(bf16[256,768]{1,0:T(8,128)(2,1)} %get-tuple-element.80), channel_id=1, source_target_pairs={{0,3},{1,2},{2,1},{3,0},{4,7},{5,6},{6,5},{7,4},{8,11},{9,10},{10,... | collective-permute-start | bytes 1179656 | tf_op jit(solution)/shard_map/ppermute | solution.py:690
  274.9 76.0 %collective-permute-start.37 = (bf16[8,96,1920]{2,1,0:T(8,128)(2,1)}, bf16[8,96,1920]{2,1,0:T(8,128)(2,1)S(1)}, u32[]{:S(2)}, u32[]{:S(2)}) collective-permute-start(bf16[8,96,1920]{2,1,0:T(8,128)(2,1)} %bitcast.66), channel_id=1, source_target_pairs={{0,1},{1,0},{2,3},{3,2},{4,5},{5,4},{6,7},{7,6},{8,9},{9,8},{10,11... | collective-permute-start | bytes 8847368 | tf_op jit(solution)/shard_map/ppermute | solution.py:690
  329.6 13.0 %collective-permute-start.33 = (bf16[8,112,1152]{2,1,0:T(8,128)(2,1)}, bf16[8,112,1152]{2,1,0:T(8,128)(2,1)}, u32[]{:S(2)}, u32[]{:S(2)}) collective-permute-start(bf16[8,112,1152]{2,1,0:T(8,128)(2,1)} %get-tuple-element.107), channel_id=1, source_target_pairs={{0,1},{1,0},{2,3},{3,2},{4,5},{5,4},{6,7},{7,6},{8,9},{9,8},{10,11... | collective-permute-start | bytes 6193160 | tf_op jit(solution)/shard_map/ppermute | solution.py:690
  345.5 25.0 %collective-permute-start.34 = (bf16[4,112,1152]{2,1,0:T(8,128)(2,1)S(1)}, bf16[4,112,1152]{2,1,0:T(8,128)(2,1)S(1)}, u32[]{:S(2)}, u32[]{:S(2)}) collective-permute-start(bf16[4,112,1152]{2,1,0:T(8,128)(2,1)S(1)} %dynamic-slice_bitcast_fusion.2), channel_id=1, source_target_pairs={{0,4},{4,0},{8,12},{12,8},{16,20},{20,16},{24,28},{28,24},{1,5},{5... | collective-permute-start | bytes 3096584 | tf_op jit(solution)/shard_map/ppermute | solution.py:693
  356.3 57.0 %collective-permute-start.38 = (bf16[8,48,1920]{2,1,0:T(8,128)(2,1)}, bf16[8,48,1920]{2,1,0:T(8,128)(2,1)}, u32[]{:S(2)}, u32[]{:S(2)}) collective-permute-start(bf16[8,48,1920]{2,1,0:T(8,128)(2,1)} %dynamic-slice_bitcast_fusion), channel_id=1, source_target_pairs={{0,2},{1,3},{2,0},{3,1},{4,6},{5,7},{6,4},{7,5},{8,10},{9,11},{10,... | collective-permute-start | bytes 4423688 | tf_op jit(solution)/shard_map/ppermute | solution.py:690
  371.7 36.8 %all-to-all-start.2 = ((bf16[4,112,1152]{2,1,0:T(8,128)(2,1)}), bf16[4,112,1152]{2,1,0:T(8,128)(2,1)}, u32[]{:S(2)}, u32[]{:S(2)}) async-start(bf16[4,112,1152]{2,1,0:T(8,128)(2,1)} %fusion.3), calls=%async_computation.2 | async-start | bytes 2064384 | tf_op jit(solution)/shard_map/all_to_all | solution.py:701
  378.4 27.6 %collective-permute-start.43 = (bf16[4,192,768]{2,1,0:T(8,128)(2,1)}, bf16[4,192,768]{2,1,0:T(8,128)(2,1)}, u32[]{:S(2)}, u32[]{:S(2)}) collective-permute-start(bf16[4,192,768]{2,1,0:T(8,128)(2,1)} %dynamic-slice_bitcast_fusion.1), channel_id=1, source_target_pairs={{0,4},{4,0},{8,12},{12,8},{16,20},{20,16},{24,28},{28,24},{1,5},{5... | collective-permute-start | bytes 3538952 | tf_op jit(solution)/shard_map/ppermute | solution.py:693
  390.6 27.2 %collective-permute-start.30 = (bf16[256,768]{1,0:T(8,128)(2,1)}, bf16[256,768]{1,0:T(8,128)(2,1)}, u32[]{:S(2)}, u32[]{:S(2)}) collective-permute-start(bf16[256,768]{1,0:T(8,128)(2,1)} %get-tuple-element.100), channel_id=1, source_target_pairs={{0,1},{1,0},{2,3},{3,2},{4,5},{5,4},{6,7},{7,6},{8,9},{9,8},{10,11... | collective-permute-start | bytes 1179656 | tf_op jit(solution)/shard_map/ppermute | solution.py:690
  390.7 28.7 %collective-permute-start.31 = (bf16[256,768]{1,0:T(8,128)(2,1)}, bf16[256,768]{1,0:T(8,128)(2,1)}, u32[]{:S(2)}, u32[]{:S(2)}) collective-permute-start(bf16[256,768]{1,0:T(8,128)(2,1)} %get-tuple-element.101), channel_id=1, source_target_pairs={{0,2},{1,3},{2,0},{3,1},{4,6},{5,7},{6,4},{7,5},{8,10},{9,11},{10,... | collective-permute-start | bytes 1179656 | tf_op jit(solution)/shard_map/ppermute | solution.py:690
  392.3 27.5 %collective-permute-start.32 = (bf16[256,768]{1,0:T(8,128)(2,1)}, bf16[256,768]{1,0:T(8,128)(2,1)}, u32[]{:S(2)}, u32[]{:S(2)}) collective-permute-start(bf16[256,768]{1,0:T(8,128)(2,1)} %get-tuple-element.102), channel_id=1, source_target_pairs={{0,3},{1,2},{2,1},{3,0},{4,7},{5,6},{6,5},{7,4},{8,11},{9,10},{10,... | collective-permute-start | bytes 1179656 | tf_op jit(solution)/shard_map/ppermute | solution.py:690
  408.6 37.6 %all-to-all-start.4 = ((bf16[4,192,768]{2,1,0:T(8,128)(2,1)}), bf16[4,192,768]{2,1,0:T(8,128)(2,1)}, u32[]{:S(2)}, u32[]{:S(2)}) async-start(bf16[4,192,768]{2,1,0:T(8,128)(2,1)} %fusion.2), calls=%async_computation.4 | async-start | bytes 2359296 | tf_op jit(solution)/shard_map/all_to_all | solution.py:701
  416.3 28.9 %collective-permute-start.39 = (bf16[4,48,1920]{2,1,0:T(8,128)(2,1)S(1)}, bf16[4,48,1920]{2,1,0:T(8,128)(2,1)S(1)}, u32[]{:S(2)}, u32[]{:S(2)}) collective-permute-start(bf16[4,48,1920]{2,1,0:T(8,128)(2,1)S(1)} %dynamic-slice_bitcast_fusion.3), channel_id=1, source_target_pairs={{0,4},{4,0},{8,12},{12,8},{16,20},{20,16},{24,28},{28,24},{1,5},{5... | collective-permute-start | bytes 2211848 | tf_op jit(solution)/shard_map/ppermute | solution.py:693
  417.9 5.6 %collective-permute-start.27 = (bf16[256,768]{1,0:T(8,128)(2,1)}, bf16[256,768]{1,0:T(8,128)(2,1)S(1)}, u32[]{:S(2)}, u32[]{:S(2)}) collective-permute-start(bf16[256,768]{1,0:T(8,128)(2,1)} %get-tuple-element.82), channel_id=1, source_target_pairs={{0,1},{1,0},{2,3},{3,2},{4,5},{5,4},{6,7},{7,6},{8,9},{9,8},{10,11... | collective-permute-start | bytes 1179656 | tf_op jit(solution)/shard_map/ppermute | solution.py:690
  417.9 12.2 %collective-permute-start.28 = (bf16[256,768]{1,0:T(8,128)(2,1)}, bf16[256,768]{1,0:T(8,128)(2,1)S(1)}, u32[]{:S(2)}, u32[]{:S(2)}) collective-permute-start(bf16[256,768]{1,0:T(8,128)(2,1)} %get-tuple-element.83), channel_id=1, source_target_pairs={{0,2},{1,3},{2,0},{3,1},{4,6},{5,7},{6,4},{7,5},{8,10},{9,11},{10,... | collective-permute-start | bytes 1179656 | tf_op jit(solution)/shard_map/ppermute | solution.py:690
  419.4 18.2 %collective-permute-start.29 = (bf16[256,768]{1,0:T(8,128)(2,1)S(1)}, bf16[256,768]{1,0:T(8,128)(2,1)S(1)}, u32[]{:S(2)}, u32[]{:S(2)}) collective-permute-start(bf16[256,768]{1,0:T(8,128)(2,1)S(1)} %copy-done.15), channel_id=1, source_target_pairs={{0,3},{1,2},{2,1},{3,0},{4,7},{5,6},{6,5},{7,4},{8,11},{9,10},{10,... | collective-permute-start | bytes 1179656 | tf_op jit(solution)/shard_map/ppermute | solution.py:690
  443.6 9.0 %collective-permute-start.35 = (bf16[112,1152]{1,0:T(8,128)(2,1)S(1)}, bf16[112,1152]{1,0:T(8,128)(2,1)}, u32[]{:S(2)}, u32[]{:S(2)}) collective-permute-start(bf16[112,1152]{1,0:T(8,128)(2,1)S(1)} %reduce_sum.46), channel_id=1, source_target_pairs={{0,2},{1,3},{2,0},{3,1},{4,6},{5,7},{6,4},{7,5},{8,10},{9,11},{10,... | collective-permute-start | bytes 774152 | tf_op jit(solution)/shard_map/ppermute | solution.py:690
  446.2 24.7 %all-to-all-start.3 = ((bf16[4,48,1920]{2,1,0:T(8,128)(2,1)}), bf16[4,48,1920]{2,1,0:T(8,128)(2,1)S(1)}, u32[]{:S(2)}, u32[]{:S(2)}) async-start(bf16[4,48,1920]{2,1,0:T(8,128)(2,1)} %fusion.4), calls=%async_computation.3 | async-start | bytes 1474560 | tf_op jit(solution)/shard_map/all_to_all | solution.py:701
  455.2 16.4 %collective-permute-start.44 = (bf16[192,768]{1,0:T(8,128)(2,1)S(1)}, bf16[192,768]{1,0:T(8,128)(2,1)S(1)}, u32[]{:S(2)}, u32[]{:S(2)}) collective-permute-start(bf16[192,768]{1,0:T(8,128)(2,1)S(1)} %reduce_sum.48), channel_id=1, source_target_pairs={{0,2},{1,3},{2,0},{3,1},{4,6},{5,7},{6,4},{7,5},{8,10},{9,11},{10,... | collective-permute-start | bytes 884744 | tf_op jit(solution)/shard_map/ppermute | solution.py:690
  471.1 5.9 %collective-permute-start.40 = (bf16[48,1920]{1,0:T(8,128)(2,1)S(1)}, bf16[48,1920]{1,0:T(8,128)(2,1)S(1)}, u32[]{:S(2)}, u32[]{:S(2)}) collective-permute-start(bf16[48,1920]{1,0:T(8,128)(2,1)S(1)} %reduce_sum.47), channel_id=1, source_target_pairs={{0,2},{1,3},{2,0},{3,1},{4,6},{5,7},{6,4},{7,5},{8,10},{9,11},{10,... | collective-permute-start | bytes 552968 | tf_op jit(solution)/shard_map/ppermute | solution.py:690
  471.7 6.4 %collective-permute-start.45 = (bf16[192,768]{1,0:T(8,128)(2,1)S(1)}, bf16[192,768]{1,0:T(8,128)(2,1)S(1)}, u32[]{:S(2)}, u32[]{:S(2)}) collective-permute-start(bf16[192,768]{1,0:T(8,128)(2,1)S(1)} %add_convert_fusion.2), channel_id=1, source_target_pairs={{0,1},{1,0},{2,3},{3,2},{4,5},{5,4},{6,7},{7,6},{8,9},{9,8},{10,11... | collective-permute-start | bytes 884744 | tf_op jit(solution)/shard_map/ppermute | solution.py:690
  (29 other events, 386.7 us)

commit v3 on v2

--- a/solution.py
+++ b/solution.py
@@ -72,23 +72,23 @@
 def piece_copies(pieces, by_rows, rows, cols, dst, sems, bits):
     core, x_bit, z_at = bits
     lo, nc = cols
-    zs = len(pieces) // 4 if len(pieces[0].shape) == 2 else pieces[0].shape[0]
+    per = len(pieces) // 4
     copies = []
     for rc in range(2):
         row0 = rows * lax.bitwise_xor(core, rc) if by_rows else 0
         col0 = 0 if by_rows else pl.multiple_of(nc * lax.bitwise_xor(core, rc), nc)
         for rx in range(2):
-            for z in range(zs):
-                if len(pieces[0].shape) == 2:
-                    src, at = pieces[(rc * 2 + rx) * zs + z], lax.bitwise_xor(z_at, z)
-                else:
-                    src, at = pieces[rc * 2 + rx].at[z], z
-                row = row0 + rows * (2 if by_rows else 1) * (2 * at + lax.bitwise_xor(x_bit, rx))
+            line = []
+            for ref in pieces[(rc * 2 + rx) * per : (rc * 2 + rx + 1) * per]:
+                line += [ref] if len(ref.shape) == 2 else [ref.at[i] for i in range(ref.shape[0])]
+            for z, src in enumerate(line):
+                at = 2 * lax.bitwise_xor(z_at, z) + lax.bitwise_xor(x_bit, rx)
+                row = row0 + rows * (2 if by_rows else 1) * at
                 copies.append(
                     pltpu.make_async_copy(
                         src.at[pl.ds(0, rows), pl.ds(lo, nc)],
                         dst.at[pl.ds(pl.multiple_of(row, rows), rows), pl.ds(col0, nc)],
-                        sems.at[(rc * 2 + rx) * zs + z],
+                        sems.at[len(copies)],
                     )
                 )
     return copies
@@ -110,7 +110,7 @@
     kind, refs = weight
     if kind == "whole":
         return 1
-    return len(refs) if len(refs[0].shape) == 2 else 4 * refs[0].shape[0]
+    return sum(1 if len(v.shape) == 2 else v.shape[0] for v in refs)
 
 
 def put_block(refs, step, value):
@@ -341,7 +341,7 @@
     )(qkv, qkv, qkv, seg_col, seg_row, *before)
 
 
-def attend_back(qkv, context, grad_context, lse, seg_col, seg_row, start, count, before):
+def attend_back(qkv, context, grad_context, lse, seg_col, seg_row, start, count):
     chunk = 256
 
     def kernel(q_ref, k_ref, v_ref, o_ref, g_ref, lse_ref, sc_ref, sr_ref, *rest):
@@ -390,15 +390,16 @@
         grid=(count,),
         in_specs=[spec(0), spec(PAIRS), spec(2 * PAIRS), spec(0), spec(0),
                   pl.BlockSpec((1, 8, SEQ), lambda i: (i + start, 0, 0)), full((SEQ, 1)),
-                  full((1, SEQ))] + [ANY] * len(before),
-        out_specs=[spec(0), spec(0), spec(0), pl.BlockSpec((8, 2 * HD), lambda i: (0, i + start))],
-        input_output_aliases={8 + i: i for i in range(len(before))},
-        out_shape=[jax.ShapeDtypeStruct((SEQ, D), BF)] * 3 + [jax.ShapeDtypeStruct((8, D), F32)],
+                  full((1, SEQ))],
+        out_specs=[pl.BlockSpec((SEQ, 2 * HD), lambda i: (0, i))] * 3
+        + [pl.BlockSpec((8, 2 * HD), lambda i: (0, i))],
+        out_shape=[jax.ShapeDtypeStruct((SEQ, 2 * HD * count), BF)] * 3
+        + [jax.ShapeDtypeStruct((8, 2 * HD * count), F32)],
         scratch_shapes=[pltpu.VMEM((2 * HD, SEQ), F32), pltpu.VMEM((2 * HD, SEQ), BF)],
         compiler_params=params(),
         cost_estimate=cost(6 * count),
         name="attend_back",
-    )(qkv, qkv, qkv, context, grad_context, lse, seg_col, seg_row, *before)
+    )(qkv, qkv, qkv, context, grad_context, lse, seg_col, seg_row)
 
 
 def middle(me, context, x, g_own, g_near, vectors, up_bias, weight2, weight3, fsdp):
@@ -509,11 +510,17 @@
     )(me, context, x, vectors, up_bias, *g_args, *refs2, *refs3)
 
 
-def grad_down(me, act, grad_ffn, fsdp):
+def nearness(d, me):
+    x, z = lax.bitwise_xor(d & 1, me[1]), lax.bitwise_xor(d >> 1, me[2])
+    return x, z
+
+
+def grad_down(me, act, grad_ffn, fsdp, near):
     per = FF // fsdp
     steps = 8
     width = FF // steps
     inner = width // per
+    assert inner == 1 or not near
 
     def kernel(me_ref, a_ref, g_ref, send_ref, keep_ref, acc_ref):
         core, _, _ = bits_of(me_ref)
@@ -524,9 +531,15 @@
             send_ref[i] = take(1 - core)
             keep_ref[i] = take(core)
 
+    def where(i, me):
+        if not near:
+            return (i, 0, 0)
+        x, z = nearness(i, me)
+        return (x * (fsdp // 2) + z, 0, 0)
+
     rows = act.shape[0]
     out = jax.ShapeDtypeStruct((fsdp, per // 2, D), BF)
-    ospec = pl.BlockSpec((inner, per // 2, D), lambda i, me: (i, 0, 0))
+    ospec = pl.BlockSpec((inner, per // 2, D), where)
     return pl.pallas_call(
         kernel,
         grid_spec=pltpu.PrefetchScalarGridSpec(
@@ -544,23 +557,24 @@
     )(me, act, grad_ffn)
 
 
-def write_half(step, slots, send_ref, keep_ref, sems):
-    sending = pltpu.make_async_copy(slots.at[0], send_ref, sems.at[0])
-    keeping = pltpu.make_async_copy(slots.at[1], keep_ref, sems.at[1])
-    pl.when(step == 0)(sending.start)
+def write_half(step, moves, send_ref, keep_ref, sems):
+    sending, keeping = (
+        [pltpu.make_async_copy(a, b, sems.at[slot, i]) for i, (a, b) in enumerate(moves(slot, ref))]
+        for slot, ref in enumerate((send_ref, keep_ref)))
+    pl.when(step == 0)(lambda: start_all(sending))
 
     @pl.when(step == 1)
     def _():
-        keeping.start()
-        sending.wait()
-        keeping.wait()
+        start_all(keeping)
+        wait_all(sending)
+        wait_all(keeping)
 
 
 def half_of(i, core):
     return jnp.where(i == 0, 1 - core, core)
 
 
-def grad_up_out(me, low1, grad_pre, context, grad_attn):
+def grad_up_out(me, low1, grad_pre, context, grad_attn, fsdp, near):
     wu, wo = FF // 2, D // 2
 
     def kernel(me_ref, l_ref, p_ref, c_ref, a_ref, send_ref, keep_ref, slots, sems):
@@ -569,8 +583,19 @@
         low = l_ref[...]
         for lo in range(0, wu, D):
             slots[step, :, wo + lo : wo + lo + D] = tn(low, p_ref[:, lo : lo + D]).astype(BF)
-        write_half(step, slots, send_ref, keep_ref, sems)
-
+
+        def moves(slot, ref):
+            if not near:
+                return [(slots.at[slot], ref)]
+            return [(slots.at[slot, pl.ds((2 * d + h) * n, n)],
+                     ref.at[(lax.bitwise_xor(h, me_ref[0] >> 1),) + nearness(d, me_ref)])
+                    for d in range(fsdp) for h in range(2)]
+
+        write_half(step, moves, send_ref, keep_ref, sems)
+
+    n = D // fsdp // 2
+    count = 2 * fsdp if near else 1
+    shape = (2, 2, fsdp // 2, n, wu + wo) if near else (D, wu + wo)
     rows = low1.shape[0]
     half = lambda n: pl.BlockSpec(
         (rows, n), lambda i, me: (0, half_of(i, lax.bitwise_and(me[0], 1))))
@@ -580,68 +605,109 @@
         grid_spec=pltpu.PrefetchScalarGridSpec(
             num_scalar_prefetch=1, grid=(2,),
             in_specs=[full, half(wu), full, half(wo)], out_specs=[ANY] * 2,
-            scratch_shapes=[pltpu.VMEM((2, D, wu + wo), BF), pltpu.SemaphoreType.DMA((2,))]),
-        out_shape=[jax.ShapeDtypeStruct((D, wu + wo), BF)] * 2,
+            scratch_shapes=[pltpu.VMEM((2, D, wu + wo), BF), pltpu.SemaphoreType.DMA((2, count))]),
+        out_shape=[jax.ShapeDtypeStruct(shape, BF)] * 2,
         compiler_params=params(),
         cost_estimate=cost(12),
         name="grad_up_out",
     )(me, low1, grad_pre, context, grad_attn)
 
 
-def grad_qkv(me, x, dq, dk, dv, sums, up_sums, bias_sums, fsdp):
-    w = 3 * D // 2
+def grad_qkv(me, x, dqs, dks, dvs, sums, fsdp, near):
+    parts = len(dqs)
+    width = dqs[0].shape[1]
+    group = width * parts
+    w = 3 * group // 2
     per, per_up = D // fsdp, FF // fsdp
-    tall = per + SMALL
-
-    def kernel(me_ref, x_ref, q_ref, k_ref, v_ref, s_ref, u_ref, b_ref, send_ref, keep_ref, slots, sems):
+    tall = per + (SMALL if sums else 0)
+
+    def kernel(me_ref, x_ref, *rest):
+        q, k, v = (rest[i * parts : (i + 1) * parts] for i in range(3))
+        sum_refs, (send_ref, keep_ref, slots, sems) = rest[3 * parts : -4], rest[-4:]
         core, _, _ = bits_of(me_ref)
         step = pl.program_id(0)
         b = half_of(step, core)
 
-        def put(lo, val):
-            val = val.astype(BF)
+        def put(lo, ref, cols=slice(None)):
+            val = tn(x_ref[...], ref[:, cols]).astype(BF)
             for d in range(fsdp):
                 slots[step, d, :per, lo : lo + val.shape[1]] = val[d * per : (d + 1) * per]
 
+        def put_half_k(second, lo):
+            if parts == 1:
+                put(lo, k[0], slice(width // 2 * second, width // 2 * (second + 1)))
+            else:
+                for i in range(parts // 2):
+                    put(lo + i * width, k[parts // 2 * second + i])
+
         @pl.when(b == 0)
         def _():
-            put(0, tn(x_ref[...], q_ref[...]))
-            put(D, tn(x_ref[...], k_ref[:, : D // 2]))
+            for i in range(parts):
+                put(i * width, q[i])
+            put_half_k(0, group)
 
         @pl.when(b == 1)
         def _():
-            put(0, tn(x_ref[...], k_ref[:, D // 2 :]))
-            put(D // 2, tn(x_ref[...], v_ref[...]))
-
-        rows = jnp.concatenate([s_ref[0:6], b_ref[0:2]], 0)
-        for d in range(fsdp):
-            slots[step, d, per:, :] = jnp.zeros((SMALL, w), BF)
-            slots[step, d, per : per + 8, :per] = rows[:, d * per : (d + 1) * per].astype(BF)
-            slots[step, d, per + 8 : per + 9, :per_up] = u_ref[0:1, d * per_up : (d + 1) * per_up].astype(BF)
-        write_half(step, slots, send_ref, keep_ref, sems)
-
-    rows = x.shape[0]
-    full = lambda s: pl.BlockSpec(s, lambda i, me: (0, 0))
+            put_half_k(1, 0)
+            for i in range(parts):
+                put(group // 2 + i * width, v[i])
+
+        if sums:
+            s_ref, u_ref = sum_refs[:2]
+            biases = jnp.concatenate([r[0:2] for r in sum_refs[2:]], 1)
+            rows = jnp.concatenate([s_ref[0:6], biases], 0)
+            for d in range(fsdp):
+                slots[step, d, per:, :] = jnp.zeros((SMALL, w), BF)
+                slots[step, d, per : per + 8, :per] = rows[:, d * per : (d + 1) * per].astype(BF)
+                slots[step, d, per + 8 : per + 9, :per_up] = u_ref[0:1, d * per_up : (d + 1) * per_up].astype(BF)
+
+        def moves(slot, ref):
+            if not near:
+                return [(slots.at[slot], ref)]
+            return [(slots.at[slot, d], ref.at[nearness(d, me_ref)]) for d in range(fsdp)]
+
+        write_half(step, moves, send_ref, keep_ref, sems)
+
+    shape = (2, fsdp // 2, tall, w) if near else (fsdp, tall, w)
+    full = lambda v: pl.BlockSpec(v.shape, lambda i, me: (0, 0))
+    args = [x, *dqs, *dks, *dvs, *(sums or ())]
     return pl.pallas_call(
         kernel,
         grid_spec=pltpu.PrefetchScalarGridSpec(
             num_scalar_prefetch=1, grid=(2,),
-            in_specs=[full((rows, D))] * 4 + [full((8, D)), full((8, FF)), full((8, D))],
+            in_specs=[full(v) for v in args],
             out_specs=[ANY] * 2,
-            scratch_shapes=[pltpu.VMEM((2, fsdp, tall, w), BF), pltpu.SemaphoreType.DMA((2,))]),
-        out_shape=[jax.ShapeDtypeStruct((fsdp, tall, w), BF)] * 2,
-        compiler_params=params(),
-        cost_estimate=cost(9),
+            scratch_shapes=[pltpu.VMEM((2, fsdp, tall, w), BF),
+                            pltpu.SemaphoreType.DMA((2, fsdp if near else 1))]),
+        out_shape=[jax.ShapeDtypeStruct(shape, BF)] * 2,
+        compiler_params=params(),
+        cost_estimate=cost(3 * parts),
         name="grad_qkv",
-    )(me, x, dq, dk, dv, sums, up_sums, bias_sums)
-
-
-def grad_in(me, dq, dk, dv, res1, weight, fsdp):
+    )(me, *args)
+
+
+def columns(mine, other, core, widths):
+    zero = jnp.where(core == 0, mine, other)
+    one = jnp.where(core == 0, other, mine)
+    q, k, v = [], [], []
+    lo = 0
+    for n in widths:
+        q.append(zero[..., lo : lo + n])
+        k += [zero[..., lo + n : lo + 3 * n // 2], one[..., lo : lo + n // 2]]
+        v.append(one[..., lo + n // 2 : lo + 3 * n // 2])
+        lo += 3 * n // 2
+    return jnp.concatenate(q + k + v, -1)
+
+
+def grad_in(me, dqs, dks, dvs, res1, weight, fsdp):
     _, refs = weight
     n = 3 * D
     count = copy_count(weight)
-
-    def kernel(me_ref, q_ref, k_ref, v_ref, r_ref, *rest):
+    grads = [*dqs, *dks, *dvs]
+    width = dqs[0].shape[1]
+
+    def kernel(me_ref, *rest):
+        g_refs, r_ref, rest = rest[: len(grads)], rest[len(grads)], rest[len(grads) + 1 :]
         w_refs, o_refs, (w_ref, sems) = rest[: len(refs)], rest[len(refs) : -2], rest[-2:]
 
         @pl.when(pl.program_id(0) == 0)
@@ -650,26 +716,30 @@
             start_all(copies)
             wait_all(copies)
 
-        total = r_ref[...] + nt(q_ref[...], w_ref[:, :D])
-        total = total + nt(k_ref[...], w_ref[:, D : 2 * D])
-        total = total + nt(v_ref[...], w_ref[:, 2 * D :])
+        total = r_ref[...]
+        for i, g in enumerate(g_refs):
+            total = total + nt(g[...], w_ref[:, i * width : (i + 1) * width])
         put_block(o_refs, pl.program_id(0), total.astype(BF))
 
-    rows = dq.shape[0]
+    rows = res1.shape[0]
     blocks = rows // ROWS
-    blk = pl.BlockSpec((ROWS, D), lambda i, me: (i, 0))
+    blk = lambda c: pl.BlockSpec((ROWS, c), lambda i, me: (i, 0))
     return pl.pallas_call(
         kernel,
         grid_spec=pltpu.PrefetchScalarGridSpec(
-            num_scalar_prefetch=1, grid=(rows // ROWS,),
-            in_specs=[blk] * 4 + [ANY] * len(refs),
+            num_scalar_prefetch=1, grid=(blocks,),
+            in_specs=[blk(width)] * len(grads) + [blk(D)] + [ANY] * len(refs),
             out_specs=[pl.BlockSpec((ROWS, D), lambda i, me: (0, 0))] * blocks,
             scratch_shapes=[pltpu.VMEM((D, n), BF), pltpu.SemaphoreType.DMA((count,))]),
         out_shape=[jax.ShapeDtypeStruct((ROWS, D), BF)] * blocks,
         compiler_params=params(),
         cost_estimate=cost(9),
         name="grad_in",
-    )(me, dq, dk, dv, res1, *refs)
+    )(me, *grads, res1, *refs)
+
+
+def added(*parts):
+    return sum(v.astype(F32) for v in parts).astype(BF)
 
 
 def local(hidden_in, doc_starts, w_qkv, query_bias, value_bias, w_out, out_bias, norm1_gain,
@@ -695,11 +765,6 @@
     def across(v):
         return away(v, 1)
 
-    lines = [[2 * z + b for z in range(zs)] for b in range(2)]
-
-    def along(v):
-        return lax.all_to_all(v, "fsdp", 0, 0, axis_index_groups=lines, tiled=True)
-
     def swap(parts):
         two, three, one = [partner(parts[r - 1], r) for r in (2, 3, 1)]
         return [one, two, three]
@@ -708,21 +773,15 @@
         return swap(deal(me1, v))
 
     def deliver(parts):
-        return place(me1, [parts[0]] + swap(parts[1:]))
-
-    def each(v):
-        return jnp.broadcast_to(v[None], (zs,) + v.shape)
+        parts = [parts[0]] + swap(parts[1:])
+        return place(me1, parts)
 
     def half_cols(w):
         return lax.dynamic_slice(w, (0, core * (w.shape[1] // 2)), (w.shape[0], w.shape[1] // 2))
 
-    def spread(v):
-        a = along(each(v))
-        b = across(a)
-        return a, b, partner(a, 1), partner(b, 1)
-
-    def spread_apart(v):
-        line = [v] + [away(v, 2 * z) for z in range(1, zs)]
+    def spread(v, groups):
+        near = [v] + [away(v, 2 * z) for z in range(1, zs)]
+        line = [near[g[0]] if len(g) == 1 else jnp.stack([near[z] for z in g]) for g in groups]
         line += [across(a) for a in line]
         return line + [partner(a, 1) for a in line]
 
@@ -730,11 +789,11 @@
              value_bias, up_bias]
     x_near = fetch(hidden_in)
     if split:
-        weight1 = ("cols", spread_apart(pack(me1, w_qkv, small)))
+        weight1 = ("cols", spread(pack(me1, w_qkv, small), W1_GROUPS))
         table = None
-        weight2 = ("cols", spread(jnp.concatenate([half_cols(w_out), half_cols(w_up)], 1)))
+        weight2 = ("cols", spread(jnp.concatenate([half_cols(w_out), half_cols(w_up)], 1), W2_GROUPS))
         down = lax.dynamic_slice(w_down, (core * (rows_f // 2), 0), (rows_f // 2, D))
-        weight3 = ("rows", spread(down))
+        weight3 = ("rows", spread(down, W3_GROUPS))
     else:
         every = lax.all_gather(jnp.concatenate(small), "fsdp", axis=0).astype(F32)
         table = every[:, : 8 * rows_d].reshape(fsdp, 8, rows_d).transpose(1, 0, 2).reshape(8, D)
@@ -762,31 +821,26 @@
         me1, context, x, cotangent, g_near, table, full_up_bias, weight2, weight3, fsdp)
     layer_out = deliver(out)
 
-    def add(a, b):
-        return (a.astype(F32) + b.astype(F32)).astype(BF)
-
     def join(mine, other, axis, bit=core):
         return jnp.where(bit == 0, jnp.concatenate([mine, other], axis),
                          jnp.concatenate([other, mine], axis))
 
-    def pick(v, bit):
-        return lax.dynamic_index_in_dim(v, bit, 1, False)
-
-    def over_rows(v):
-        v = v.reshape((zs, 2) + v.shape[1:])
-        v = add(pick(v, xb), across(pick(v, 1 - xb)))
-        return jnp.sum(along(v).astype(F32), 0).astype(BF)
+    def finish(parts):
+        near = [parts[0]] + [away(v, 2 * z) for z, v in enumerate(parts) if z]
+        return added(*near)
 
     def reduce_part(send, keep):
-        total = over_rows(add(keep, partner(send, 1)))
-        total = add(total, partner(total, 2))
+        other = partner(send, 1)
+        got = across(added(keep[1], other[1]))
+        total = finish([added(keep[0, z], other[0, z], got[z]) for z in range(zs)])
+        total = added(total, partner(total, 2))
         return total, partner(total, 1)
 
     def reduce_by_high(send, keep):
-        v = add(keep, partner(send, 1))
-        v = v.reshape(fsdp, 2, v.shape[1] // 2, v.shape[2])
-        v = add(pick(v, high), partner(pick(v, 1 - high), 2))
-        total = over_rows(v)
+        other = partner(send, 1)
+        got = partner(added(keep[1], other[1]), 2)
+        far = across(added(keep[0, 1], other[0, 1], got[1]))
+        total = finish([added(keep[0, 0, z], other[0, 0, z], got[0, z], far[z]) for z in range(zs)])
         total = join(total, partner(total, 2), 0, high)
         return total, partner(total, 1)
 
@@ -794,19 +848,24 @@
         part = lax.psum_scatter(v, "fsdp", scatter_dimension=0, tiled=True)
         return lax.psum(part, "sp").astype(F32)
 
-    down_parts = grad_down(me1, act, gffn, fsdp)
-    wide_parts = grad_up_out(me1, low1, gpre, context, gattn)
+    down_parts = grad_down(me1, act, gffn, fsdp, split)
+    wide_parts = grad_up_out(me1, low1, gpre, context, gattn, fsdp, split)
     if split:
-        down = reduce_part(*down_parts)
-        wide = reduce_by_high(*[v.reshape(fsdp, rows_d, -1) for v in wide_parts])
-    grads = ()
+        down = reduce_part(*[v.reshape((2, zs) + v.shape[1:]) for v in down_parts])
+        wide = reduce_by_high(*wide_parts)
+    dqs, dks, dvs, bias_sums = [], [], [], []
+    widths, groups, halves = [], [], []
     for i in range(PARTS):
-        grads = attend_back(qkv, context, gctx, lse, seg_col, seg_row, i * per, per, grads)
-    dq, dk, dv, bias_sums = grads
-    qkv_parts = grad_qkv(me1, x, dq, dk, dv, sums, up_sums, bias_sums, fsdp)
-    if split:
-        qkv_sum = reduce_part(*qkv_parts)
-    dx = grad_in(me1, dq, dk, dv, res1, weight1, fsdp)
+        dq, dk, dv, b = attend_back(qkv, context, gctx, lse, seg_col, seg_row, i * per, per)
+        dqs, dks, dvs, bias_sums = dqs + [dq], dks + [dk], dvs + [dv], bias_sums + [b]
+        if i in GROUP_ENDS:
+            at = slice(sum(widths) // dq.shape[1], i + 1)
+            widths.append((i + 1 - at.start) * dq.shape[1])
+            extra = (sums, up_sums, *bias_sums) if i == PARTS - 1 else None
+            halves.append(grad_qkv(me1, x, dqs[at], dks[at], dvs[at], extra, fsdp, split))
+            if split:
+                groups.append(reduce_part(*halves[-1]))
+    dx = grad_in(me1, dqs, dks, dvs, res1, weight1, fsdp)
     grad_input = deliver(dx)
 
     if split:
@@ -815,8 +874,9 @@
         w1 = D // 2
         grad_out = both([v[:, :w1] for v in wide], 1)
         grad_up = both([v[:, w1:] for v in wide], 1)
-        grad_q = both([v[:rows_d] for v in qkv_sum], 1)
-        tail = qkv_sum[0][rows_d:].astype(F32)
+        beside = [jnp.concatenate([v[i][:rows_d] for v in groups], -1) for i in range(2)]
+        grad_q = columns(*beside, core, widths).astype(F32)
+        tail = groups[-1][0][rows_d:].astype(F32)
         g2, b2, db, g1, b1, ob, qb, vb = [tail[i, :rows_d] for i in range(8)]
         ub = tail[8, :rows_f]
     else:
@@ -825,8 +885,9 @@
         w1, w2 = D // 2, FF // 2
         grad_out = jnp.concatenate([wide[:, :w1], wide[:, w1 + w2 : 2 * w1 + w2]], 1)
         grad_up = jnp.concatenate([wide[:, w1 : w1 + w2], wide[:, 2 * w1 + w2 :]], 1)
-        grad_q = scatter(join(*[v[:, :rows_d] for v in qkv_parts[::-1]], 2).reshape(D, 3 * D).astype(F32))
-        by_dest = jnp.concatenate([sums[:6], bias_sums[:2]], 0).reshape(8, fsdp, rows_d)
+        sent, kept = [jnp.concatenate([h[i][:, :rows_d] for h in halves], -1) for i in range(2)]
+        grad_q = scatter(columns(kept, sent, core, widths).reshape(D, 3 * D).astype(F32))
+        by_dest = jnp.concatenate([sums[:6], jnp.concatenate([b[:2] for b in bias_sums], 1)], 0).reshape(8, fsdp, rows_d)
         by_dest = by_dest.transpose(1, 0, 2).reshape(fsdp, 8 * rows_d)
         extra = jnp.concatenate([by_dest, up_sums[0].reshape(fsdp, rows_f)], 1)
         tail = scatter(extra).reshape(-1)
@@ -837,6 +898,11 @@
 
 
 PARTS = 3
+GROUP_ENDS = (1, 2)
+
+W1_GROUPS = ((0,), (1,), (2,), (3,))
+W2_GROUPS = ((0,), (1,), (2, 3))
+W3_GROUPS = ((0,), (1, 2, 3))
 
 
 def in_pieces(fsdp):

time: 490 us -> 501 us (1.022)
  waiting for transfers between devices: 178 us -> 196 us
  starting transfers between devices: 56.2 us -> 68.5 us
  other arithmetic: 24.7 us -> 12.7 us
  local copies, waits for them, and re-layouts: 14.8 us -> 7.15 us
    all_to_all x5 -> x0, waiting for transfers between devices: 41.4 us -> none  [along(): return lax.all_to_all(v, 'fsdp', 0, 0, axis_index_groups=lines, tiled=True)]
    ppermute x12 -> x34, waiting for transfers between devices: 116 us -> 152 us  [away(): return lax.ppermute(v, 'fsdp', [(i, i ^ bits) for i in range(fsdp)])]
    ppermute x12 -> x34, starting transfers between devices: 16.2 us -> 50.5 us  [away(): return lax.ppermute(v, 'fsdp', [(i, i ^ bits) for i in range(fsdp)])]
    all_to_all x5 -> x0, starting transfers between devices: 24.1 us -> none  [along(): return lax.all_to_all(v, 'fsdp', 0, 0, axis_index_groups=lines, tiled=True)]
    ppermute x34 -> x43, waiting for transfers between devices: 20.6 us -> 44.3 us  [partner(): return lax.ppermute(v, 'sp', [(i, i ^ bit) for i in range(sp)])]
    convert_element_type x10 -> x18, other arithmetic: 16.8 us -> 8.61 us  [the longest x16 7.64 us: added(): return sum((v.astype(F32) for v in parts)).astype(BF)]
    pallas_call x1 -> x2, Pallas kernels: 9.78 us -> 12.9 us  [grad_qkv(): pl.pallas_call(kernel, grid_spec=pltpu.PrefetchScalarGridSpec(num_scalar_...]
    ppermute x34 -> x43, starting transfers between devices: 15.8 us -> 18 us  [partner(): return lax.ppermute(v, 'sp', [(i, i ^ bit) for i in range(sp)])]
  transfers between devices with their start and end apart: 51 -> 77, of which waited for: 17 -> 21; matrix products, arithmetic and copies ran while one was open for 6% -> 3% of each run, Pallas kernels for 30% -> 23%
where the time goes in v3:
time: 501 us; the launch traced here: 497 us
  Pallas kernels  211 us (42%)
  waiting for transfers between devices  196 us (39%)
  starting transfers between devices  68.5 us (14%)
  other arithmetic  12.7 us (3%)
  local copies, waits for them, and re-layouts  7.15 us (1%)
    ppermute x34, waiting for transfers between devices, away(): return lax.ppermute(v, 'fsdp', [(i, i ^ bits) for i in range(fsdp)])  152 us
    ppermute x34, starting transfers between devices, away(): return lax.ppermute(v, 'fsdp', [(i, i ^ bits) for i in range(fsdp)])  50.5 us
    pallas_call x1, Pallas kernels, middle(): pl.pallas_call(kernel, grid_spec=pltpu.PrefetchScalarGridSpec(num_scalar_...  49.1 us
    pallas_call x3, Pallas kernels, attend_back(): pl.pallas_call(kernel, grid=(count,), in_specs=[spec(0), spec(PAIRS), spe...  44.4 us
    ppermute x43, waiting for transfers between devices, partner(): return lax.ppermute(v, 'sp', [(i, i ^ bit) for i in range(sp)])  44.3 us
    pallas_call x3, Pallas kernels, attend(): pl.pallas_call(kernel, grid=(count,), in_specs=[spec(0), spec(PAIRS), spe...  41.3 us
    ppermute x43, starting transfers between devices, partner(): return lax.ppermute(v, 'sp', [(i, i ^ bit) for i in range(sp)])  18 us
    pallas_call x2, Pallas kernels, grad_qkv(): pl.pallas_call(kernel, grid_spec=pltpu.PrefetchScalarGridSpec(num_scalar_...  12.9 us
  transfers between devices with their start and end apart: 77, of which 21 were waited for; matrix products, arithmetic and copies ran while one was open for 3% of the time, Pallas kernels for 23%

profile of v3, /device:TPU:0, one launch (start us, length us, event | category | flops | bytes accessed | tf_op | source)
XLA Modules:
  0.0 496.9 jit_solution(14644564060096288696)
XLA Ops:
  1.3 2.6 pack.1.rest_4_.rest_10_
  4.3 2.5 collective-permute-start.6
  6.8 3.6 collective-permute-start.5
  11.3 3.7 collective-permute-start.35
  15.0 2.9 deal.2
  18.6 10.5 %collective-permute-start.33 = (bf16[192,768]{1,0:T(8,128)(2,1)S(1)}, bf16[192,768]{1,0:T(8,128)(2,1)S(1)}, u32[]{:S(2)}, u32[]{:S(2)}) collective-permute-start(bf16[192,768]{1,0:T(8,128)(2,1)S(1)} %constant_dynamic-slice_fusion.rest_16_), channel_id=1, source_target_pairs={{0,8},{4,12},{8,0},{12,4},{16,24},{20,28},{24,16},{28,20},{1,9},{5... | collective-permute-start | bytes 884744 | tf_op jit(solution)/shard_map/ppermute | solution.py:763
  29.2 17.2 %collective-permute-done.4.rest_6_.rest_12_ = bf16[112,1152]{1,0:T(8,128)(2,1)S(1)} collective-permute-done((bf16[112,1152]{1,0:T(8,128)(2,1)}, bf16[112,1152]{1,0:T(8,128)(2,1)S(1)}, u32[]{:S(2)}, u32[]{:S(2)}) %collective-permute-start.4) | collective-permute-done | bytes 258080 | tf_op jit(solution)/shard_map/ppermute | solution.py:763
  49.0 9.3 %collective-permute-done.34 = bf16[192,768]{1,0:T(8,128)(2,1)S(1)} collective-permute-done((bf16[192,768]{1,0:T(8,128)(2,1)S(1)}, bf16[192,768]{1,0:T(8,128)(2,1)S(1)}, u32[]{:S(2)}, u32[]{:S(2)}) %collective-permute-start.34) | collective-permute-done | bytes 294944 | tf_op jit(solution)/shard_map/ppermute | solution.py:763
  58.2 2.6 collective-permute-start.23
  61.6 10.0 %collective-permute-done.23 = bf16[96,1920]{1,0:T(8,128)(2,1)S(1)} collective-permute-done((bf16[96,1920]{1,0:T(8,128)(2,1)S(1)}, bf16[96,1920]{1,0:T(8,128)(2,1)S(1)}, u32[]{:S(2)}, u32[]{:S(2)}) %collective-permute-start.23) | collective-permute-done | bytes 368672 | tf_op jit(solution)/shard_map/ppermute | solution.py:763
  71.6 19.4 %collective-permute-done.22 = bf16[96,1920]{1,0:T(8,128)(2,1)S(1)} collective-permute-done((bf16[96,1920]{1,0:T(8,128)(2,1)S(1)}, bf16[96,1920]{1,0:T(8,128)(2,1)S(1)}, u32[]{:S(2)}, u32[]{:S(2)}) %collective-permute-start.22) | collective-permute-done | bytes 368672 | tf_op jit(solution)/shard_map/ppermute | solution.py:763
  94.8 3.1 deal.3
  98.5 1.8 collective-permute-done.9.rest_11_.rest_17_
  100.3 5.5 %collective-permute-done.8.rest_10_.rest_16_ = bf16[112,1152]{1,0:T(8,128)(2,1)} collective-permute-done((bf16[112,1152]{1,0:T(8,128)(2,1)}, bf16[112,1152]{1,0:T(8,128)(2,1)}, u32[]{:S(2)}, u32[]{:S(2)}) %collective-permute-start.8) | collective-permute-done | bytes 258080 | tf_op jit(solution)/shard_map/ppermute | solution.py:763
  105.9 3.0 collective-permute-done.7.rest_9_.rest_15_
  111.9 10.3 %project.1 = (bf16[1024,2304]{1,0:T(8,128)(2,1)}, bf16[1024,768]{1,0:T(8,128)(2,1)}, f32[8,768]{1,0:T(8,128)}, f32[8,3072]{1,0:T(8,128)}) custom-call(s32[3]{0:T(128)} %pad_add_fusion.me_ref, bf16[4,256,768]{2,1,0:T(8,128)(2,1)} %rest_0_.4, bf16[256,768]{1,0:T(8,128)(2,1)} %copy-done.20, bf16[256,768]{1,0:T(8,128)(2,1)} %copy-done.21, ...), custom_call_target="tpu_custom_call" | custom-call | flops 8999999488 | bytes 1048576 | tf_op jit(solution)/shard_map/project/pallas_call | solution.py:280
  126.6 13.7 %attend.3 = (bf16[1024,768]{1,0:T(8,128)(2,1)}, f32[6,8,1024]{2,1,0:T(8,128)}) custom-call(bf16[1024,2304]{1,0:T(8,128)(2,1)} %get-tuple-element.71.q_ref.k_ref.v_ref, bf16[1024,2304]{1,0:T(8,128)(2,1)} %get-tuple-element.71.q_ref.k_ref.v_ref, bf16[1024,2304]{1,0:T(8,128)(2,1)} %get-tuple-element.71.q_ref.k_ref.v_ref, s32[1024,1]{1,0:T(8,128)} %copy.43.sc_ref, ...), custom_call_target="tpu_custom_call" | custom-call | flops 12000000000 | bytes 1048576 | tf_op jit(solution)/shard_map/attend/pallas_call | solution.py:327
  143.2 14.0 %attend.4 = (bf16[1024,768]{1,0:T(8,128)(2,1)}, f32[6,8,1024]{2,1,0:T(8,128)}) custom-call(bf16[1024,2304]{1,0:T(8,128)(2,1)} %get-tuple-element.71.q_ref.k_ref.v_ref, bf16[1024,2304]{1,0:T(8,128)(2,1)} %get-tuple-element.71.q_ref.k_ref.v_ref, bf16[1024,2304]{1,0:T(8,128)(2,1)} %get-tuple-element.71.q_ref.k_ref.v_ref, ...), custom_call_target="tpu_custom_call", output_to_operand_aliasing={{0}: (5, {}), {1}: (6, {})} | custom-call | flops 12000000000 | bytes 1048576 | tf_op jit(solution)/shard_map/attend/pallas_call | solution.py:327
  157.8 28.2 %collective-permute-done.25.rest_8_ = bf16[96,1920]{1,0:T(8,128)(2,1)} collective-permute-done((bf16[96,1920]{1,0:T(8,128)(2,1)}, bf16[96,1920]{1,0:T(8,128)(2,1)}, u32[]{:S(2)}, u32[]{:S(2)}) %collective-permute-start.25) | collective-permute-done | bytes 368672 | tf_op jit(solution)/shard_map/ppermute | solution.py:763
  186.7 13.7 %attend.5 = (bf16[1024,768]{1,0:T(8,128)(2,1)}, f32[6,8,1024]{2,1,0:T(8,128)}) custom-call(bf16[1024,2304]{1,0:T(8,128)(2,1)} %get-tuple-element.71.q_ref.k_ref.v_ref, bf16[1024,2304]{1,0:T(8,128)(2,1)} %get-tuple-element.71.q_ref.k_ref.v_ref, bf16[1024,2304]{1,0:T(8,128)(2,1)} %get-tuple-element.71.q_ref.k_ref.v_ref, ...), custom_call_target="tpu_custom_call", output_to_operand_aliasing={{0}: (5, {}), {1}: (6, {})} | custom-call | flops 12000000000 | bytes 1048576 | tf_op jit(solution)/shard_map/attend/pallas_call | solution.py:327
  201.9 49.1 %middle.1 = (bf16[256,768]{1,0:T(8,128)(2,1)}, bf16[256,768]{1,0:T(8,128)(2,1)}, bf16[256,768]{1,0:T(8,128)(2,1)}, bf16[256,768]{1,0:T(8,128)(2,1)}, bf16[1024,3...) custom-call(s32[3]{0:T(128)} %pad_add_fusion.me_ref, ...), custom_call_target="tpu_custom_call" | custom-call | flops 48000000000 | bytes 1048576 | tf_op jit(solution)/shard_map/middle/pallas_call | solution.py:488
  251.0 14.8 %attend_back.5 = (bf16[1024,256]{1,0:T(8,128)(2,1)}, bf16[1024,256]{1,0:T(8,128)(2,1)}, bf16[1024,256]{1,0:T(8,128)(2,1)}, f32[8,256]{1,0:T(8,128)}) custom-call(bf16[1024,2304]{1,0:T(8,128)(2,1)} %get-tuple-element.71.q_ref.k_ref.v_ref, bf16[1024,2304]{1,0:T(8,128)(2,1)} %get-tuple-element.71.q_ref.k_ref.v_ref, ...), custom_call_target="tpu_custom_call" | custom-call | flops 12000000000 | bytes 1048576 | tf_op jit(solution)/shard_map/attend_back/pallas_call | solution.py:388
  265.9 14.7 %attend_back.4 = (bf16[1024,256]{1,0:T(8,128)(2,1)}, bf16[1024,256]{1,0:T(8,128)(2,1)}, bf16[1024,256]{1,0:T(8,128)(2,1)}, f32[8,256]{1,0:T(8,128)}) custom-call(bf16[1024,2304]{1,0:T(8,128)(2,1)} %get-tuple-element.71.q_ref.k_ref.v_ref, bf16[1024,2304]{1,0:T(8,128)(2,1)} %get-tuple-element.71.q_ref.k_ref.v_ref, ...), custom_call_target="tpu_custom_call" | custom-call | flops 12000000000 | bytes 1048576 | tf_op jit(solution)/shard_map/attend_back/pallas_call | solution.py:388
  280.6 14.9 %attend_back.3 = (bf16[1024,256]{1,0:T(8,128)(2,1)}, bf16[1024,256]{1,0:T(8,128)(2,1)}, bf16[1024,256]{1,0:T(8,128)(2,1)}, f32[8,256]{1,0:T(8,128)}) custom-call(bf16[1024,2304]{1,0:T(8,128)(2,1)} %get-tuple-element.71.q_ref.k_ref.v_ref, bf16[1024,2304]{1,0:T(8,128)(2,1)} %get-tuple-element.71.q_ref.k_ref.v_ref, ...), custom_call_target="tpu_custom_call" | custom-call | flops 12000000000 | bytes 1048576 | tf_op jit(solution)/shard_map/attend_back/pallas_call | solution.py:388
  297.4 5.8 %grad_qkv.3 = (bf16[2,4,112,384]{3,2,1,0:T(8,128)(2,1)}, bf16[2,4,112,384]{3,2,1,0:T(8,128)(2,1)}) custom-call(s32[3]{0:T(128)} %pad_add_fusion.me_ref, bf16[1024,768]{1,0:T(8,128)(2,1)} %get-tuple-element.77.x_ref, bf16[1024,256]{1,0:T(8,128)(2,1)} %get-tuple-element.91.rest_2_.rest_0_, bf16[1024,256]{1,0:T(8,128)(2,1)} %get-tuple-element.94.rest_5_.rest_1_, ...), custom_call_target="tpu_custom_call" | custom-call | flops 3000000000 | bytes 1048576 | tf_op jit(solution)/shard_map/grad_qkv/pallas_call | solution.py:674
  303.8 7.1 %grad_qkv.2 = (bf16[2,4,96,768]{3,2,1,0:T(8,128)(2,1)}, bf16[2,4,96,768]{3,2,1,0:T(8,128)(2,1)}) custom-call(s32[3]{0:T(128)} %pad_add_fusion.me_ref, bf16[1024,768]{1,0:T(8,128)(2,1)} %get-tuple-element.77.x_ref, bf16[1024,256]{1,0:T(8,128)(2,1)} %get-tuple-element.89.rest_0_, bf16[1024,256]{1,0:T(8,128)(2,1)} %get-tuple-element.90.rest_1_, ...), custom_call_target="tpu_custom_call" | custom-call | flops 6000000000 | bytes 1048576 | tf_op jit(solution)/shard_map/grad_qkv/pallas_call | solution.py:674
  311.0 12.9 %grad_down.1 = (bf16[8,192,768]{2,1,0:T(8,128)(2,1)}, bf16[8,192,768]{2,1,0:T(8,128)(2,1)}) custom-call(s32[3]{0:T(128)} %pad_add_fusion.me_ref, bf16[1024,3072]{1,0:T(8,128)(2,1)} %get-tuple-element.117.a_ref, bf16[1024,768]{1,0:T(8,128)(2,1)} %get-tuple-element.118.g_ref), custom_call_target="tpu_custom_call" | custom-call | flops 12000000000 | bytes 1048576 | tf_op jit(solution)/shard_map/grad_down/pallas_call | solution.py:543
  324.7 12.5 %grad_up_out.1 = (bf16[2,2,4,48,1920]{4,3,2,1,0:T(8,128)(2,1)}, bf16[2,2,4,48,1920]{4,3,2,1,0:T(8,128)(2,1)}) custom-call(s32[3]{0:T(128)} %pad_add_fusion.me_ref, bf16[1024,768]{1,0:T(8,128)(2,1)} %get-tuple-element.112.l_ref, bf16[1024,3072]{1,0:T(8,128)(2,1)} %get-tuple-element.113.p_ref, bf16[1024,768]{1,0:T(8,128)(2,1)} %get-tuple-element.76.c_ref.o_ref, ...), custom_call_target="tpu_custom_call" | custom-call | flops 12000000000 | bytes 1048576 | tf_op jit(solution)/shard_map/grad_up_out/pallas_call | solution.py:603
  337.5 10.8 %grad_in.1 = (bf16[256,768]{1,0:T(8,128)(2,1)}, bf16[256,768]{1,0:T(8,128)(2,1)}, bf16[256,768]{1,0:T(8,128)(2,1)}, bf16[256,768]{1,0:T(8,128)(2,1)}) custom-call(s32[3]{0:T(128)} %pad_add_fusion.me_ref, bf16[1024,256]{1,0:T(8,128)(2,1)} %get-tuple-element.89.rest_0_, bf16[1024,256]{1,0:T(8,128)(2,1)} %get-tuple-element.90.rest_1_, ...), custom_call_target="tpu_custom_call" | custom-call | flops 8999999488 | bytes 1048576 | tf_op jit(solution)/shard_map/grad_in/pallas_call | solution.py:727
  351.9 3.9 place.2
  359.4 6.0 %collective-permute-done.57 = bf16[112,384]{1,0:T(8,128)(2,1)S(1)} collective-permute-done((bf16[112,384]{1,0:T(8,128)(2,1)S(1)}, bf16[112,384]{1,0:T(8,128)(2,1)S(1)}, u32[]{:S(2)}, u32[]{:S(2)}) %collective-permute-start.57) | collective-permute-done | bytes 86048 | tf_op jit(solution)/shard_map/ppermute | solution.py:763
  369.6 5.5 %collective-permute-done.47.refs_3_ = bf16[256,768]{1,0:T(8,128)(2,1)} collective-permute-done((bf16[256,768]{1,0:T(8,128)(2,1)}, bf16[256,768]{1,0:T(8,128)(2,1)}, u32[]{:S(2)}, u32[]{:S(2)}) %collective-permute-start.47) | collective-permute-done | bytes 393248 | tf_op jit(solution)/shard_map/ppermute | solution.py:760
  375.1 3.7 place.3
  378.9 2.1 collective-permute-done.49
  382.4 1.7 collective-permute-start.52
  384.2 1.7 collective-permute-start.51
  385.9 3.9 collective-permute-done.50
  389.8 2.3 collective-permute-done.52
  392.1 6.2 %collective-permute-done.51 = bf16[96,768]{1,0:T(8,128)(2,1)S(1)} collective-permute-done((bf16[96,768]{1,0:T(8,128)(2,1)S(1)}, bf16[96,768]{1,0:T(8,128)(2,1)S(1)}, u32[]{:S(2)}, u32[]{:S(2)}) %collective-permute-start.51) | collective-permute-done | bytes 147488 | tf_op jit(solution)/shard_map/ppermute | solution.py:763
  401.1 3.5 collective-permute-done.53
  409.0 30.9 %collective-permute-done.63 = bf16[2,4,48,1920]{3,2,1,0:T(8,128)(2,1)S(1)} collective-permute-done((bf16[2,4,48,1920]{3,2,1,0:T(8,128)(2,1)S(1)}, bf16[2,4,48,1920]{3,2,1,0:T(8,128)(2,1)S(1)}, u32[]{:S(2)}, u32[]{:S(2)}) %collective-permute-start.63) | collective-permute-done | bytes 1474592 | tf_op jit(solution)/shard_map/ppermute | solution.py:760
  442.2 2.0 collective-permute-start.74
  445.7 12.6 %collective-permute-done.64 = bf16[4,48,1920]{2,1,0:T(8,128)(2,1)S(1)} collective-permute-done((bf16[4,48,1920]{2,1,0:T(8,128)(2,1)S(1)}, bf16[4,48,1920]{2,1,0:T(8,128)(2,1)S(1)}, u32[]{:S(2)}, u32[]{:S(2)}) %collective-permute-start.64) | collective-permute-done | bytes 737312 | tf_op jit(solution)/shard_map/ppermute | solution.py:763
  458.6 1.8 collective-permute-start.67
  460.5 1.6 collective-permute-start.66
  462.1 18.2 %collective-permute-done.73 = bf16[192,768]{1,0:T(8,128)(2,1)S(1)} collective-permute-done((bf16[192,768]{1,0:T(8,128)(2,1)S(1)}, bf16[192,768]{1,0:T(8,128)(2,1)S(1)}, u32[]{:S(2)}, u32[]{:S(2)}) %collective-permute-start.73) | collective-permute-done | bytes 294944 | tf_op jit(solution)/shard_map/ppermute | solution.py:763
  481.8 4.5 collective-permute-done.66
  487.9 4.2 collective-permute-done.68
  (264 shorter events, 58.0 us)
Async XLA Ops:
  10.4 35.9 %collective-permute-start.4 = (bf16[112,1152]{1,0:T(8,128)(2,1)}, bf16[112,1152]{1,0:T(8,128)(2,1)S(1)}, u32[]{:S(2)}, u32[]{:S(2)}) collective-permute-start(bf16[112,1152]{1,0:T(8,128)(2,1)} %pack.1.rest_4_.rest_10_), channel_id=1, source_target_pairs={{0,16},{4,20},{8,24},{12,28},{16,0},{20,4},{24,8},{28,12},{1,17},{... | collective-permute-start | bytes 774152 | tf_op jit(solution)/shard_map/ppermute | solution.py:763
  10.4 35.9 %collective-permute-start.3 = (bf16[112,1152]{1,0:T(8,128)(2,1)}, bf16[112,1152]{1,0:T(8,128)(2,1)S(1)}, u32[]{:S(2)}, u32[]{:S(2)}) collective-permute-start(bf16[112,1152]{1,0:T(8,128)(2,1)} %pack.1.rest_4_.rest_10_), channel_id=1, source_target_pairs={{0,8},{4,12},{8,0},{12,4},{16,24},{20,28},{24,16},{28,20},{1,9},{5... | collective-permute-start | bytes 774152 | tf_op jit(solution)/shard_map/ppermute | solution.py:763
  11.3 37.3 %collective-permute-start.35 = (bf16[192,768]{1,0:T(8,128)(2,1)S(1)}, bf16[192,768]{1,0:T(8,128)(2,1)S(1)}, u32[]{:S(2)}, u32[]{:S(2)}) collective-permute-start(bf16[192,768]{1,0:T(8,128)(2,1)S(1)} %constant_dynamic-slice_fusion.rest_16_), channel_id=1, source_target_pairs={{0,24},{4,28},{8,16},{12,20},{16,8},{20,12},{24,0},{28,4},{1,25},{... | collective-permute-start | bytes 884744 | tf_op jit(solution)/shard_map/ppermute | solution.py:763
  17.9 40.3 %collective-permute-start.34 = (bf16[192,768]{1,0:T(8,128)(2,1)S(1)}, bf16[192,768]{1,0:T(8,128)(2,1)S(1)}, u32[]{:S(2)}, u32[]{:S(2)}) collective-permute-start(bf16[192,768]{1,0:T(8,128)(2,1)S(1)} %constant_dynamic-slice_fusion.rest_16_), channel_id=1, source_target_pairs={{0,16},{4,20},{8,24},{12,28},{16,0},{20,4},{24,8},{28,12},{1,17},{... | collective-permute-start | bytes 884744 | tf_op jit(solution)/shard_map/ppermute | solution.py:763
  18.6 42.3 %collective-permute-start.33 = (bf16[192,768]{1,0:T(8,128)(2,1)S(1)}, bf16[192,768]{1,0:T(8,128)(2,1)S(1)}, u32[]{:S(2)}, u32[]{:S(2)}) collective-permute-start(bf16[192,768]{1,0:T(8,128)(2,1)S(1)} %constant_dynamic-slice_fusion.rest_16_), channel_id=1, source_target_pairs={{0,8},{4,12},{8,0},{12,4},{16,24},{20,28},{24,16},{28,20},{1,9},{5... | collective-permute-start | bytes 884744 | tf_op jit(solution)/shard_map/ppermute | solution.py:763
  46.3 45.1 %collective-permute-start = (bf16[256,768]{1,0:T(8,128)(2,1)}, bf16[256,768]{1,0:T(8,128)(2,1)S(1)}, u32[]{:S(2)}, u32[]{:S(2)}) collective-permute-start(bf16[256,768]{1,0:T(8,128)(2,1)} %get-tuple-element.68), channel_id=1, source_target_pairs={{0,1},{1,0},{2,3},{3,2},{4,5},{5,4},{6,7},{7,6},{8,9},{9,8},{10,11... | collective-permute-start | bytes 1179656 | tf_op jit(solution)/shard_map/ppermute | solution.py:760
  47.1 44.4 %collective-permute-start.1 = (bf16[256,768]{1,0:T(8,128)(2,1)}, bf16[256,768]{1,0:T(8,128)(2,1)S(1)}, u32[]{:S(2)}, u32[]{:S(2)}) collective-permute-start(bf16[256,768]{1,0:T(8,128)(2,1)} %get-tuple-element.69), channel_id=1, source_target_pairs={{0,2},{1,3},{2,0},{3,1},{4,6},{5,7},{6,4},{7,5},{8,10},{9,11},{10,... | collective-permute-start | bytes 1179656 | tf_op jit(solution)/shard_map/ppermute | solution.py:760
  48.6 44.5 %collective-permute-start.2 = (bf16[256,768]{1,0:T(8,128)(2,1)}, bf16[256,768]{1,0:T(8,128)(2,1)S(1)}, u32[]{:S(2)}, u32[]{:S(2)}) collective-permute-start(bf16[256,768]{1,0:T(8,128)(2,1)} %get-tuple-element.70), channel_id=1, source_target_pairs={{0,3},{1,2},{2,1},{3,0},{4,7},{5,6},{6,5},{7,4},{8,11},{9,10},{10,... | collective-permute-start | bytes 1179656 | tf_op jit(solution)/shard_map/ppermute | solution.py:760
  60.9 30.1 %collective-permute-start.22 = (bf16[96,1920]{1,0:T(8,128)(2,1)S(1)}, bf16[96,1920]{1,0:T(8,128)(2,1)S(1)}, u32[]{:S(2)}, u32[]{:S(2)}) collective-permute-start(bf16[96,1920]{1,0:T(8,128)(2,1)S(1)} %pad_maximum_fusion.2.rest_4_), channel_id=1, source_target_pairs={{0,16},{4,20},{8,24},{12,28},{16,0},{20,4},{24,8},{28,12},{1,17},{... | collective-permute-start | bytes 1105928 | tf_op jit(solution)/shard_map/ppermute | solution.py:763
  71.5 26.4 %collective-permute-start.13 = (bf16[112,1152]{1,0:T(8,128)(2,1)}, bf16[112,1152]{1,0:T(8,128)(2,1)}, u32[]{:S(2)}, u32[]{:S(2)}) collective-permute-start(bf16[112,1152]{1,0:T(8,128)(2,1)} %copy-done.36), channel_id=1, source_target_pairs={{0,1},{1,0},{2,3},{3,2},{4,5},{5,4},{6,7},{7,6},{8,9},{9,8},{10,11... | collective-permute-start | bytes 774152 | tf_op jit(solution)/shard_map/ppermute | solution.py:760
  91.5 14.4 %collective-permute-start.8 = (bf16[112,1152]{1,0:T(8,128)(2,1)}, bf16[112,1152]{1,0:T(8,128)(2,1)}, u32[]{:S(2)}, u32[]{:S(2)}) collective-permute-start(bf16[112,1152]{1,0:T(8,128)(2,1)} %copy-done.37), channel_id=1, source_target_pairs={{0,4},{4,0},{8,12},{12,8},{16,20},{20,16},{24,28},{28,24},{1,5},{5... | collective-permute-start | bytes 774152 | tf_op jit(solution)/shard_map/ppermute | solution.py:763
  93.1 15.8 %collective-permute-start.7 = (bf16[112,1152]{1,0:T(8,128)(2,1)}, bf16[112,1152]{1,0:T(8,128)(2,1)}, u32[]{:S(2)}, u32[]{:S(2)}) collective-permute-start(bf16[112,1152]{1,0:T(8,128)(2,1)} %copy-done.39), channel_id=1, source_target_pairs={{0,4},{4,0},{8,12},{12,8},{16,20},{20,16},{24,28},{28,24},{1,5},{5... | collective-permute-start | bytes 774152 | tf_op jit(solution)/shard_map/ppermute | solution.py:763
  110.3 14.2 %collective-permute-start.27 = (bf16[96,1920]{1,0:T(8,128)(2,1)S(1)}, bf16[96,1920]{1,0:T(8,128)(2,1)S(1)}, u32[]{:S(2)}, u32[]{:S(2)}) collective-permute-start(bf16[96,1920]{1,0:T(8,128)(2,1)S(1)} %pad_maximum_fusion.2.rest_4_), channel_id=1, source_target_pairs={{0,1},{1,0},{2,3},{3,2},{4,5},{5,4},{6,7},{7,6},{8,9},{9,8},{10,11... | collective-permute-start | bytes 1105928 | tf_op jit(solution)/shard_map/ppermute | solution.py:760
  110.3 16.3 %collective-permute-start.24 = (bf16[96,1920]{1,0:T(8,128)(2,1)S(1)}, bf16[96,1920]{1,0:T(8,128)(2,1)S(1)}, u32[]{:S(2)}, u32[]{:S(2)}) collective-permute-start(bf16[96,1920]{1,0:T(8,128)(2,1)S(1)} %pad_maximum_fusion.2.rest_4_), channel_id=1, source_target_pairs={{0,4},{4,0},{8,12},{12,8},{16,20},{20,16},{24,28},{28,24},{1,5},{5... | collective-permute-start | bytes 1105928 | tf_op jit(solution)/shard_map/ppermute | solution.py:763
  111.9 28.4 %collective-permute-start.21 = (bf16[96,1920]{1,0:T(8,128)(2,1)S(1)}, bf16[96,1920]{1,0:T(8,128)(2,1)}, u32[]{:S(2)}, u32[]{:S(2)}) collective-permute-start(bf16[96,1920]{1,0:T(8,128)(2,1)S(1)} %pad_maximum_fusion.2.rest_4_), channel_id=1, source_target_pairs={{0,8},{4,12},{8,0},{12,4},{16,24},{20,28},{24,16},{28,20},{1,9},{5... | collective-permute-start | bytes 1105928 | tf_op jit(solution)/shard_map/ppermute | solution.py:763
  122.3 18.6 %collective-permute-start.18 = (bf16[256,768]{1,0:T(8,128)(2,1)S(1)}, bf16[256,768]{1,0:T(8,128)(2,1)S(1)}, u32[]{:S(2)}, u32[]{:S(2)}) collective-permute-start(bf16[256,768]{1,0:T(8,128)(2,1)S(1)} %copy-done.28), channel_id=1, source_target_pairs={{0,1},{1,0},{2,3},{3,2},{4,5},{5,4},{6,7},{7,6},{8,9},{9,8},{10,11... | collective-permute-start | bytes 1179656 | tf_op jit(solution)/shard_map/ppermute | solution.py:760
  123.0 19.4 %collective-permute-start.19 = (bf16[256,768]{1,0:T(8,128)(2,1)S(1)}, bf16[256,768]{1,0:T(8,128)(2,1)S(1)}, u32[]{:S(2)}, u32[]{:S(2)}) collective-permute-start(bf16[256,768]{1,0:T(8,128)(2,1)S(1)} %copy-done.27), channel_id=1, source_target_pairs={{0,2},{1,3},{2,0},{3,1},{4,6},{5,7},{6,4},{7,5},{8,10},{9,11},{10,... | collective-permute-start | bytes 1179656 | tf_op jit(solution)/shard_map/ppermute | solution.py:760
  125.2 17.2 %collective-permute-start.20 = (bf16[256,768]{1,0:T(8,128)(2,1)S(1)}, bf16[256,768]{1,0:T(8,128)(2,1)S(1)}, u32[]{:S(2)}, u32[]{:S(2)}) collective-permute-start(bf16[256,768]{1,0:T(8,128)(2,1)S(1)} %copy-done.25), channel_id=1, source_target_pairs={{0,3},{1,2},{2,1},{3,0},{4,7},{5,6},{6,5},{7,4},{8,11},{9,10},{10,... | collective-permute-start | bytes 1179656 | tf_op jit(solution)/shard_map/ppermute | solution.py:760
  126.6 16.4 %collective-permute-start.40 = (bf16[192,768]{1,0:T(8,128)(2,1)}, bf16[192,768]{1,0:T(8,128)(2,1)}, u32[]{:S(2)}, u32[]{:S(2)}) collective-permute-start(bf16[192,768]{1,0:T(8,128)(2,1)} %collective-permute-done.36.rest_18_), channel_id=1, source_target_pairs={{0,1},{1,0},{2,3},{3,2},{4,5},{5,4},{6,7},{7,6},{8,9},{9,8},{10,11... | collective-permute-start | bytes 884744 | tf_op jit(solution)/shard_map/ppermute | solution.py:760
  140.3 46.3 %collective-permute-start.37 = (bf16[3,192,768]{2,1,0:T(8,128)(2,1)S(1)}, bf16[3,192,768]{2,1,0:T(8,128)(2,1)S(1)}, u32[]{:S(2)}, u32[]{:S(2)}) collective-permute-start(bf16[3,192,768]{2,1,0:T(8,128)(2,1)S(1)} %pad_maximum_fusion.rest_17_), channel_id=1, source_target_pairs={{0,4},{4,0},{8,12},{12,8},{16,20},{20,16},{24,28},{28,24},{1,5},{5... | collective-permute-start | bytes 2654216 | tf_op jit(solution)/shard_map/ppermute | solution.py:763
  140.9 45.2 %collective-permute-start.26 = (bf16[2,96,1920]{2,1,0:T(8,128)(2,1)S(1)}, bf16[2,96,1920]{2,1,0:T(8,128)(2,1)S(1)}, u32[]{:S(2)}, u32[]{:S(2)}) collective-permute-start(bf16[2,96,1920]{2,1,0:T(8,128)(2,1)S(1)} %pad_maximum_fusion.1.rest_6_), channel_id=1, source_target_pairs={{0,4},{4,0},{8,12},{12,8},{16,20},{20,16},{24,28},{28,24},{1,5},{5... | collective-permute-start | bytes 2211848 | tf_op jit(solution)/shard_map/ppermute | solution.py:763
  142.4 15.2 %collective-permute-start.28 = (bf16[96,1920]{1,0:T(8,128)(2,1)}, bf16[96,1920]{1,0:T(8,128)(2,1)S(1)}, u32[]{:S(2)}, u32[]{:S(2)}) collective-permute-start(bf16[96,1920]{1,0:T(8,128)(2,1)} %collective-permute-done.21.rest_5_), channel_id=1, source_target_pairs={{0,1},{1,0},{2,3},{3,2},{4,5},{5,4},{6,7},{7,6},{8,9},{9,8},{10,11... | collective-permute-start | bytes 1105928 | tf_op jit(solution)/shard_map/ppermute | solution.py:760
  142.4 43.7 %collective-permute-start.25 = (bf16[96,1920]{1,0:T(8,128)(2,1)}, bf16[96,1920]{1,0:T(8,128)(2,1)}, u32[]{:S(2)}, u32[]{:S(2)}) collective-permute-start(bf16[96,1920]{1,0:T(8,128)(2,1)} %collective-permute-done.21.rest_5_), channel_id=1, source_target_pairs={{0,4},{4,0},{8,12},{12,8},{16,20},{20,16},{24,28},{28,24},{1,5},{5... | collective-permute-start | bytes 1105928 | tf_op jit(solution)/shard_map/ppermute | solution.py:763
  143.0 14.1 %collective-permute-start.30 = (bf16[96,1920]{1,0:T(8,128)(2,1)}, bf16[96,1920]{1,0:T(8,128)(2,1)}, u32[]{:S(2)}, u32[]{:S(2)}) collective-permute-start(bf16[96,1920]{1,0:T(8,128)(2,1)} %copy-done.30), channel_id=1, source_target_pairs={{0,1},{1,0},{2,3},{3,2},{4,5},{5,4},{6,7},{7,6},{8,9},{9,8},{10,11... | collective-permute-start | bytes 1105928 | tf_op jit(solution)/shard_map/ppermute | solution.py:760
  157.2 43.3 %collective-permute-start.39 = (bf16[3,192,768]{2,1,0:T(8,128)(2,1)S(1)}, bf16[3,192,768]{2,1,0:T(8,128)(2,1)S(1)}, u32[]{:S(2)}, u32[]{:S(2)}) collective-permute-start(bf16[3,192,768]{2,1,0:T(8,128)(2,1)S(1)} %pad_maximum_fusion.rest_17_), channel_id=1, source_target_pairs={{0,1},{1,0},{2,3},{3,2},{4,5},{5,4},{6,7},{7,6},{8,9},{9,8},{10,11... | collective-permute-start | bytes 2654216 | tf_op jit(solution)/shard_map/ppermute | solution.py:760
  157.6 42.9 %collective-permute-start.29 = (bf16[2,96,1920]{2,1,0:T(8,128)(2,1)S(1)}, bf16[2,96,1920]{2,1,0:T(8,128)(2,1)}, u32[]{:S(2)}, u32[]{:S(2)}) collective-permute-start(bf16[2,96,1920]{2,1,0:T(8,128)(2,1)S(1)} %pad_maximum_fusion.1.rest_6_), channel_id=1, source_target_pairs={{0,1},{1,0},{2,3},{3,2},{4,5},{5,4},{6,7},{7,6},{8,9},{9,8},{10,11... | collective-permute-start | bytes 2211848 | tf_op jit(solution)/shard_map/ppermute | solution.py:760
  186.1 14.4 %collective-permute-start.31 = (bf16[96,1920]{1,0:T(8,128)(2,1)}, bf16[96,1920]{1,0:T(8,128)(2,1)S(1)}, u32[]{:S(2)}, u32[]{:S(2)}) collective-permute-start(bf16[96,1920]{1,0:T(8,128)(2,1)} %collective-permute-done.25.rest_8_), channel_id=1, source_target_pairs={{0,1},{1,0},{2,3},{3,2},{4,5},{5,4},{6,7},{7,6},{8,9},{9,8},{10,11... | collective-permute-start | bytes 1105928 | tf_op jit(solution)/shard_map/ppermute | solution.py:760
  186.1 14.4 %collective-permute-start.32 = (bf16[2,96,1920]{2,1,0:T(8,128)(2,1)S(1)}, bf16[2,96,1920]{2,1,0:T(8,128)(2,1)}, u32[]{:S(2)}, u32[]{:S(2)}) collective-permute-start(bf16[2,96,1920]{2,1,0:T(8,128)(2,1)S(1)} %collective-permute-done.26.rest_9_), channel_id=1, source_target_pairs={{0,1},{1,0},{2,3},{3,2},{4,5},{5,4},{6,7},{7,6},{8,9},{9,8},{10,11... | collective-permute-start | bytes 2211848 | tf_op jit(solution)/shard_map/ppermute | solution.py:760
  295.4 53.6 %collective-permute-start.42 = (bf16[256,768]{1,0:T(8,128)(2,1)}, bf16[256,768]{1,0:T(8,128)(2,1)}, u32[]{:S(2)}, u32[]{:S(2)}) collective-permute-start(bf16[256,768]{1,0:T(8,128)(2,1)} %get-tuple-element.84), channel_id=1, source_target_pairs={{0,1},{1,0},{2,3},{3,2},{4,5},{5,4},{6,7},{7,6},{8,9},{9,8},{10,11... | collective-permute-start | bytes 1179656 | tf_op jit(solution)/shard_map/ppermute | solution.py:760
  295.8 53.6 %collective-permute-start.43 = (bf16[256,768]{1,0:T(8,128)(2,1)}, bf16[256,768]{1,0:T(8,128)(2,1)}, u32[]{:S(2)}, u32[]{:S(2)}) collective-permute-start(bf16[256,768]{1,0:T(8,128)(2,1)} %get-tuple-element.85), channel_id=1, source_target_pairs={{0,2},{1,3},{2,0},{3,1},{4,6},{5,7},{6,4},{7,5},{8,10},{9,11},{10,... | collective-permute-start | bytes 1179656 | tf_op jit(solution)/shard_map/ppermute | solution.py:760
  297.3 52.9 %collective-permute-start.44 = (bf16[256,768]{1,0:T(8,128)(2,1)}, bf16[256,768]{1,0:T(8,128)(2,1)}, u32[]{:S(2)}, u32[]{:S(2)}) collective-permute-start(bf16[256,768]{1,0:T(8,128)(2,1)} %get-tuple-element.86), channel_id=1, source_target_pairs={{0,3},{1,2},{2,1},{3,0},{4,7},{5,6},{6,5},{7,4},{8,11},{9,10},{10,... | collective-permute-start | bytes 1179656 | tf_op jit(solution)/shard_map/ppermute | solution.py:760
  303.2 20.7 %collective-permute-start.54 = (bf16[2,4,112,384]{3,2,1,0:T(8,128)(2,1)}, bf16[2,4,112,384]{3,2,1,0:T(8,128)(2,1)S(1)}, u32[]{:S(2)}, u32[]{:S(2)}) collective-permute-start(bf16[2,4,112,384]{3,2,1,0:T(8,128)(2,1)} %get-tuple-element.111), channel_id=1, source_target_pairs={{0,1},{1,0},{2,3},{3,2},{4,5},{5,4},{6,7},{7,6},{8,9},{9,8},{10,11... | collective-permute-start | bytes 2064392 | tf_op jit(solution)/shard_map/ppermute | solution.py:760
  310.9 46.3 %collective-permute-start.48 = (bf16[2,4,96,768]{3,2,1,0:T(8,128)(2,1)}, bf16[2,4,96,768]{3,2,1,0:T(8,128)(2,1)S(1)}, u32[]{:S(2)}, u32[]{:S(2)}) collective-permute-start(bf16[2,4,96,768]{3,2,1,0:T(8,128)(2,1)} %get-tuple-element.104), channel_id=1, source_target_pairs={{0,1},{1,0},{2,3},{3,2},{4,5},{5,4},{6,7},{7,6},{8,9},{9,8},{10,11... | collective-permute-start | bytes 3538952 | tf_op jit(solution)/shard_map/ppermute | solution.py:760
  337.2 67.5 %collective-permute-start.62 = (bf16[2,2,4,48,1920]{4,3,2,1,0:T(8,128)(2,1)}, bf16[2,2,4,48,1920]{4,3,2,1,0:T(8,128)(2,1)S(1)}, u32[]{:S(2)}, u32[]{:S(2)}) collective-permute-start(bf16[2,2,4,48,1920]{4,3,2,1,0:T(8,128)(2,1)} %get-tuple-element.116), channel_id=1, source_target_pairs={{0,1},{1,0},{2,3},{3,2},{4,5},{5,4},{6,7},{7,6},{8,9},{9,8},{10,11... | collective-permute-start | bytes 8847368 | tf_op jit(solution)/shard_map/ppermute | solution.py:760
  349.0 18.8 %collective-permute-start.45 = (bf16[256,768]{1,0:T(8,128)(2,1)}, bf16[256,768]{1,0:T(8,128)(2,1)}, u32[]{:S(2)}, u32[]{:S(2)}) collective-permute-start(bf16[256,768]{1,0:T(8,128)(2,1)} %get-tuple-element.100), channel_id=1, source_target_pairs={{0,1},{1,0},{2,3},{3,2},{4,5},{5,4},{6,7},{7,6},{8,9},{9,8},{10,11... | collective-permute-start | bytes 1179656 | tf_op jit(solution)/shard_map/ppermute | solution.py:760
  357.3 17.8 %collective-permute-start.47 = (bf16[256,768]{1,0:T(8,128)(2,1)}, bf16[256,768]{1,0:T(8,128)(2,1)}, u32[]{:S(2)}, u32[]{:S(2)}) collective-permute-start(bf16[256,768]{1,0:T(8,128)(2,1)} %get-tuple-element.102), channel_id=1, source_target_pairs={{0,3},{1,2},{2,1},{3,0},{4,7},{5,6},{6,5},{7,4},{8,11},{9,10},{10,... | collective-permute-start | bytes 1179656 | tf_op jit(solution)/shard_map/ppermute | solution.py:760
  365.4 15.6 %collective-permute-start.49 = (bf16[4,96,768]{2,1,0:T(8,128)(2,1)}, bf16[4,96,768]{2,1,0:T(8,128)(2,1)S(1)}, u32[]{:S(2)}, u32[]{:S(2)}) collective-permute-start(bf16[4,96,768]{2,1,0:T(8,128)(2,1)} %fusion.3), channel_id=1, source_target_pairs={{0,4},{4,0},{8,12},{12,8},{16,20},{20,16},{24,28},{28,24},{1,5},{5... | collective-permute-start | bytes 1769480 | tf_op jit(solution)/shard_map/ppermute | solution.py:763
  367.9 39.2 %collective-permute-start.70 = (bf16[2,4,192,768]{3,2,1,0:T(8,128)(2,1)}, bf16[2,4,192,768]{3,2,1,0:T(8,128)(2,1)S(1)}, u32[]{:S(2)}, u32[]{:S(2)}) collective-permute-start(bf16[2,4,192,768]{3,2,1,0:T(8,128)(2,1)} %bitcast.50), channel_id=1, source_target_pairs={{0,1},{1,0},{2,3},{3,2},{4,5},{5,4},{6,7},{7,6},{8,9},{9,8},{10,11... | collective-permute-start | bytes 7077896 | tf_op jit(solution)/shard_map/ppermute | solution.py:760
  389.8 17.2 %collective-permute-start.61 = (bf16[112,384]{1,0:T(8,128)(2,1)S(1)}, bf16[112,384]{1,0:T(8,128)(2,1)S(1)}, u32[]{:S(2)}, u32[]{:S(2)}) collective-permute-start(bf16[112,384]{1,0:T(8,128)(2,1)S(1)} %add_convert_fusion.8), channel_id=1, source_target_pairs={{0,1},{1,0},{2,3},{3,2},{4,5},{5,4},{6,7},{7,6},{8,9},{9,8},{10,11... | collective-permute-start | bytes 258056 | tf_op jit(solution)/shard_map/ppermute | solution.py:760
  405.1 34.7 %collective-permute-start.63 = (bf16[2,4,48,1920]{3,2,1,0:T(8,128)(2,1)S(1)}, bf16[2,4,48,1920]{3,2,1,0:T(8,128)(2,1)S(1)}, u32[]{:S(2)}, u32[]{:S(2)}) collective-permute-start(bf16[2,4,48,1920]{3,2,1,0:T(8,128)(2,1)S(1)} %fusion.1), channel_id=1, source_target_pairs={{0,2},{1,3},{2,0},{3,1},{4,6},{5,7},{6,4},{7,5},{8,10},{9,11},{10,... | collective-permute-start | bytes 4423688 | tf_op jit(solution)/shard_map/ppermute | solution.py:760
  407.5 34.3 %collective-permute-start.71 = (bf16[4,192,768]{2,1,0:T(8,128)(2,1)S(1)}, bf16[4,192,768]{2,1,0:T(8,128)(2,1)S(1)}, u32[]{:S(2)}, u32[]{:S(2)}) collective-permute-start(bf16[4,192,768]{2,1,0:T(8,128)(2,1)S(1)} %fusion), channel_id=1, source_target_pairs={{0,4},{4,0},{8,12},{12,8},{16,20},{20,16},{24,28},{28,24},{1,5},{5... | collective-permute-start | bytes 3538952 | tf_op jit(solution)/shard_map/ppermute | solution.py:763
  440.2 18.1 %collective-permute-start.64 = (bf16[4,48,1920]{2,1,0:T(8,128)(2,1)S(1)}, bf16[4,48,1920]{2,1,0:T(8,128)(2,1)S(1)}, u32[]{:S(2)}, u32[]{:S(2)}) collective-permute-start(bf16[4,48,1920]{2,1,0:T(8,128)(2,1)S(1)} %fusion.2), channel_id=1, source_target_pairs={{0,4},{4,0},{8,12},{12,8},{16,20},{20,16},{24,28},{28,24},{1,5},{5... | collective-permute-start | bytes 2211848 | tf_op jit(solution)/shard_map/ppermute | solution.py:763
  442.1 18.4 %collective-permute-start.72 = (bf16[192,768]{1,0:T(8,128)(2,1)S(1)}, bf16[192,768]{1,0:T(8,128)(2,1)S(1)}, u32[]{:S(2)}, u32[]{:S(2)}) collective-permute-start(bf16[192,768]{1,0:T(8,128)(2,1)S(1)} %get-tuple-element.124), channel_id=1, source_target_pairs={{0,8},{4,12},{8,0},{12,4},{16,24},{20,28},{24,16},{28,20},{1,9},{5... | collective-permute-start | bytes 884744 | tf_op jit(solution)/shard_map/ppermute | solution.py:763
  442.2 20.0 %collective-permute-start.74 = (bf16[192,768]{1,0:T(8,128)(2,1)S(1)}, bf16[192,768]{1,0:T(8,128)(2,1)S(1)}, u32[]{:S(2)}, u32[]{:S(2)}) collective-permute-start(bf16[192,768]{1,0:T(8,128)(2,1)S(1)} %get-tuple-element.125), channel_id=1, source_target_pairs={{0,24},{4,28},{8,16},{12,20},{16,8},{20,12},{24,0},{28,4},{1,25},{... | collective-permute-start | bytes 884744 | tf_op jit(solution)/shard_map/ppermute | solution.py:763
  444.2 36.2 %collective-permute-start.73 = (bf16[192,768]{1,0:T(8,128)(2,1)S(1)}, bf16[192,768]{1,0:T(8,128)(2,1)S(1)}, u32[]{:S(2)}, u32[]{:S(2)}) collective-permute-start(bf16[192,768]{1,0:T(8,128)(2,1)S(1)} %get-tuple-element.126), channel_id=1, source_target_pairs={{0,16},{4,20},{8,24},{12,28},{16,0},{20,4},{24,8},{28,12},{1,17},{... | collective-permute-start | bytes 884744 | tf_op jit(solution)/shard_map/ppermute | solution.py:763
  458.6 23.3 %collective-permute-start.65 = (bf16[48,1920]{1,0:T(8,128)(2,1)S(1)}, bf16[48,1920]{1,0:T(8,128)(2,1)S(1)}, u32[]{:S(2)}, u32[]{:S(2)}) collective-permute-start(bf16[48,1920]{1,0:T(8,128)(2,1)S(1)} %get-tuple-element.121), channel_id=1, source_target_pairs={{0,8},{4,12},{8,0},{12,4},{16,24},{20,28},{24,16},{28,20},{1,9},{5... | collective-permute-start | bytes 552968 | tf_op jit(solution)/shard_map/ppermute | solution.py:763
  458.6 23.2 %collective-permute-start.67 = (bf16[48,1920]{1,0:T(8,128)(2,1)S(1)}, bf16[48,1920]{1,0:T(8,128)(2,1)S(1)}, u32[]{:S(2)}, u32[]{:S(2)}) collective-permute-start(bf16[48,1920]{1,0:T(8,128)(2,1)S(1)} %get-tuple-element.122), channel_id=1, source_target_pairs={{0,24},{4,28},{8,16},{12,20},{16,8},{20,12},{24,0},{28,4},{1,25},{... | collective-permute-start | bytes 552968 | tf_op jit(solution)/shard_map/ppermute | solution.py:763
  460.5 25.9 %collective-permute-start.66 = (bf16[48,1920]{1,0:T(8,128)(2,1)S(1)}, bf16[48,1920]{1,0:T(8,128)(2,1)S(1)}, u32[]{:S(2)}, u32[]{:S(2)}) collective-permute-start(bf16[48,1920]{1,0:T(8,128)(2,1)S(1)} %get-tuple-element.123), channel_id=1, source_target_pairs={{0,16},{4,20},{8,24},{12,28},{16,0},{20,4},{24,8},{28,12},{1,17},{... | collective-permute-start | bytes 552968 | tf_op jit(solution)/shard_map/ppermute | solution.py:763
  (74 other events, 905.0 us)
